TPU v7x, 32 devices: a whole 2x2x4 slice. The times are simulated.
32 devices in a mesh: row: 8 (over y, x, core), col: 4 (over z).
Axes of the slice: x: 2, y: 2, z: 4, core: 2. Of those that a mesh axis runs over, the one named last changes fastest.
Arguments:
- trailing: float32 [4096, 8192], P('row', 'col'), may hold values from -6 to 6
- leaf_v: float32 [4096, 256], P(('row', 'col')), may hold values from -0.25 to 0.25
- leaf_t: float32 [2048, 256], P(('row', 'col')), may hold values from -0.375 to 0.375
- tree_y: float32 [2048, 256], P(('row', 'col')), may hold values from -0.375 to 0.375
- tree_t: float32 [2048, 256], P(('row', 'col')), may hold values from -0.1875 to 0.1875
Outputs:
- updated: float32 [4096, 8192], P('row', 'col')
All inputs are finite; a program needn't handle non-finite values.
Results may differ from a plain program's by a relative error of at most 0.00016.
Values sent between devices are 32-bit elements; how exact they have to be, the bound alone decides.
No kernel may reach another device: no remote copies, remote signals or barrier semaphores. Data moves between devices by JAX's collectives and lax.ppermute only.
A program may use at most 64 MiB of HBM per device.

v0:
```python
import jax
import jax.numpy as jnp
from jax import lax
from jax.sharding import PartitionSpec as P


def from_partner(value, axis, stride):
    mask = 2**stride
    pairs = [(source, source ^ mask) for source in range(lax.axis_size(axis))]
    return lax.ppermute(value, axis, pairs)


def product(left, right):
    return jnp.dot(left, right, precision=lax.Precision.HIGHEST, preferred_element_type=jnp.float32)


def per_device(trailing, leaf_v, leaf_t, tree_y, tree_t):
    width = leaf_t.shape[1]
    vectors, coeffs, own_y, own_t = (
        lax.all_gather(leaf_v, "col", axis=0, tiled=True),
        lax.all_gather(leaf_t, "col", axis=0, tiled=True),
        lax.all_gather(tree_y, "col", axis=0, tiled=True),
        lax.all_gather(tree_t, "col", axis=0, tiled=True),
    )
    inner = product(vectors.T, trailing)
    changed = trailing - product(vectors, product(coeffs.T, inner))
    top = changed[:width]
    rest = changed[width:]
    position = lax.axis_index("row")
    depth = lax.axis_size("row").bit_length() - 1
    far_factors = []
    for level in range(depth):
        far_factors.append(from_partner((own_y, own_t), "row", level))
    for level in range(depth):
        stride = 1 << level
        is_lower = position // stride % 2 == 1
        far_top = from_partner(top, "row", level)
        far_y = far_factors[level][0]
        far_t = far_factors[level][1]
        pair_y = jnp.where(is_lower, own_y, far_y)
        pair_t = jnp.where(is_lower, far_t, own_t)
        top_upper = jnp.where(is_lower, far_top, top)
        top_lower = jnp.where(is_lower, top, far_top)
        pair_rows = product(pair_t.T, top_upper + product(pair_y.T, top_lower))
        top = jnp.where(is_lower, top_lower - product(pair_y, pair_rows), top_upper - pair_rows)
    return jnp.concatenate([top, rest], axis=0)


def solution(mesh):
    return jax.shard_map(
        per_device,
        mesh=mesh,
        in_specs=(
            P("row", "col"),
            P(("row", "col"), None),
            P(("row", "col"), None),
            P(("row", "col"), None),
            P(("row", "col"), None),
        ),
        out_specs=P("row", "col"),
        check_vma=False,
    )
```

profile of v0, /device:TPU:0, one launch (start us, length us, event | category | flops | bytes accessed | tf_op | source)
XLA Modules:
  0.0 221.4 jit_solution(12751075513140949062)
XLA Ops:
  0.0 17.6 %all_gather.12 = f32[512,256]{1,0:T(8,128)S(1)} all-gather(f32[128,256]{1,0:T(8,128)} %param.6), channel_id=1, replica_groups=mesh['row'=8,'col'=4] {'col'}, dimensions={0}, use_global_device_ids=true | all-gather | bytes 655360 | tf_op jit(solution)/shard_map/all_gather | solution.py:20
  17.6 14.9 %all_gather.13 = f32[256,256]{1,0:T(8,128)S(1)} all-gather(f32[64,256]{1,0:T(8,128)} %param.7), channel_id=1, replica_groups=mesh['row'=8,'col'=4] {'col'}, dimensions={0}, use_global_device_ids=true | all-gather | bytes 327680 | tf_op jit(solution)/shard_map/all_gather | solution.py:21
  32.4 5.5 %fusion.14 = f32[256,2048]{1,0:T(8,128)S(1)} fusion(f32[512,256]{1,0:T(8,128)S(1)} %all_gather.12, f32[512,2048]{1,0:T(8,128)} %param.5), kind=kOutput, calls=%fused_computation.31 | convolution fusion | flops 3221225472 | bytes 6815744 | tf_op jit(solution)/shard_map/dot_general | solution.py:14
  37.9 3.6 %fusion.15 = f32[2048,256]{1,0:T(8,128)S(1)} fusion(f32[256,2048]{1,0:T(8,128)S(1)} %fusion.14, f32[256,256]{1,0:T(8,128)S(1)} %all_gather.13), kind=kOutput, calls=%fused_computation.32 | convolution fusion | flops 1610612736 | bytes 4456448 | tf_op jit(solution)/shard_map/dot_general | solution.py:14
  41.5 3.6 %bitcast_subtract_fusion = f32[512,2048]{1,0:T(8,128)S(1)} fusion(f32[512,2048]{1,0:T(8,128)S(1)} %copy-done.4, f32[2048,256]{1,0:T(8,128)S(1)} %fusion.15, f32[512,256]{1,0:T(8,128)S(1)} %all_gather.12), kind=kOutput, calls=%fused_computation.1 | convolution fusion | flops 3222274048 | bytes 11010048 | tf_op jit(solution)/shard_map/dot_general | solution.py:14
  45.1 2.5 %fusion.13 = (f32[256,2048]{1,0:T(8,128)}, f32[256,2048]{1,0:T(8,128)}) fusion(f32[512,2048]{1,0:T(8,128)S(1)} %bitcast_subtract_fusion), kind=kLoop, calls=%fused_computation.30 | loop fusion | bytes 8388608 | tf_op jit(solution)/shard_map/slice | solution.py:27
  48.4 14.1 %all_gather.14 = f32[256,256]{1,0:T(8,128)S(1)} all-gather(f32[64,256]{1,0:T(8,128)S(1)} %copy-done.7), channel_id=1, replica_groups=mesh['row'=8,'col'=4] {'col'}, dimensions={0}, use_global_device_ids=true | all-gather | bytes 327680 | tf_op jit(solution)/shard_map/all_gather | solution.py:22
  62.5 14.8 %all_gather.15 = f32[256,256]{1,0:T(8,128)S(1)} all-gather(f32[64,256]{1,0:T(8,128)S(1)} %copy-done.8), channel_id=1, replica_groups=mesh['row'=8,'col'=4] {'col'}, dimensions={0}, use_global_device_ids=true | all-gather | bytes 327680 | tf_op jit(solution)/shard_map/all_gather | solution.py:23
  77.3 5.1 %convolution_add_fusion.2 = f32[256,2048]{1,0:T(8,128)S(1)} fusion(f32[256,2048]{1,0:T(8,128)S(1)} %collective-permute-done, pred[]{:T(512)S(6)} %eq.15, f32[256,256]{1,0:T(8,128)S(1)} %all_gather.14, f32[256,256]{1,0:T(8,128)S(1)} %collective-permute-done.1, f32[512,2048]{1,0:T(8,128)} %copy-done), kind=kOutput, calls=%fused_computation.10 | convolution fusion | flops 1612251136 | bytes 11011584 | tf_op jit(solution)/shard_map/dot_general | solution.py:14
  82.4 1.9 fusion.7
  84.6 4.0 %fusion.2 = f32[256,2048]{1,0:T(8,128)S(1)} fusion(f32[256,2048]{1,0:T(8,128)S(1)} %fusion.7, pred[]{:T(512)S(6)} %eq.15, f32[256,2048]{1,0:T(8,128)} %copy-done.5, f32[256,256]{1,0:T(8,128)S(1)} %all_gather.14, f32[256,256]{1,0:T(8,128)S(1)} %collective-permute-done.1, f32[512,2048]{1,0:T(8,128)S(1)} %copy-done.1), kind=kOutput, calls=%fused_computation.9 | convolution fusion | flops 1613299712 | bytes 11011072 | tf_op jit(solution)/shard_map/dot_general | solution.py:14
  88.6 1.6 collective-permute-start.3
  90.7 1.5 collective-permute-start.5
  92.2 50.5 %collective-permute-done.4 = f32[256,256]{1,0:T(8,128)S(1)} collective-permute-done((f32[256,256]{1,0:T(8,128)S(1)}, f32[256,256]{1,0:T(8,128)S(1)}, u32[]{:S(2)}, u32[]{:S(2)}) %collective-permute-start.4) | collective-permute-done | bytes 262176 | tf_op jit(solution)/shard_map/ppermute | solution.py:10
  142.7 4.3 %convolution_add_fusion.1 = f32[256,2048]{1,0:T(8,128)S(1)} fusion(f32[256,2048]{1,0:T(8,128)S(1)} %fusion.2, f32[256,2048]{1,0:T(8,128)} %collective-permute-done.3, pred[]{:T(512)S(6)} %eq.14, f32[256,256]{1,0:T(8,128)S(1)} %all_gather.14, f32[256,256]{1,0:T(8,128)S(1)} %collective-permute-done.4), kind=kOutput, calls=%fused_computation.7 | convolution fusion | flops 1612251136 | bytes 6815745 | tf_op jit(solution)/shard_map/dot_general | solution.py:14
  148.0 1.9 fusion.5
  149.9 4.3 %fusion.1 = f32[256,2048]{1,0:T(8,128)S(1)} fusion(f32[256,2048]{1,0:T(8,128)S(1)} %fusion.5, pred[]{:T(512)S(6)} %eq.14, f32[256,2048]{1,0:T(8,128)S(1)} %copy-done.3, f32[256,2048]{1,0:T(8,128)} %collective-permute-done.3, f32[256,256]{1,0:T(8,128)S(1)} %all_gather.14, f32[256,256]{1,0:T(8,128)S(1)} %collective-permute-done.4), kind=kOutput, calls=%fused_computation.6 | convolution fusion | flops 1613299712 | bytes 8912897 | tf_op jit(solution)/shard_map/dot_general | solution.py:14
  154.2 1.6 collective-permute-start.6
  156.3 1.5 collective-permute-start.8
  157.8 50.6 %collective-permute-done.7 = f32[256,256]{1,0:T(8,128)S(1)} collective-permute-done((f32[256,256]{1,0:T(8,128)S(1)}, f32[256,256]{1,0:T(8,128)S(1)}, u32[]{:S(2)}, u32[]{:S(2)}) %collective-permute-start.7) | collective-permute-done | bytes 262176 | tf_op jit(solution)/shard_map/ppermute | solution.py:10
  208.4 4.3 %convolution_add_fusion = f32[256,2048]{1,0:T(8,128)S(1)} fusion(f32[256,2048]{1,0:T(8,128)S(1)} %fusion.1, f32[256,2048]{1,0:T(8,128)} %collective-permute-done.6, pred[]{:T(512)S(6)} %eq.13, f32[256,256]{1,0:T(8,128)S(1)} %all_gather.14, f32[256,256]{1,0:T(8,128)S(1)} %collective-permute-done.7), kind=kOutput, calls=%fused_computation.4 | convolution fusion | flops 1612251136 | bytes 6815745 | tf_op jit(solution)/shard_map/dot_general | solution.py:14
  212.8 1.9 fusion.3
  214.7 4.2 %fusion = f32[256,2048]{1,0:T(8,128)S(1)} fusion(f32[256,2048]{1,0:T(8,128)S(1)} %fusion.3, pred[]{:T(512)S(6)} %eq.13, f32[256,2048]{1,0:T(8,128)S(1)} %fusion.1, f32[256,2048]{1,0:T(8,128)} %collective-permute-done.6, f32[256,256]{1,0:T(8,128)S(1)} %all_gather.14, f32[256,256]{1,0:T(8,128)S(1)} %collective-permute-done.7), kind=kOutput, calls=%fused_computation.3 | convolution fusion | flops 1613299712 | bytes 8912897 | tf_op jit(solution)/shard_map/dot_general | solution.py:14
  218.9 2.5 %pad_maximum_fusion = f32[512,2048]{1,0:T(8,128)} fusion(f32[256,2048]{1,0:T(8,128)S(1)} %copy-done.6, f32[256,2048]{1,0:T(8,128)S(1)} %fusion), kind=kLoop, calls=%fused_computation | loop fusion | flops 1048576 | bytes 8388608 | tf_op jit(solution)/shard_map/concatenate | solution.py:46
  (30 shorter events, 2.9 us)
Async XLA Ops:
  37.9 3.6 %copy-start.4 = (f32[512,2048]{1,0:T(8,128)S(1)}, f32[512,2048]{1,0:T(8,128)}, u32[]{:S(2)}) copy-start(f32[512,2048]{1,0:T(8,128)} %param.5) | copy-start | bytes 12582916
  45.1 3.3 %copy-start = (f32[512,2048]{1,0:T(8,128)}, f32[512,2048]{1,0:T(8,128)S(1)}, u32[]{:S(2)}) copy-start(f32[512,2048]{1,0:T(8,128)S(1)} %bitcast_subtract_fusion) | copy-start | bytes 12582916
  45.1 3.3 %copy-start.7 = (f32[64,256]{1,0:T(8,128)S(1)}, f32[64,256]{1,0:T(8,128)}, u32[]{:S(2)}) copy-start(f32[64,256]{1,0:T(8,128)} %param.8) | copy-start | bytes 196612
  45.1 17.4 %copy-start.8 = (f32[64,256]{1,0:T(8,128)S(1)}, f32[64,256]{1,0:T(8,128)}, u32[]{:S(2)}) copy-start(f32[64,256]{1,0:T(8,128)} %param.9) | copy-start | bytes 196612
  48.4 28.9 %collective-permute-start = (f32[256,2048]{1,0:T(8,128)}, f32[256,2048]{1,0:T(8,128)S(1)}, u32[]{:S(2)}, u32[]{:S(2)}) collective-permute-start(f32[256,2048]{1,0:T(8,128)} %get-tuple-element.5), channel_id=1, source_target_pairs={{0,4},{4,0},{8,12},{12,8},{16,20},{20,16},{24,28},{28,24},{1,5},{5... | collective-permute-start | bytes 6291464 | tf_op jit(solution)/shard_map/ppermute | solution.py:10
  62.5 14.8 %collective-permute-start.1 = (f32[256,256]{1,0:T(8,128)S(1)}, f32[256,256]{1,0:T(8,128)S(1)}, u32[]{:S(2)}, u32[]{:S(2)}) collective-permute-start(f32[256,256]{1,0:T(8,128)S(1)} %all_gather.14), channel_id=1, source_target_pairs={{0,4},{4,0},{8,12},{12,8},{16,20},{20,16},{24,28},{28,24},{1,5},{5... | collective-permute-start | bytes 786440 | tf_op jit(solution)/shard_map/ppermute | solution.py:10
  77.3 5.2 %collective-permute-start.2 = (f32[256,256]{1,0:T(8,128)S(1)}, f32[256,256]{1,0:T(8,128)S(1)}, u32[]{:S(2)}, u32[]{:S(2)}) collective-permute-start(f32[256,256]{1,0:T(8,128)S(1)} %all_gather.15), channel_id=1, source_target_pairs={{0,4},{4,0},{8,12},{12,8},{16,20},{20,16},{24,28},{28,24},{1,5},{5... | collective-permute-start | bytes 786440 | tf_op jit(solution)/shard_map/ppermute | solution.py:10
  77.3 5.1 %copy-start.5 = (f32[256,2048]{1,0:T(8,128)}, f32[256,2048]{1,0:T(8,128)S(1)}, u32[]{:S(2)}) copy-start(f32[256,2048]{1,0:T(8,128)S(1)} %collective-permute-done) | copy-start | bytes 6291460
  82.4 2.2 copy-start.1
  88.6 58.5 %copy-start.2 = (f32[256,2048]{1,0:T(8,128)}, f32[256,2048]{1,0:T(8,128)S(1)}, u32[]{:S(2)}) copy-start(f32[256,2048]{1,0:T(8,128)S(1)} %fusion.2) | copy-start | bytes 6291460
  88.6 54.1 %collective-permute-start.3 = (f32[256,2048]{1,0:T(8,128)S(1)}, f32[256,2048]{1,0:T(8,128)}, u32[]{:S(2)}, u32[]{:S(2)}) collective-permute-start(f32[256,2048]{1,0:T(8,128)S(1)} %fusion.2), channel_id=1, source_target_pairs={{0,8},{4,12},{8,0},{12,4},{16,24},{20,28},{24,16},{28,20},{1,9},{5... | collective-permute-start | bytes 6291464 | tf_op jit(solution)/shard_map/ppermute | solution.py:10
  90.2 52.5 %collective-permute-start.4 = (f32[256,256]{1,0:T(8,128)S(1)}, f32[256,256]{1,0:T(8,128)S(1)}, u32[]{:S(2)}, u32[]{:S(2)}) collective-permute-start(f32[256,256]{1,0:T(8,128)S(1)} %all_gather.14), channel_id=1, source_target_pairs={{0,8},{4,12},{8,0},{12,4},{16,24},{20,28},{24,16},{28,20},{1,9},{5... | collective-permute-start | bytes 786440 | tf_op jit(solution)/shard_map/ppermute | solution.py:10
  90.7 57.2 %collective-permute-start.5 = (f32[256,256]{1,0:T(8,128)S(1)}, f32[256,256]{1,0:T(8,128)S(1)}, u32[]{:S(2)}, u32[]{:S(2)}) collective-permute-start(f32[256,256]{1,0:T(8,128)S(1)} %all_gather.15), channel_id=1, source_target_pairs={{0,8},{4,12},{8,0},{12,4},{16,24},{20,28},{24,16},{28,20},{1,9},{5... | collective-permute-start | bytes 786440 | tf_op jit(solution)/shard_map/ppermute | solution.py:10
  148.0 1.9 copy-start.3
  154.2 54.2 %collective-permute-start.6 = (f32[256,2048]{1,0:T(8,128)S(1)}, f32[256,2048]{1,0:T(8,128)}, u32[]{:S(2)}, u32[]{:S(2)}) collective-permute-start(f32[256,2048]{1,0:T(8,128)S(1)} %fusion.1), channel_id=1, source_target_pairs={{0,16},{4,20},{8,24},{12,28},{16,0},{20,4},{24,8},{28,12},{1,17},{... | collective-permute-start | bytes 6291464 | tf_op jit(solution)/shard_map/ppermute | solution.py:10
  155.8 52.6 %collective-permute-start.7 = (f32[256,256]{1,0:T(8,128)S(1)}, f32[256,256]{1,0:T(8,128)S(1)}, u32[]{:S(2)}, u32[]{:S(2)}) collective-permute-start(f32[256,256]{1,0:T(8,128)S(1)} %all_gather.14), channel_id=1, source_target_pairs={{0,16},{4,20},{8,24},{12,28},{16,0},{20,4},{24,8},{28,12},{1,17},{... | collective-permute-start | bytes 786440 | tf_op jit(solution)/shard_map/ppermute | solution.py:10
  156.3 56.5 %collective-permute-start.8 = (f32[256,256]{1,0:T(8,128)S(1)}, f32[256,256]{1,0:T(8,128)S(1)}, u32[]{:S(2)}, u32[]{:S(2)}) collective-permute-start(f32[256,256]{1,0:T(8,128)S(1)} %all_gather.15), channel_id=1, source_target_pairs={{0,16},{4,20},{8,24},{12,28},{16,0},{20,4},{24,8},{28,12},{1,17},{... | collective-permute-start | bytes 786440 | tf_op jit(solution)/shard_map/ppermute | solution.py:10
  214.7 4.2 %copy-start.6 = (f32[256,2048]{1,0:T(8,128)S(1)}, f32[256,2048]{1,0:T(8,128)}, u32[]{:S(2)}) copy-start(f32[256,2048]{1,0:T(8,128)} %get-tuple-element.6) | copy-start | bytes 6291460
where the time goes:
time: 222 us; the launch traced here: 221 us
  waiting for transfers between devices  102 us (46%)
  blocking collectives  61.3 us (28%)
  matrix products  44.7 us (20%)
  starting transfers between devices  7.2 us (3%)
  local copies, waits for them, and re-layouts  3.51 us (2%)
  other arithmetic  2.51 us (1%)
    ppermute x9, waiting for transfers between devices, from_partner(): return lax.ppermute(value, axis, pairs)  102 us
    dot_general x12, matrix products, product(): jnp.dot(left, right, precision=lax.Precision.HIGHEST, preferred_element_t...  44.7 us
    all_gather x1, blocking collectives, per_device(): lax.all_gather(leaf_v, 'col', axis=0, tiled=True)  17.6 us
    all_gather x1, blocking collectives, per_device(): lax.all_gather(leaf_t, 'col', axis=0, tiled=True)  14.9 us
    all_gather x1, blocking collectives, per_device(): lax.all_gather(tree_t, 'col', axis=0, tiled=True)  14.8 us
    all_gather x1, blocking collectives, per_device(): lax.all_gather(tree_y, 'col', axis=0, tiled=True)  14.1 us
    ppermute x9, starting transfers between devices, from_partner(): return lax.ppermute(value, axis, pairs)  7.2 us
  transfers between devices with their start and end apart: 9, of which 3 were waited for; matrix products, arithmetic and copies ran while one was open for 6% of the time, Pallas kernels for 0%

commit v1 on v0

v1 whole, which is shorter than its diff:
```python
import functools

import jax
import jax.numpy as jnp
from jax import lax
from jax.experimental import pallas as pl
from jax.experimental.pallas import tpu as pltpu
from jax.sharding import PartitionSpec as P

CHUNKS = 4
F32, BF16 = jnp.float32, jnp.bfloat16
VMEM = pl.BlockSpec(memory_space=pltpu.VMEM)
SMEM = pl.BlockSpec(memory_space=pltpu.SMEM)


def swap(value, axis, mask):
    return lax.ppermute(value, axis, [(i, i ^ mask) for i in range(lax.axis_size(axis))])


def spread(piece, axis):
    return [piece] + [swap(piece, axis, k) for k in range(1, lax.axis_size(axis))]


def split(x):
    high = x.astype(BF16)
    return high, (x - high.astype(F32)).astype(BF16)


def dot3(ah, al, bh, bl, dims=((1,), (0,))):
    d = functools.partial(lax.dot_general, dimension_numbers=(dims, ((), ())), preferred_element_type=F32)
    return d(ah, bh) + (d(ah, bl) + d(al, bh))


def dotf(a, b, dims=((1,), (0,))):
    return dot3(*split(a), *split(b), dims)


def place(index_ref, pieces, offset, rows, out):
    own = index_ref[1]
    for k, piece in enumerate(pieces):
        out[pl.ds(pl.multiple_of((own ^ k) * rows, rows), rows), :] = piece[offset:offset + rows, :]


def leaf_factors(n, vr, tr, index_ref, *refs):
    pieces, (vth, vtl, ph, plo, block), (v, t) = refs[:n], refs[n:n + 5], refs[n + 5:]
    place(index_ref, pieces, 0, vr, v)
    place(index_ref, pieces, vr, tr, t)
    place(index_ref, pieces, vr + tr, tr, block)
    full = v[...]
    vth[...], vtl[...] = split(full.T)
    ph[...], plo[...] = split(dotf(full, t[...], ((1,), (1,))))


def level_factors(level, n, tr, offset, index_ref, *refs):
    width = refs[-1].shape[0]
    own, far = refs[-2:]
    fh, fl = refs[-4:-2]
    first, second, pieces = refs[0], refs[1], refs[2:2 + n]
    place(index_ref, pieces, offset, tr, far)
    row = index_ref[0]
    bit = (row >> level) & 1

    @pl.when(bit == (row & 1))
    def _():
        own[...] = first[...]

    @pl.when(bit != (row & 1))
    def _():
        own[...] = second[...]

    form_factors(width, bit, own, far, fh, fl)


def form_factors(width, bit, own, far, fh, fl):
    @pl.when(bit == 0)
    def _():
        s, y = own[...], far[...]
        fh[:, :width], fl[:, :width] = split(s.T)
        fh[:, width:], fl[:, width:] = split(dotf(y, s).T)

    @pl.when(bit == 1)
    def _():
        y, s = own[...], far[...]
        ys = dotf(y, s, ((1,), (1,)))
        fh[:, width:], fl[:, width:] = split(ys)
        fh[:, :width], fl[:, :width] = split(dotf(ys, y, ((1,), (1,))))


def first_factors(index_ref, own, far, fh, fl):
    form_factors(own.shape[0], index_ref[0] & 1, own, far, fh, fl)


def second_block(n, tr, index_ref, *refs):
    place(index_ref, refs[:n], 0, tr, refs[n])


def leaf_apply(width, c, vth, vtl, ph, plo, _, top, rest):
    block = c[...]
    ih, il = split(dot3(vth[...], vtl[...], *split(block)))
    change = dot3(ph[...], plo[...], ih, il)
    top[...] = block[:width] - change[:width]
    rest[...] = block[width:] - change[width:]


def level_apply(width, own, far, fh, fl, *refs):
    out = refs[-1]
    mine = own[...]
    oh, ol = split(mine)
    xh, xl = split(far[...])
    change = dot3(fh[:, :width], fl[:, :width], oh, ol) + dot3(fh[:, width:], fl[:, width:], xh, xl)
    out[...] = mine - change


def cost(flops, size):
    return pl.CostEstimate(flops=flops, bytes_accessed=size, transcendentals=0)


def per_device(trailing, leaf_v, leaf_t, tree_y, tree_t):
    height, columns = trailing.shape
    width = leaf_v.shape[1]
    vr, tr = leaf_v.shape[0], leaf_t.shape[0]
    n = lax.axis_size("col")
    depth = lax.axis_size("row").bit_length() - 1
    row = lax.axis_index("row")
    index = jnp.stack([row, lax.axis_index("col")]).astype(jnp.int32)
    small = jax.ShapeDtypeStruct((width, width), F32)
    pair = [jax.ShapeDtypeStruct((width, 2 * width), BF16)] * 2
    scratch = pltpu.VMEM((width, width), F32)

    def role(level, flip=False):
        return jnp.where((row >> level & 1 == 1) != flip, tree_y, tree_t)

    group0 = jnp.concatenate([leaf_v, leaf_t, role(0)], axis=0)
    far_shards = [swap(role(level), "row", 1 << level) for level in range(1, depth)]
    pieces0 = spread(group0, "col")
    vth, vtl, ph, plo, block0 = pl.pallas_call(
        functools.partial(leaf_factors, n, vr, tr),
        out_shape=[jax.ShapeDtypeStruct((width, height), BF16)] * 2 + [jax.ShapeDtypeStruct((height, width), BF16)] * 2 + [small],
        in_specs=[SMEM] + [VMEM] * n,
        out_specs=[VMEM] * 5,
        scratch_shapes=[pltpu.VMEM((height, width), F32), scratch],
        name="leaf_factors",
    )(index, *pieces0)
    far0 = swap(block0, "row", 1)
    factors = [
        pl.pallas_call(first_factors, out_shape=pair, in_specs=[SMEM] + [VMEM] * 2, out_specs=[VMEM] * 2, name="factors0")(
            index, block0, far0
        )
    ]
    group1 = jnp.concatenate([role(0, True), far_shards[0]], axis=0)
    group2 = jnp.concatenate(far_shards[1:], axis=0)
    group1, pieces0[1:] = lax.optimization_barrier((group1, pieces0[1:]))
    pieces1 = spread(group1, "col")
    group2, pieces1[1:] = lax.optimization_barrier((group2, pieces1[1:]))
    pieces2 = spread(group2, "col")
    block1 = pl.pallas_call(
        functools.partial(second_block, n, tr), out_shape=small, in_specs=[SMEM] + [VMEM] * n, out_specs=VMEM, name="block1"
    )(index, *pieces1)
    for level in range(1, depth):
        pieces, offset = (pieces1, tr) if level == 1 else (pieces2, (level - 2) * tr)
        factors.append(
            pl.pallas_call(
                functools.partial(level_factors, level, n, tr, offset),
                out_shape=pair,
                in_specs=[SMEM] + [VMEM] * (2 + n),
                out_specs=[VMEM] * 2,
                scratch_shapes=[scratch, scratch],
                name=f"factors{level}",
            )(index, block0, block1, *pieces)
        )

    part = columns // CHUNKS
    chunk = jax.ShapeDtypeStruct((width, part), F32)
    whole = jax.ShapeDtypeStruct((height, columns), F32)
    out = None
    tops = []
    for i in range(CHUNKS):
        at = functools.partial(lambda i, *_: (0, i), i)
        below = functools.partial(lambda i, *_: (1, i), i)
        held = [pl.BlockSpec(a.shape, lambda *_: (0, 0)) for a in (vth, vtl, ph, plo)]
        extra = trailing if out is None else out
        top, out = pl.pallas_call(
            functools.partial(leaf_apply, width),
            grid=(1,),
            out_shape=[chunk, whole],
            in_specs=[pl.BlockSpec((height, part), at)] + held + [pl.BlockSpec(memory_space=pl.ANY)],
            out_specs=[pl.BlockSpec((width, part), lambda *_: (0, 0)), pl.BlockSpec((height - width, part), below)],
            input_output_aliases={} if out is None else {5: 1},
            cost_estimate=cost(12 * height * width * part, 8 * height * part),
            name=f"leaf_{i}",
        )(trailing, vth, vtl, ph, plo, extra)
        tops.append(top)
    for level in range(depth):
        for i in range(CHUNKS):
            far = swap(tops[i], "row", 1 << level)
            last = level == depth - 1
            at = functools.partial(lambda i, *_: (0, i), i)
            zero = lambda *_: (0, 0)
            result = pl.pallas_call(
                functools.partial(level_apply, width),
                grid=(1,),
                out_shape=whole if last else chunk,
                in_specs=[pl.BlockSpec((width, part), zero)] * 2
                + [pl.BlockSpec((width, 2 * width), zero)] * 2
                + [pl.BlockSpec(memory_space=pl.ANY)] * last,
                out_specs=pl.BlockSpec((width, part), at if last else zero),
                input_output_aliases={4: 0} if last else {},
                cost_estimate=cost(12 * width * width * part, 12 * width * part),
                name=f"level{level}_{i}",
            )(tops[i], far, *factors[level], *([out] * last))
            if last:
                out = result
            else:
                tops[i] = result
    return out


def solution(mesh):
    return jax.shard_map(
        per_device,
        mesh=mesh,
        in_specs=(
            P("row", "col"),
            P(("row", "col"), None),
            P(("row", "col"), None),
            P(("row", "col"), None),
            P(("row", "col"), None),
        ),
        out_specs=P("row", "col"),
        check_vma=False,
    )
```

time: 222 us -> 154 us (0.69)
  blocking collectives: 61.3 us -> 0 us
  Pallas kernels: 0 us -> 58.4 us
  waiting for transfers between devices: 102 us -> 45.9 us
  matrix products: 44.7 us -> 0 us
  starting transfers between devices: 7.2 us -> 37.1 us
  local copies, waits for them, and re-layouts: 3.51 us -> 9.21 us
    all_gather x4 -> x0, blocking collectives: 61.3 us -> none  [the longest x1 17.6 us: per_device(): lax.all_gather(leaf_v, 'col', axis=0, tiled=True)]
    pallas_call x0 -> x21, Pallas kernels: none -> 58.4 us  [the longest x12 32.8 us: per_device(): pl.pallas_call(functools.partial(level_apply, width), grid=(1,), out_shap...]
    ppermute x9 -> x24, waiting for transfers between devices: 102 us -> 45.9 us  [swap(): lax.ppermute(value, axis, [(i, i ^ mask) for i in range(lax.axis_size(axi...]
    dot_general x12 -> x0, matrix products: 44.7 us -> none  [product(): jnp.dot(left, right, precision=lax.Precision.HIGHEST, preferred_element_t...]
    ppermute x9 -> x24, starting transfers between devices: 7.2 us -> 37.1 us  [swap(): lax.ppermute(value, axis, [(i, i ^ mask) for i in range(lax.axis_size(axi...]
    unnamed x18 -> x54, local copies, waits for them, and re-layouts: 1 us -> 9.21 us
    slice x1 -> x0, local copies, waits for them, and re-layouts: 2.51 us -> none  [per_device(): top = changed[:width]]
  transfers between devices with their start and end apart: 9 -> 24, of which waited for: 3 -> 10; matrix products, arithmetic and copies ran while one was open for 6% -> 0% of each run, Pallas kernels for 0% -> 25%
where the time goes in v1:
time: 154 us; the launch traced here: 153 us
  Pallas kernels  58.4 us (38%)
  waiting for transfers between devices  45.9 us (30%)
  starting transfers between devices  37.1 us (24%)
  local copies, waits for them, and re-layouts  9.21 us (6%)
  other arithmetic  2.53 us (2%)
    ppermute x24, waiting for transfers between devices, swap(): lax.ppermute(value, axis, [(i, i ^ mask) for i in range(lax.axis_size(axi...  45.9 us
    ppermute x24, starting transfers between devices, swap(): lax.ppermute(value, axis, [(i, i ^ mask) for i in range(lax.axis_size(axi...  37.1 us
    pallas_call x12, Pallas kernels, per_device(): pl.pallas_call(functools.partial(level_apply, width), grid=(1,), out_shap...  32.8 us
    pallas_call x4, Pallas kernels, per_device(): pl.pallas_call(functools.partial(leaf_apply, width), grid=(1,), out_shape...  14.3 us
    unnamed x54, local copies, waits for them, and re-layouts  9.21 us
    pallas_call x2, Pallas kernels, per_device(): pl.pallas_call(functools.partial(level_factors, level, n, tr, offset), ou...  4.68 us
  transfers between devices with their start and end apart: 24, of which 10 were waited for; matrix products, arithmetic and copies ran while one was open for 0% of the time, Pallas kernels for 25%

profile of v1, /device:TPU:0, one launch (start us, length us, event | category | flops | bytes accessed | tf_op | source)
XLA Modules:
  0.0 153.2 jit_solution(1143309894823865251)
XLA Ops:
  1.9 3.1 %collective-permute-start = (f32[256,256]{1,0:T(8,128)S(1)}, f32[256,256]{1,0:T(8,128)S(1)}, u32[]{:S(2)}, u32[]{:S(2)}) collective-permute-start(f32[256,256]{1,0:T(8,128)S(1)} %pad_maximum_fusion.refs_0_), channel_id=1, source_target_pairs={{0,1},{1,0},{2,3},{3,2},{4,5},{5,4},{6,7},{7,6},{8,9},{9,8},{10,11... | collective-permute-start | bytes 786440 | tf_op jit(solution)/shard_map/ppermute | solution.py:17
  8.2 7.9 %collective-permute-done.refs_1_ = f32[256,256]{1,0:T(8,128)S(1)} collective-permute-done((f32[256,256]{1,0:T(8,128)S(1)}, f32[256,256]{1,0:T(8,128)S(1)}, u32[]{:S(2)}, u32[]{:S(2)}) %collective-permute-start) | collective-permute-done | bytes 262176 | tf_op jit(solution)/shard_map/ppermute | solution.py:17
  16.1 10.2 %collective-permute-done.1.refs_2_ = f32[256,256]{1,0:T(8,128)S(1)} collective-permute-done((f32[256,256]{1,0:T(8,128)S(1)}, f32[256,256]{1,0:T(8,128)S(1)}, u32[]{:S(2)}, u32[]{:S(2)}) %collective-permute-start.1) | collective-permute-done | bytes 262176 | tf_op jit(solution)/shard_map/ppermute | solution.py:17
  30.4 3.5 %leaf_0.1 = (f32[256,512]{1,0:T(8,128)}, f32[512,2048]{1,0:T(8,128)}) custom-call(f32[512,2048]{1,0:T(8,128)} %c.7, bf16[256,512]{1,0:T(8,128)(2,1)} %get-tuple-element.29.vth, bf16[256,512]{1,0:T(8,128)(2,1)} %get-tuple-element.30.vtl, bf16[512,256]{1,0:T(8,128)(2,1)} %get-tuple-element.31.ph, bf16[512,256]{1,0:T(8,128)(2,1)} %get-tuple-element.32.plo, ...), custom_call_target="tpu_custom_call" | custom-call | flops 805306368 | bytes 2097152 | tf_op jit(solution)/shard_map/leaf_0/pallas_call | solution.py:182
  33.9 3.5 %leaf_1.1 = (f32[256,512]{1,0:T(8,128)}, f32[512,2048]{1,0:T(8,128)}) custom-call(f32[512,2048]{1,0:T(8,128)} %c.7, bf16[256,512]{1,0:T(8,128)(2,1)} %get-tuple-element.29.vth, bf16[256,512]{1,0:T(8,128)(2,1)} %get-tuple-element.30.vtl, bf16[512,256]{1,0:T(8,128)(2,1)} %get-tuple-element.31.ph, ...), custom_call_target="tpu_custom_call", output_to_operand_aliasing={{1}: (5, {})} | custom-call | flops 805306368 | bytes 2097152 | tf_op jit(solution)/shard_map/leaf_1/pallas_call | solution.py:182
  37.4 3.5 %leaf_2.1 = (f32[256,512]{1,0:T(8,128)}, f32[512,2048]{1,0:T(8,128)}) custom-call(f32[512,2048]{1,0:T(8,128)} %c.7, bf16[256,512]{1,0:T(8,128)(2,1)} %get-tuple-element.29.vth, bf16[256,512]{1,0:T(8,128)(2,1)} %get-tuple-element.30.vtl, bf16[512,256]{1,0:T(8,128)(2,1)} %get-tuple-element.31.ph, ...), custom_call_target="tpu_custom_call", output_to_operand_aliasing={{1}: (5, {})} | custom-call | flops 805306368 | bytes 2097152 | tf_op jit(solution)/shard_map/leaf_2/pallas_call | solution.py:182
  41.0 3.7 %leaf_3.1 = (f32[256,512]{1,0:T(8,128)}, f32[512,2048]{1,0:T(8,128)}) custom-call(f32[512,2048]{1,0:T(8,128)} %c.7, bf16[256,512]{1,0:T(8,128)(2,1)} %get-tuple-element.29.vth, bf16[256,512]{1,0:T(8,128)(2,1)} %get-tuple-element.30.vtl, bf16[512,256]{1,0:T(8,128)(2,1)} %get-tuple-element.31.ph, ...), custom_call_target="tpu_custom_call", output_to_operand_aliasing={{1}: (5, {})} | custom-call | flops 805306368 | bytes 2097152 | tf_op jit(solution)/shard_map/leaf_3/pallas_call | solution.py:182
  45.7 3.1 %collective-permute-done.4.far = f32[256,256]{1,0:T(8,128)S(1)} collective-permute-done((f32[256,256]{1,0:T(8,128)S(1)}, f32[256,256]{1,0:T(8,128)S(1)}, u32[]{:S(2)}, u32[]{:S(2)}) %collective-permute-start.4) | collective-permute-done | bytes 262176 | tf_op jit(solution)/shard_map/ppermute | solution.py:17
  54.1 2.7 %level0_3.1.own = f32[256,512]{1,0:T(8,128)} custom-call(f32[256,512]{1,0:T(8,128)} %get-tuple-element.36.own, f32[256,512]{1,0:T(8,128)} %copy-done.15, bf16[256,512]{1,0:T(8,128)(2,1)} %get-tuple-element.38.fh, bf16[256,512]{1,0:T(8,128)(2,1)} %get-tuple-element.39.fl), custom_call_target="tpu_custom_call" | custom-call | flops 402653184 | bytes 1572864 | tf_op jit(solution)/shard_map/level0_3/pallas_call | solution.py:199
  57.6 2.7 %level0_2.1.own = f32[256,512]{1,0:T(8,128)} custom-call(f32[256,512]{1,0:T(8,128)} %get-tuple-element.49.own, f32[256,512]{1,0:T(8,128)} %collective-permute-done.15.far, bf16[256,512]{1,0:T(8,128)(2,1)} %get-tuple-element.38.fh, bf16[256,512]{1,0:T(8,128)(2,1)} %get-tuple-element.39.fl), custom_call_target="tpu_custom_call" | custom-call | flops 402653184 | bytes 1572864 | tf_op jit(solution)/shard_map/level0_2/pallas_call | solution.py:199
  61.7 2.7 %level0_0.1.own = f32[256,512]{1,0:T(8,128)} custom-call(f32[256,512]{1,0:T(8,128)} %get-tuple-element.51.own, f32[256,512]{1,0:T(8,128)} %collective-permute-done.21.far, bf16[256,512]{1,0:T(8,128)(2,1)} %get-tuple-element.38.fh, bf16[256,512]{1,0:T(8,128)(2,1)} %get-tuple-element.39.fl), custom_call_target="tpu_custom_call" | custom-call | flops 402653184 | bytes 1572864 | tf_op jit(solution)/shard_map/level0_0/pallas_call | solution.py:199
  69.2 4.1 %collective-permute-start.8 = (f32[128,256]{1,0:T(8,128)S(1)}, f32[128,256]{1,0:T(8,128)S(1)}, u32[]{:S(2)}, u32[]{:S(2)}) collective-permute-start(f32[128,256]{1,0:T(8,128)S(1)} %pad_maximum_fusion.1.refs_0_.refs_2_), channel_id=1, source_target_pairs={{0,1},{1,0},{2,3},{3,2},{4,5},{5,4},{6,7},{7,6},{8,9},{9,8},{10,11... | collective-permute-start | bytes 393224 | tf_op jit(solution)/shard_map/ppermute | solution.py:17
  73.4 2.9 %collective-permute-done.8.refs_1_.refs_3_ = f32[128,256]{1,0:T(8,128)S(1)} collective-permute-done((f32[128,256]{1,0:T(8,128)S(1)}, f32[128,256]{1,0:T(8,128)S(1)}, u32[]{:S(2)}, u32[]{:S(2)}) %collective-permute-start.8) | collective-permute-done | bytes 131104 | tf_op jit(solution)/shard_map/ppermute | solution.py:17
  76.3 3.0 %collective-permute-start.9 = (f32[128,256]{1,0:T(8,128)S(1)}, f32[128,256]{1,0:T(8,128)S(1)}, u32[]{:S(2)}, u32[]{:S(2)}) collective-permute-start(f32[128,256]{1,0:T(8,128)S(1)} %pad_maximum_fusion.1.refs_0_.refs_2_), channel_id=1, source_target_pairs={{0,2},{1,3},{2,0},{3,1},{4,6},{5,7},{6,4},{7,5},{8,10},{9,11},{10,... | collective-permute-start | bytes 393224 | tf_op jit(solution)/shard_map/ppermute | solution.py:17
  79.3 4.6 %collective-permute-done.9.refs_2_.refs_4_ = f32[128,256]{1,0:T(8,128)S(1)} collective-permute-done((f32[128,256]{1,0:T(8,128)S(1)}, f32[128,256]{1,0:T(8,128)S(1)}, u32[]{:S(2)}, u32[]{:S(2)}) %collective-permute-start.9) | collective-permute-done | bytes 131104 | tf_op jit(solution)/shard_map/ppermute | solution.py:17
  86.2 4.5 %collective-permute-done.10.refs_3_.refs_5_ = f32[128,256]{1,0:T(8,128)S(1)} collective-permute-done((f32[128,256]{1,0:T(8,128)S(1)}, f32[128,256]{1,0:T(8,128)S(1)}, u32[]{:S(2)}, u32[]{:S(2)}) %collective-permute-start.10) | collective-permute-done | bytes 131104 | tf_op jit(solution)/shard_map/ppermute | solution.py:17
  100.5 4.2 %collective-permute-done.19.far = f32[256,512]{1,0:T(8,128)S(1)} collective-permute-done((f32[256,512]{1,0:T(8,128)}, f32[256,512]{1,0:T(8,128)S(1)}, u32[]{:S(2)}, u32[]{:S(2)}) %collective-permute-start.19) | collective-permute-done | bytes 524320 | tf_op jit(solution)/shard_map/ppermute | solution.py:17
  105.5 2.7 %level1_1.1.own = f32[256,512]{1,0:T(8,128)} custom-call(f32[256,512]{1,0:T(8,128)} %level0_1.1.own, f32[256,512]{1,0:T(8,128)} %copy-done.14, bf16[256,512]{1,0:T(8,128)(2,1)} %get-tuple-element.44.fh, bf16[256,512]{1,0:T(8,128)(2,1)} %get-tuple-element.45.fl), custom_call_target="tpu_custom_call" | custom-call | flops 402653184 | bytes 1572864 | tf_op jit(solution)/shard_map/level1_1/pallas_call | solution.py:199
  114.6 2.7 %level1_3.1.own = f32[256,512]{1,0:T(8,128)} custom-call(f32[256,512]{1,0:T(8,128)} %level0_3.1.own, f32[256,512]{1,0:T(8,128)} %copy-done.7, bf16[256,512]{1,0:T(8,128)(2,1)} %get-tuple-element.44.fh, bf16[256,512]{1,0:T(8,128)(2,1)} %get-tuple-element.45.fl), custom_call_target="tpu_custom_call" | custom-call | flops 402653184 | bytes 1572864 | tf_op jit(solution)/shard_map/level1_3/pallas_call | solution.py:199
  118.3 4.1 %collective-permute-start.12 = (f32[64,256]{1,0:T(8,128)S(1)}, f32[64,256]{1,0:T(8,128)S(1)}, u32[]{:S(2)}, u32[]{:S(2)}) collective-permute-start(f32[64,256]{1,0:T(8,128)S(1)} %collective-permute-done.7.refs_2_), channel_id=1, source_target_pairs={{0,1},{1,0},{2,3},{3,2},{4,5},{5,4},{6,7},{7,6},{8,9},{9,8},{10,11... | collective-permute-start | bytes 196616 | tf_op jit(solution)/shard_map/ppermute | solution.py:17
  124.7 3.0 %collective-permute-start.13 = (f32[64,256]{1,0:T(8,128)S(1)}, f32[64,256]{1,0:T(8,128)S(1)}, u32[]{:S(2)}, u32[]{:S(2)}) collective-permute-start(f32[64,256]{1,0:T(8,128)S(1)} %collective-permute-done.7.refs_2_), channel_id=1, source_target_pairs={{0,2},{1,3},{2,0},{3,1},{4,6},{5,7},{6,4},{7,5},{8,10},{9,11},{10,... | collective-permute-start | bytes 196616 | tf_op jit(solution)/shard_map/ppermute | solution.py:17
  132.3 3.8 %collective-permute-done.14.refs_5_ = f32[64,256]{1,0:T(8,128)S(1)} collective-permute-done((f32[64,256]{1,0:T(8,128)S(1)}, f32[64,256]{1,0:T(8,128)S(1)}, u32[]{:S(2)}, u32[]{:S(2)}) %collective-permute-start.14) | collective-permute-done | bytes 65568 | tf_op jit(solution)/shard_map/ppermute | solution.py:17
  139.8 2.7 %level2_0.1.refs_0_ = f32[512,2048]{1,0:T(8,128)} custom-call(f32[256,512]{1,0:T(8,128)} %level1_0.1.own, f32[256,512]{1,0:T(8,128)} %copy-done.3, bf16[256,512]{1,0:T(8,128)(2,1)} %get-tuple-element.47.fh, bf16[256,512]{1,0:T(8,128)(2,1)} %get-tuple-element.48.fl, f32[512,2048]{1,0:T(8,128)} %get-tuple-element.52.refs_0_), custom_call_target="tpu_custom_call", output_to_operand_aliasing={{}: (4, {})} | custom-call | flops 402653184 | bytes 1572864 | tf_op jit(solution)/shard_map/level2_0/pallas_call | solution.py:199
  143.4 2.7 %level2_1.1.refs_0_ = f32[512,2048]{1,0:T(8,128)} custom-call(f32[256,512]{1,0:T(8,128)} %level1_1.1.own, f32[256,512]{1,0:T(8,128)} %copy-done.4, bf16[256,512]{1,0:T(8,128)(2,1)} %get-tuple-element.47.fh, bf16[256,512]{1,0:T(8,128)(2,1)} %get-tuple-element.48.fl, f32[512,2048]{1,0:T(8,128)} %level2_0.1.refs_0_), custom_call_target="tpu_custom_call", output_to_operand_aliasing={{}: (4, {})} | custom-call | flops 402653184 | bytes 1572864 | tf_op jit(solution)/shard_map/level2_1/pallas_call | solution.py:199
  (103 shorter events, 60.9 us)
Async XLA Ops:
  1.9 14.2 %collective-permute-start = (f32[256,256]{1,0:T(8,128)S(1)}, f32[256,256]{1,0:T(8,128)S(1)}, u32[]{:S(2)}, u32[]{:S(2)}) collective-permute-start(f32[256,256]{1,0:T(8,128)S(1)} %pad_maximum_fusion.refs_0_), channel_id=1, source_target_pairs={{0,1},{1,0},{2,3},{3,2},{4,5},{5,4},{6,7},{7,6},{8,9},{9,8},{10,11... | collective-permute-start | bytes 786440 | tf_op jit(solution)/shard_map/ppermute | solution.py:17
  5.0 21.4 %collective-permute-start.1 = (f32[256,256]{1,0:T(8,128)S(1)}, f32[256,256]{1,0:T(8,128)S(1)}, u32[]{:S(2)}, u32[]{:S(2)}) collective-permute-start(f32[256,256]{1,0:T(8,128)S(1)} %pad_maximum_fusion.refs_0_), channel_id=1, source_target_pairs={{0,2},{1,3},{2,0},{3,1},{4,6},{5,7},{6,4},{7,5},{8,10},{9,11},{10,... | collective-permute-start | bytes 786440 | tf_op jit(solution)/shard_map/ppermute | solution.py:17
  7.6 18.8 %collective-permute-start.2 = (f32[256,256]{1,0:T(8,128)S(1)}, f32[256,256]{1,0:T(8,128)S(1)}, u32[]{:S(2)}, u32[]{:S(2)}) collective-permute-start(f32[256,256]{1,0:T(8,128)S(1)} %pad_maximum_fusion.refs_0_), channel_id=1, source_target_pairs={{0,3},{1,2},{2,1},{3,0},{4,7},{5,6},{6,5},{7,4},{8,11},{9,10},{10,... | collective-permute-start | bytes 786440 | tf_op jit(solution)/shard_map/ppermute | solution.py:17
  44.6 8.0 %collective-permute-start.3 = (f32[256,512]{1,0:T(8,128)}, f32[256,512]{1,0:T(8,128)S(1)}, u32[]{:S(2)}, u32[]{:S(2)}) collective-permute-start(f32[256,512]{1,0:T(8,128)} %get-tuple-element.36.own), channel_id=1, source_target_pairs={{0,4},{4,0},{8,12},{12,8},{16,20},{20,16},{24,28},{28,24},{1,5},{5... | collective-permute-start | bytes 1572872 | tf_op jit(solution)/shard_map/ppermute | solution.py:17
  44.6 12.3 %collective-permute-start.15 = (f32[256,512]{1,0:T(8,128)S(1)}, f32[256,512]{1,0:T(8,128)}, u32[]{:S(2)}, u32[]{:S(2)}) collective-permute-start(f32[256,512]{1,0:T(8,128)S(1)} %copy-done.11), channel_id=1, source_target_pairs={{0,4},{4,0},{8,12},{12,8},{16,20},{20,16},{24,28},{28,24},{1,5},{5... | collective-permute-start | bytes 1572872 | tf_op jit(solution)/shard_map/ppermute | solution.py:17
  45.1 15.2 %collective-permute-start.21 = (f32[256,512]{1,0:T(8,128)S(1)}, f32[256,512]{1,0:T(8,128)}, u32[]{:S(2)}, u32[]{:S(2)}) collective-permute-start(f32[256,512]{1,0:T(8,128)S(1)} %copy-done.10), channel_id=1, source_target_pairs={{0,4},{4,0},{8,12},{12,8},{16,20},{20,16},{24,28},{28,24},{1,5},{5... | collective-permute-start | bytes 1572872 | tf_op jit(solution)/shard_map/ppermute | solution.py:17
  45.2 19.2 %collective-permute-start.18 = (f32[256,512]{1,0:T(8,128)S(1)}, f32[256,512]{1,0:T(8,128)S(1)}, u32[]{:S(2)}, u32[]{:S(2)}) collective-permute-start(f32[256,512]{1,0:T(8,128)S(1)} %copy-done.8), channel_id=1, source_target_pairs={{0,4},{4,0},{8,12},{12,8},{16,20},{20,16},{24,28},{28,24},{1,5},{5... | collective-permute-start | bytes 1572872 | tf_op jit(solution)/shard_map/ppermute | solution.py:17
  45.7 3.2 %collective-permute-start.4 = (f32[256,256]{1,0:T(8,128)S(1)}, f32[256,256]{1,0:T(8,128)S(1)}, u32[]{:S(2)}, u32[]{:S(2)}) collective-permute-start(f32[256,256]{1,0:T(8,128)S(1)} %copy-done), channel_id=1, source_target_pairs={{0,4},{4,0},{8,12},{12,8},{16,20},{20,16},{24,28},{28,24},{1,5},{5... | collective-permute-start | bytes 786440 | tf_op jit(solution)/shard_map/ppermute | solution.py:17
  48.9 19.1 %collective-permute-start.6 = (f32[64,256]{1,0:T(8,128)S(1)}, f32[64,256]{1,0:T(8,128)S(1)}, u32[]{:S(2)}, u32[]{:S(2)}) collective-permute-start(f32[64,256]{1,0:T(8,128)S(1)} %get-tuple-element.56), channel_id=1, source_target_pairs={{0,8},{4,12},{8,0},{12,4},{16,24},{20,28},{24,16},{28,20},{1,9},{5... | collective-permute-start | bytes 196616 | tf_op jit(solution)/shard_map/ppermute | solution.py:17
  52.6 16.6 %collective-permute-start.7 = (f32[64,256]{1,0:T(8,128)S(1)}, f32[64,256]{1,0:T(8,128)S(1)}, u32[]{:S(2)}, u32[]{:S(2)}) collective-permute-start(f32[64,256]{1,0:T(8,128)S(1)} %get-tuple-element.53), channel_id=1, source_target_pairs={{0,16},{4,20},{8,24},{12,28},{16,0},{20,4},{24,8},{28,12},{1,17},{... | collective-permute-start | bytes 196616 | tf_op jit(solution)/shard_map/ppermute | solution.py:17
  56.9 56.9 %collective-permute-start.5 = (f32[256,512]{1,0:T(8,128)}, f32[256,512]{1,0:T(8,128)S(1)}, u32[]{:S(2)}, u32[]{:S(2)}) collective-permute-start(f32[256,512]{1,0:T(8,128)} %level0_3.1.own), channel_id=1, source_target_pairs={{0,8},{4,12},{8,0},{12,4},{16,24},{20,28},{24,16},{28,20},{1,9},{5... | collective-permute-start | bytes 1572872 | tf_op jit(solution)/shard_map/ppermute | solution.py:17
  60.3 48.9 %collective-permute-start.16 = (f32[256,512]{1,0:T(8,128)}, f32[256,512]{1,0:T(8,128)S(1)}, u32[]{:S(2)}, u32[]{:S(2)}) collective-permute-start(f32[256,512]{1,0:T(8,128)} %level0_2.1.own), channel_id=1, source_target_pairs={{0,8},{4,12},{8,0},{12,4},{16,24},{20,28},{24,16},{28,20},{1,9},{5... | collective-permute-start | bytes 1572872 | tf_op jit(solution)/shard_map/ppermute | solution.py:17
  64.4 31.2 %collective-permute-start.22 = (f32[256,512]{1,0:T(8,128)}, f32[256,512]{1,0:T(8,128)S(1)}, u32[]{:S(2)}, u32[]{:S(2)}) collective-permute-start(f32[256,512]{1,0:T(8,128)} %level0_0.1.own), channel_id=1, source_target_pairs={{0,8},{4,12},{8,0},{12,4},{16,24},{20,28},{24,16},{28,20},{1,9},{5... | collective-permute-start | bytes 1572872 | tf_op jit(solution)/shard_map/ppermute | solution.py:17
  67.9 36.7 %collective-permute-start.19 = (f32[256,512]{1,0:T(8,128)}, f32[256,512]{1,0:T(8,128)S(1)}, u32[]{:S(2)}, u32[]{:S(2)}) collective-permute-start(f32[256,512]{1,0:T(8,128)} %level0_1.1.own), channel_id=1, source_target_pairs={{0,8},{4,12},{8,0},{12,4},{16,24},{20,28},{24,16},{28,20},{1,9},{5... | collective-permute-start | bytes 1572872 | tf_op jit(solution)/shard_map/ppermute | solution.py:17
  69.2 7.1 %collective-permute-start.8 = (f32[128,256]{1,0:T(8,128)S(1)}, f32[128,256]{1,0:T(8,128)S(1)}, u32[]{:S(2)}, u32[]{:S(2)}) collective-permute-start(f32[128,256]{1,0:T(8,128)S(1)} %pad_maximum_fusion.1.refs_0_.refs_2_), channel_id=1, source_target_pairs={{0,1},{1,0},{2,3},{3,2},{4,5},{5,4},{6,7},{7,6},{8,9},{9,8},{10,11... | collective-permute-start | bytes 393224 | tf_op jit(solution)/shard_map/ppermute | solution.py:17
  76.3 7.6 %collective-permute-start.9 = (f32[128,256]{1,0:T(8,128)S(1)}, f32[128,256]{1,0:T(8,128)S(1)}, u32[]{:S(2)}, u32[]{:S(2)}) collective-permute-start(f32[128,256]{1,0:T(8,128)S(1)} %pad_maximum_fusion.1.refs_0_.refs_2_), channel_id=1, source_target_pairs={{0,2},{1,3},{2,0},{3,1},{4,6},{5,7},{6,4},{7,5},{8,10},{9,11},{10,... | collective-permute-start | bytes 393224 | tf_op jit(solution)/shard_map/ppermute | solution.py:17
  83.9 6.8 %collective-permute-start.10 = (f32[128,256]{1,0:T(8,128)S(1)}, f32[128,256]{1,0:T(8,128)S(1)}, u32[]{:S(2)}, u32[]{:S(2)}) collective-permute-start(f32[128,256]{1,0:T(8,128)S(1)} %pad_maximum_fusion.1.refs_0_.refs_2_), channel_id=1, source_target_pairs={{0,3},{1,2},{2,1},{3,0},{4,7},{5,6},{6,5},{7,4},{8,11},{9,10},{10,... | collective-permute-start | bytes 393224 | tf_op jit(solution)/shard_map/ppermute | solution.py:17
  99.1 39.9 %collective-permute-start.23 = (f32[256,512]{1,0:T(8,128)}, f32[256,512]{1,0:T(8,128)S(1)}, u32[]{:S(2)}, u32[]{:S(2)}) collective-permute-start(f32[256,512]{1,0:T(8,128)} %level1_0.1.own), channel_id=1, source_target_pairs={{0,16},{4,20},{8,24},{12,28},{16,0},{20,4},{24,8},{28,12},{1,17},{... | collective-permute-start | bytes 1572872 | tf_op jit(solution)/shard_map/ppermute | solution.py:17
  108.2 34.4 %collective-permute-start.20 = (f32[256,512]{1,0:T(8,128)}, f32[256,512]{1,0:T(8,128)S(1)}, u32[]{:S(2)}, u32[]{:S(2)}) collective-permute-start(f32[256,512]{1,0:T(8,128)} %level1_1.1.own), channel_id=1, source_target_pairs={{0,16},{4,20},{8,24},{12,28},{16,0},{20,4},{24,8},{28,12},{1,17},{... | collective-permute-start | bytes 1572872 | tf_op jit(solution)/shard_map/ppermute | solution.py:17
  112.8 33.3 %collective-permute-start.17 = (f32[256,512]{1,0:T(8,128)}, f32[256,512]{1,0:T(8,128)S(1)}, u32[]{:S(2)}, u32[]{:S(2)}) collective-permute-start(f32[256,512]{1,0:T(8,128)} %level1_2.1.own), channel_id=1, source_target_pairs={{0,16},{4,20},{8,24},{12,28},{16,0},{20,4},{24,8},{28,12},{1,17},{... | collective-permute-start | bytes 1572872 | tf_op jit(solution)/shard_map/ppermute | solution.py:17
  117.3 32.4 %collective-permute-start.11 = (f32[256,512]{1,0:T(8,128)}, f32[256,512]{1,0:T(8,128)S(1)}, u32[]{:S(2)}, u32[]{:S(2)}) collective-permute-start(f32[256,512]{1,0:T(8,128)} %level1_3.1.own), channel_id=1, source_target_pairs={{0,16},{4,20},{8,24},{12,28},{16,0},{20,4},{24,8},{28,12},{1,17},{... | collective-permute-start | bytes 1572872 | tf_op jit(solution)/shard_map/ppermute | solution.py:17
  118.3 6.3 %collective-permute-start.12 = (f32[64,256]{1,0:T(8,128)S(1)}, f32[64,256]{1,0:T(8,128)S(1)}, u32[]{:S(2)}, u32[]{:S(2)}) collective-permute-start(f32[64,256]{1,0:T(8,128)S(1)} %collective-permute-done.7.refs_2_), channel_id=1, source_target_pairs={{0,1},{1,0},{2,3},{3,2},{4,5},{5,4},{6,7},{7,6},{8,9},{9,8},{10,11... | collective-permute-start | bytes 196616 | tf_op jit(solution)/shard_map/ppermute | solution.py:17
  124.7 5.3 %collective-permute-start.13 = (f32[64,256]{1,0:T(8,128)S(1)}, f32[64,256]{1,0:T(8,128)S(1)}, u32[]{:S(2)}, u32[]{:S(2)}) collective-permute-start(f32[64,256]{1,0:T(8,128)S(1)} %collective-permute-done.7.refs_2_), channel_id=1, source_target_pairs={{0,2},{1,3},{2,0},{3,1},{4,6},{5,7},{6,4},{7,5},{8,10},{9,11},{10,... | collective-permute-start | bytes 196616 | tf_op jit(solution)/shard_map/ppermute | solution.py:17
  129.9 6.2 %collective-permute-start.14 = (f32[64,256]{1,0:T(8,128)S(1)}, f32[64,256]{1,0:T(8,128)S(1)}, u32[]{:S(2)}, u32[]{:S(2)}) collective-permute-start(f32[64,256]{1,0:T(8,128)S(1)} %collective-permute-done.7.refs_2_), channel_id=1, source_target_pairs={{0,3},{1,2},{2,1},{3,0},{4,7},{5,6},{6,5},{7,4},{8,11},{9,10},{10,... | collective-permute-start | bytes 196616 | tf_op jit(solution)/shard_map/ppermute | solution.py:17
  (27 other events, 191.8 us)

commit v2 on v0

v2 whole, which is shorter than its diff:
```python
import functools

import jax
import jax.numpy as jnp
from jax import lax
from jax.experimental import pallas as pl
from jax.experimental.pallas import tpu as pltpu
from jax.sharding import PartitionSpec as P

CHUNKS = 8
STEP = 512
F32, BF16 = jnp.float32, jnp.bfloat16
VMEM = pl.BlockSpec(memory_space=pltpu.VMEM)
ANY = pl.BlockSpec(memory_space=pl.ANY)
TOKEN = pltpu.VMEM((8, 128), F32)


def call(kernel, name, args, outs, scratch=(), hbm_in=(), hbm_out=(), alias=None, after=()):
    count, waits = len(args), len(after)

    def body(*refs):
        kernel(*refs[:count], *refs[count + waits:])

    spaces = [pltpu.HBM if k in hbm_in else pltpu.VMEM for k in range(count)] + [pltpu.VMEM] * waits
    return pl.pallas_call(
        body,
        out_shape=[jax.ShapeDtypeStruct(o.shape, o.dtype) if k in hbm_out else o for k, o in enumerate(outs)],
        in_specs=[ANY if s is pltpu.HBM else VMEM for s in spaces],
        out_specs=[ANY if k in hbm_out else VMEM for k in range(len(outs))],
        scratch_shapes=list(scratch),
        input_output_aliases=alias or {},
        compiler_params=pltpu.CompilerParams(vmem_limit_bytes=20 << 20),
        cost_estimate=pl.CostEstimate(flops=1000, bytes_accessed=1000, transcendentals=0),
        name=name,
    )(*map(pltpu.with_memory_space_constraint, (*args, *after), spaces))


def swap(value, axis, mask):
    return lax.ppermute(value, axis, [(i, i ^ mask) for i in range(lax.axis_size(axis))])


def spread(piece, axis):
    n = lax.axis_size(axis)
    if n != 4:
        return [piece] + [swap(piece, axis, k) for k in range(1, n)]
    second = swap(piece, axis, 2)
    first = swap(piece, axis, 1)
    middle = lax.ppermute(piece, axis, [(1, 2), (2, 1)])
    ends = lax.ppermute(second, axis, [(1, 0), (2, 3)])
    return [piece, first, second, middle, ends]


def split(x):
    high = x.astype(BF16)
    return high, (x - high.astype(F32)).astype(BF16)


def dot3(ah, al, bh, bl, dims=((1,), (0,))):
    d = functools.partial(lax.dot_general, dimension_numbers=(dims, ((), ())), preferred_element_type=F32)
    return d(ah, bh) + (d(ah, bl) + d(al, bh))


def dotf(a, b, dims=((1,), (0,))):
    return dot3(*split(a), *split(b), dims)


def bit_of(level):
    return (lax.axis_index("row") >> level) & 1


def place(pieces, offset, rows, out):
    mine = lax.axis_index("col")

    def put(k, piece):
        to = pl.ds(pl.multiple_of((mine ^ k) * rows, rows), rows)
        out[to, :] = piece[pl.ds(offset, rows), :]

    whole = pieces if out.shape[0] == rows * len(pieces) else pieces[:-2]
    for k, piece in enumerate(whole):
        put(k, piece)
    if len(whole) < len(pieces):
        inner = (mine == 1) | (mine == 2)
        pl.when(inner)(lambda: put(3, pieces[-2]))
        pl.when(jnp.logical_not(inner))(lambda: put(3, pieces[-1]))


def pack(*refs):
    *sources, out, sems = refs
    copies, start = [], 0
    for k, source in enumerate(sources):
        copies.append(pltpu.make_async_copy(source, out.at[pl.ds(start, source.shape[0])], sems.at[k]))
        copies[-1].start()
        start += source.shape[0]
    for c in copies:
        c.wait()


def tree_blocks(n, start, rows, *refs):
    pieces, outs = refs[:n], refs[n:]
    for level, out in enumerate(outs):
        place(pieces, pl.multiple_of(start + bit_of(level) * rows, rows), rows, out)


def level_factors(level, own, far, fh, fl):
    width = own.shape[0]

    @pl.when(bit_of(level) == 0)
    def _():
        s, y = own[...], far[...]
        fh[:, :width], fl[:, :width] = split(s.T)
        fh[:, width:], fl[:, width:] = split(dotf(y, s).T)

    @pl.when(bit_of(level) == 1)
    def _():
        y, s = own[...], far[...]
        ys = dotf(y, s, ((1,), (1,)))
        fh[:, width:], fl[:, width:] = split(ys)
        fh[:, :width], fl[:, :width] = split(dotf(ys, y, ((1,), (1,))))


def load(c, out, high, low, buffer, sems):
    size = buffer.shape[2]
    copies = []
    for k in range(buffer.shape[0]):
        copies.append(pltpu.make_async_copy(c.at[:, pl.ds(k * size, size)], buffer.at[k], sems.at[k]))
        copies[-1].start()
    for k, copy in enumerate(copies):
        at = pl.ds(k * size, size)
        copy.wait()
        out[:, at] = buffer[k]
        high[:, at], low[:, at] = split(buffer[k])


def leaf_factors(n, vr, tr, *refs):
    pieces, (vth, vtl, ph, plo), (v, t) = refs[:n], refs[n:n + 4], refs[n + 4:]
    place(pieces, 0, vr, v)
    place(pieces, vr, tr, t)
    full = v[...]
    vth[...], vtl[...] = split(full.T)
    ph[...], plo[...] = split(dotf(full, t[...], ((1,), (1,))))


def leaf_apply(start, c, ch, cl, vth, vtl, ph, plo, top, *outs):
    width, size = top.shape
    at = pl.ds(start, size)
    h, l = split(dot3(vth[...], vtl[...], ch[:, at], cl[:, at]))
    if len(outs) == 2:
        outs[0][...], outs[1][...] = h, l
        top[...] = c[:width, at] - dot3(ph[:width, :], plo[:width, :], h, l)
    else:
        change = dot3(ph[...], plo[...], h, l)
        top[...] = c[:width, at] - change[:width]
        outs[0][...] = c[width:, at] - change[width:]


def rest_apply(start, c, ph, plo, ih, il, out):
    width, size = ih.shape
    out[...] = c[width:, pl.ds(start, size)] - dot3(ph[width:, :], plo[width:, :], ih[...], il[...])


def level_result(start, own, far, fh, fl, size):
    width = own.shape[0]
    mine, other = own[:, pl.ds(start, size)], far[:, pl.ds(start, size)]
    change = dot3(fh[:, :width], fl[:, :width], *split(mine)) + dot3(fh[:, width:], fl[:, width:], *split(other))
    return mine - change


def level_apply(start, own, far, fh, fl, out):
    out[...] = level_result(start, own, far, fh, fl, out.shape[1])


def store(sources, out, top, sems):
    copies = []
    for k, source in enumerate(sources):
        rows, size = source.shape
        to = out.at[pl.ds(top, rows), pl.ds(k * size, size)]
        copies.append(pltpu.make_async_copy(source, to, sems.at[k]))
        copies[-1].start()
    return copies


def lower_store(*refs):
    *sources, out, sems = refs
    for copy in store(sources, out, out.shape[0] - sources[0].shape[0], sems):
        copy.wait()


def last_apply(own, far, fh, fl, *refs):
    *sources, _, out, buffer, sems = refs
    copies = store(sources, out, 0, sems)
    width, size = own.shape
    buffer[...] = level_result(0, own, far, fh, fl, size)
    to = out.at[pl.ds(0, width), pl.ds(len(sources) * size, size)]
    copies.append(pltpu.make_async_copy(buffer, to, sems.at[len(sources)]))
    copies[-1].start()
    for copy in copies:
        copy.wait()


def per_device(trailing, leaf_v, leaf_t, tree_y, tree_t):
    height, columns = trailing.shape
    width = leaf_v.shape[1]
    vr, tr = leaf_v.shape[0], leaf_t.shape[0]
    depth = lax.axis_size("row").bit_length() - 1
    part = columns // CHUNKS
    steps = columns // STEP
    block, block16 = pltpu.VMEM((width, width), F32), lambda *shape: pltpu.VMEM(shape, BF16)

    (packed,) = call(
        pack,
        "pack",
        (leaf_v, leaf_t, tree_t, tree_y),
        [pltpu.VMEM((vr + 3 * tr, width), F32)],
        [pltpu.SemaphoreType.DMA((4,))],
        hbm_in=range(4),
    )
    pieces = spread(packed, "col")
    c, ch, cl = call(
        load,
        "load",
        (trailing,),
        [pltpu.VMEM((height, columns), F32)] + [block16(height, columns)] * 2,
        [pltpu.VMEM((steps, height, STEP), F32), pltpu.SemaphoreType.DMA((steps,))],
        hbm_in=(0,),
        after=pieces[2:3],
    )
    owns = call(functools.partial(tree_blocks, len(pieces), vr + tr, tr), "tree_blocks", pieces, [block] * depth, after=[ch])
    factors = [
        call(
            functools.partial(level_factors, level),
            f"factors{level}",
            (owns[level], swap(owns[level], "row", 1 << level)),
            [block16(width, 2 * width)] * 2,
        )
        for level in range(depth)
    ]
    vth, vtl, ph, plo = call(
        functools.partial(leaf_factors, len(pieces), vr, tr),
        "leaf_factors",
        pieces,
        [block16(width, height)] * 2 + [block16(height, width)] * 2,
        [pltpu.VMEM((height, width), F32), block],
    )

    made = [[] for _ in range(depth - 1)]
    sent = [[] for _ in range(depth - 1)]
    pending = {}

    def advance(level, own, far, at, waits):
        (chunk,) = call(
            functools.partial(level_apply, at),
            f"level{level}",
            (own, far, *factors[level]),
            [pltpu.VMEM((width, part), F32)],
            after=waits,
        )
        made[level].append(chunk)
        sent[level].append(swap(chunk, "row", 2 << level))

    def later(k):
        for level in range(1, depth - 1):
            waits = [made[0][1]] if level == 1 and k == 0 else []
            if level == 1 and k == 1:
                waits = [factors[-1][0]]
            if level == depth - 2 and k >= 2:
                waits = done[k - 2:k - 1]
            advance(level, made[level - 1][k], sent[level - 1][k], 0, waits)

    done, rests, tops, fars = [], [], [], []

    def leaf(k):
        above, below = pltpu.VMEM((width, part), F32), pltpu.VMEM((height - width, part), F32)
        top, *others = call(
            functools.partial(leaf_apply, k * part),
            f"leaf_{k}",
            (c, ch, cl, vth, vtl, ph, plo),
            [above] + ([block16(width, part)] * 2 if k < 2 else [below]),
            after=tops if k == 1 else made[0][k - 2:k - 1] if k else (),
        )
        if k < 2:
            others = call(
                functools.partial(rest_apply, k * part), f"rest_{k}", (c, ph, plo, *others), [below], after=made[0][k:k + 1]
            )
        rests.extend(others)
        tops.append(top)
        fars.append(swap(top, "row", 1))

    def first_level(k):
        waits = made[min(1, depth - 2)][k - 2:k - 1] if k >= 2 else [factors[1][0]] * k
        advance(0, tops[k], fars[k], 0, waits)

    leaf(0)
    leaf(1)
    first_level(0)
    first_level(1)
    leaf(2)
    for k in range(CHUNKS):
        later(k)
        if k + 2 < CHUNKS:
            first_level(k + 2)
        if k + 3 < CHUNKS:
            leaf(k + 3)
        if k < CHUNKS - 1:
            done += call(
                functools.partial(level_apply, 0),
                "last",
                (made[-1][k], sent[-1][k], *factors[-1]),
                [pltpu.VMEM((width, part), F32)],
            )
    whole = jax.ShapeDtypeStruct((height, columns), F32)
    sems = pltpu.SemaphoreType.DMA((CHUNKS,))
    (out,) = call(lower_store, "lower_store", rests, [whole], [sems], hbm_out=(0,))
    (out,) = call(
        last_apply,
        "finish",
        (made[-1][-1], sent[-1][-1], *factors[-1], *done, out),
        [whole],
        [pltpu.VMEM((width, part), F32), sems],
        hbm_in=(3 + CHUNKS,),
        hbm_out=(0,),
        alias={3 + CHUNKS: 0},
    )
    return out


def solution(mesh):
    return jax.shard_map(
        per_device,
        mesh=mesh,
        in_specs=(
            P("row", "col"),
            P(("row", "col"), None),
            P(("row", "col"), None),
            P(("row", "col"), None),
            P(("row", "col"), None),
        ),
        out_specs=P("row", "col"),
        check_vma=False,
    )
```

time: 222 us -> 97.5 us (0.44)
  waiting for transfers between devices: 102 us -> 36.7 us
  blocking collectives: 61.3 us -> 0 us
  matrix products: 44.7 us -> 0 us
  starting transfers between devices: 7.2 us -> 34.4 us
  Pallas kernels: 0 us -> 25.6 us
  local copies, waits for them, and re-layouts: 3.51 us -> 0 us
  other arithmetic: 2.51 us -> 0 us
    ppermute x9 -> x31, waiting for transfers between devices: 102 us -> 36.7 us  [the longest x29 30.5 us: swap(): lax.ppermute(value, axis, [(i, i ^ mask) for i in range(lax.axis_size(axi...]
    all_gather x4 -> x0, blocking collectives: 61.3 us -> none  [the longest x1 17.6 us: per_device(): lax.all_gather(leaf_v, 'col', axis=0, tiled=True)]
    dot_general x12 -> x0, matrix products: 44.7 us -> none  [product(): jnp.dot(left, right, precision=lax.Precision.HIGHEST, preferred_element_t...]
    ppermute x9 -> x31, starting transfers between devices: 7.2 us -> 34.4 us  [the longest x29 32.5 us: swap(): lax.ppermute(value, axis, [(i, i ^ mask) for i in range(lax.axis_size(axi...]
    pallas_call x0 -> x42, Pallas kernels: none -> 25.6 us  [call(): pl.pallas_call(body, out_shape=[jax.ShapeDtypeStruct(o.shape, o.dtype) if...]
    concatenate x1 -> x0, other arithmetic: 2.51 us -> none  [per_device(): return jnp.concatenate([top, rest], axis=0)]
    slice x1 -> x0, local copies, waits for them, and re-layouts: 2.51 us -> none  [per_device(): top = changed[:width]]
  transfers between devices with their start and end apart: 9 -> 31, of which waited for: 3 -> 12; matrix products, arithmetic and copies ran while one was open for 6% -> 0% of each run, Pallas kernels for 0% -> 24%
where the time goes in v2:
time: 97.5 us; the launch traced here: 97.4 us
  waiting for transfers between devices  36.7 us (38%)
  starting transfers between devices  34.4 us (35%)
  Pallas kernels  25.6 us (26%)
    ppermute x29, starting transfers between devices, swap(): lax.ppermute(value, axis, [(i, i ^ mask) for i in range(lax.axis_size(axi...  32.5 us
    ppermute x29, waiting for transfers between devices, swap(): lax.ppermute(value, axis, [(i, i ^ mask) for i in range(lax.axis_size(axi...  30.5 us
    pallas_call x42, Pallas kernels, call(): pl.pallas_call(body, out_shape=[jax.ShapeDtypeStruct(o.shape, o.dtype) if...  25.6 us
    ppermute x1, waiting for transfers between devices, spread(): ends = lax.ppermute(second, axis, [(1, 0), (2, 3)])  6.21 us
  transfers between devices with their start and end apart: 31, of which 12 were waited for; matrix products, arithmetic and copies ran while one was open for 0% of the time, Pallas kernels for 24%

profile of v2, /device:TPU:0, one launch (start us, length us, event | category | flops | bytes accessed | tf_op | source)
XLA Modules:
  0.0 97.4 jit_solution(17074832906350016916)
XLA Ops:
  1.0 4.1 %collective-permute-start = (f32[320,256]{1,0:T(8,128)S(1)}, f32[320,256]{1,0:T(8,128)S(1)}, u32[]{:S(2)}, u32[]{:S(2)}) collective-permute-start(f32[320,256]{1,0:T(8,128)S(1)} %pack.1.refs_0_), channel_id=1, source_target_pairs={{0,2},{1,3},{2,0},{3,1},{4,6},{5,7},{6,4},{7,5},{8,10},{9,11},{10,... | collective-permute-start | bytes 983048 | tf_op jit(solution)/shard_map/ppermute | solution.py:39
  5.1 1.6 %collective-permute-start.1 = (f32[320,256]{1,0:T(8,128)S(1)}, f32[320,256]{1,0:T(8,128)S(1)}, u32[]{:S(2)}, u32[]{:S(2)}) collective-permute-start(f32[320,256]{1,0:T(8,128)S(1)} %pack.1.refs_0_), channel_id=1, source_target_pairs={{0,1},{1,0},{2,3},{3,2},{4,5},{5,4},{6,7},{7,6},{8,9},{9,8},{10,11... | collective-permute-start | bytes 983048 | tf_op jit(solution)/shard_map/ppermute | solution.py:39
  7.4 13.4 %collective-permute-done.refs_1_.refs_2_ = f32[320,256]{1,0:T(8,128)S(1)} collective-permute-done((f32[320,256]{1,0:T(8,128)S(1)}, f32[320,256]{1,0:T(8,128)S(1)}, u32[]{:S(2)}, u32[]{:S(2)}) %collective-permute-start) | collective-permute-done | bytes 327712 | tf_op jit(solution)/shard_map/ppermute | solution.py:39
  22.0 2.4 %load.1 = (f32[512,2048]{1,0:T(8,128)S(1)}, bf16[512,2048]{1,0:T(8,128)(2,1)S(1)}, bf16[512,2048]{1,0:T(8,128)(2,1)S(1)}) custom-call(f32[512,2048]{1,0:T(8,128)} %refs_0_.3, f32[320,256]{1,0:T(8,128)S(1)} %collective-permute-done.refs_1_.refs_2_), custom_call_target="tpu_custom_call" | custom-call | flops 1000 | bytes 1000 | tf_op jit(solution)/shard_map/load/pallas_call | solution.py:25
  24.5 6.2 %collective-permute-done.3.refs_4_ = f32[320,256]{1,0:T(8,128)S(1)} collective-permute-done((f32[320,256]{1,0:T(8,128)S(1)}, f32[320,256]{1,0:T(8,128)S(1)}, u32[]{:S(2)}, u32[]{:S(2)}) %collective-permute-start.3) | collective-permute-done | bytes 327712 | tf_op jit(solution)/shard_map/ppermute | solution.py:49
  39.3 2.5 %collective-permute-done.6.refs_1_ = f32[256,256]{1,0:T(8,128)S(1)} collective-permute-done((f32[256,256]{1,0:T(8,128)S(1)}, f32[256,256]{1,0:T(8,128)S(1)}, u32[]{:S(2)}, u32[]{:S(2)}) %collective-permute-start.6) | collective-permute-done | bytes 262176 | tf_op jit(solution)/shard_map/ppermute | solution.py:39
  42.6 1.6 %collective-permute-start.8 = (f32[256,256]{1,0:T(8,128)S(1)}, f32[256,256]{1,0:T(8,128)S(1)}, u32[]{:S(2)}, u32[]{:S(2)}) collective-permute-start(f32[256,256]{1,0:T(8,128)S(1)} %level0.8.refs_7_.refs_0_.refs_4_), channel_id=1, source_target_pairs={{0,8},{4,12},{8,0},{12,4},{16,24},{20,28},{24,16},{28,20},{1,9},{5... | collective-permute-start | bytes 786440 | tf_op jit(solution)/shard_map/ppermute | solution.py:39
  45.4 2.1 %collective-permute-done.20.refs_1_ = f32[256,256]{1,0:T(8,128)S(1)} collective-permute-done((f32[256,256]{1,0:T(8,128)S(1)}, f32[256,256]{1,0:T(8,128)S(1)}, u32[]{:S(2)}, u32[]{:S(2)}) %collective-permute-start.20) | collective-permute-done | bytes 262176 | tf_op jit(solution)/shard_map/ppermute | solution.py:39
  47.8 1.3 %collective-permute-start.21 = (f32[256,256]{1,0:T(8,128)S(1)}, f32[256,256]{1,0:T(8,128)S(1)}, u32[]{:S(2)}, u32[]{:S(2)}) collective-permute-start(f32[256,256]{1,0:T(8,128)S(1)} %level1.12.refs_0_.refs_4_), channel_id=1, source_target_pairs={{0,16},{4,20},{8,24},{12,28},{16,0},{20,4},{24,8},{28,12},{1,17},{... | collective-permute-start | bytes 786440 | tf_op jit(solution)/shard_map/ppermute | solution.py:39
  49.6 1.6 %collective-permute-start.23 = (f32[256,256]{1,0:T(8,128)S(1)}, f32[256,256]{1,0:T(8,128)S(1)}, u32[]{:S(2)}, u32[]{:S(2)}) collective-permute-start(f32[256,256]{1,0:T(8,128)S(1)} %level0.13.refs_0_.refs_7_), channel_id=1, source_target_pairs={{0,8},{4,12},{8,0},{12,4},{16,24},{20,28},{24,16},{28,20},{1,9},{5... | collective-permute-start | bytes 786440 | tf_op jit(solution)/shard_map/ppermute | solution.py:39
  53.5 1.3 %collective-permute-start.12 = (f32[256,256]{1,0:T(8,128)S(1)}, f32[256,256]{1,0:T(8,128)S(1)}, u32[]{:S(2)}, u32[]{:S(2)}) collective-permute-start(f32[256,256]{1,0:T(8,128)S(1)} %level1.8.refs_4_.refs_0_), channel_id=1, source_target_pairs={{0,16},{4,20},{8,24},{12,28},{16,0},{20,4},{24,8},{28,12},{1,17},{... | collective-permute-start | bytes 786440 | tf_op jit(solution)/shard_map/ppermute | solution.py:39
  55.2 1.6 %collective-permute-start.11 = (f32[256,256]{1,0:T(8,128)S(1)}, f32[256,256]{1,0:T(8,128)S(1)}, u32[]{:S(2)}, u32[]{:S(2)}) collective-permute-start(f32[256,256]{1,0:T(8,128)S(1)} %level0.9.refs_7_.refs_0_), channel_id=1, source_target_pairs={{0,8},{4,12},{8,0},{12,4},{16,24},{20,28},{24,16},{28,20},{1,9},{5... | collective-permute-start | bytes 786440 | tf_op jit(solution)/shard_map/ppermute | solution.py:39
  61.4 2.0 %collective-permute-start.26 = (f32[256,256]{1,0:T(8,128)S(1)}, f32[256,256]{1,0:T(8,128)S(1)}, u32[]{:S(2)}, u32[]{:S(2)}) collective-permute-start(f32[256,256]{1,0:T(8,128)S(1)} %level0.14.refs_0_.refs_7_), channel_id=1, source_target_pairs={{0,8},{4,12},{8,0},{12,4},{16,24},{20,28},{24,16},{28,20},{1,9},{5... | collective-permute-start | bytes 786440 | tf_op jit(solution)/shard_map/ppermute | solution.py:39
  65.6 2.0 %collective-permute-start.14 = (f32[256,256]{1,0:T(8,128)S(1)}, f32[256,256]{1,0:T(8,128)S(1)}, u32[]{:S(2)}, u32[]{:S(2)}) collective-permute-start(f32[256,256]{1,0:T(8,128)S(1)} %level0.10.refs_7_.refs_0_), channel_id=1, source_target_pairs={{0,8},{4,12},{8,0},{12,4},{16,24},{20,28},{24,16},{28,20},{1,9},{5... | collective-permute-start | bytes 786440 | tf_op jit(solution)/shard_map/ppermute | solution.py:39
  69.1 1.3 %collective-permute-done.26.refs_1_ = f32[256,256]{1,0:T(8,128)S(1)} collective-permute-done((f32[256,256]{1,0:T(8,128)S(1)}, f32[256,256]{1,0:T(8,128)S(1)}, u32[]{:S(2)}, u32[]{:S(2)}) %collective-permute-start.26) | collective-permute-done | bytes 262176 | tf_op jit(solution)/shard_map/ppermute | solution.py:39
  72.4 1.7 %collective-permute-start.29 = (f32[256,256]{1,0:T(8,128)S(1)}, f32[256,256]{1,0:T(8,128)S(1)}, u32[]{:S(2)}, u32[]{:S(2)}) collective-permute-start(f32[256,256]{1,0:T(8,128)S(1)} %level0.15.refs_0_), channel_id=1, source_target_pairs={{0,8},{4,12},{8,0},{12,4},{16,24},{20,28},{24,16},{28,20},{1,9},{5... | collective-permute-start | bytes 786440 | tf_op jit(solution)/shard_map/ppermute | solution.py:39
  74.5 1.6 %collective-permute-done.14.refs_1_ = f32[256,256]{1,0:T(8,128)S(1)} collective-permute-done((f32[256,256]{1,0:T(8,128)S(1)}, f32[256,256]{1,0:T(8,128)S(1)}, u32[]{:S(2)}, u32[]{:S(2)}) %collective-permute-start.14) | collective-permute-done | bytes 262176 | tf_op jit(solution)/shard_map/ppermute | solution.py:39
  78.0 1.7 %collective-permute-start.16 = (f32[256,256]{1,0:T(8,128)S(1)}, f32[256,256]{1,0:T(8,128)S(1)}, u32[]{:S(2)}, u32[]{:S(2)}) collective-permute-start(f32[256,256]{1,0:T(8,128)S(1)} %level0.11.refs_0_), channel_id=1, source_target_pairs={{0,8},{4,12},{8,0},{12,4},{16,24},{20,28},{24,16},{28,20},{1,9},{5... | collective-permute-start | bytes 786440 | tf_op jit(solution)/shard_map/ppermute | solution.py:39
  83.2 2.5 %collective-permute-done.17.refs_1_ = f32[256,256]{1,0:T(8,128)S(1)} collective-permute-done((f32[256,256]{1,0:T(8,128)S(1)}, f32[256,256]{1,0:T(8,128)S(1)}, u32[]{:S(2)}, u32[]{:S(2)}) %collective-permute-start.17) | collective-permute-done | bytes 262176 | tf_op jit(solution)/shard_map/ppermute | solution.py:39
  86.6 1.6 %collective-permute-start.18 = (f32[256,256]{1,0:T(8,128)S(1)}, f32[256,256]{1,0:T(8,128)S(1)}, u32[]{:S(2)}, u32[]{:S(2)}) collective-permute-start(f32[256,256]{1,0:T(8,128)S(1)} %level1.11.refs_0_), channel_id=1, source_target_pairs={{0,16},{4,20},{8,24},{12,28},{16,0},{20,4},{24,8},{28,12},{1,17},{... | collective-permute-start | bytes 786440 | tf_op jit(solution)/shard_map/ppermute | solution.py:39
  88.7 1.4 %lower_store.1.refs_11_ = f32[512,2048]{1,0:T(8,128)} custom-call(f32[256,256]{1,0:T(8,128)S(1)} %rest_0.1.refs_0_, f32[256,256]{1,0:T(8,128)S(1)} %rest_1.1.refs_1_, f32[256,256]{1,0:T(8,128)S(1)} %get-tuple-element.67.refs_2_, f32[256,256]{1,0:T(8,128)S(1)} %get-tuple-element.68.refs_3_, f32[256,256]{1,0:T(8,128)S(1)} %get-tuple-element.69.refs_4_, ...), custom_call_target="tpu_custom_call" | custom-call | flops 1000 | bytes 1000 | tf_op jit(solution)/shard_map/lower_store/pallas_call | solution.py:25
  90.1 1.3 %collective-permute-done.30.refs_1_ = f32[256,256]{1,0:T(8,128)S(1)} collective-permute-done((f32[256,256]{1,0:T(8,128)S(1)}, f32[256,256]{1,0:T(8,128)S(1)}, u32[]{:S(2)}, u32[]{:S(2)}) %collective-permute-start.30) | collective-permute-done | bytes 262176 | tf_op jit(solution)/shard_map/ppermute | solution.py:39
  91.8 4.0 %collective-permute-done.18.refs_1_ = f32[256,256]{1,0:T(8,128)S(1)} collective-permute-done((f32[256,256]{1,0:T(8,128)S(1)}, f32[256,256]{1,0:T(8,128)S(1)}, u32[]{:S(2)}, u32[]{:S(2)}) %collective-permute-start.18) | collective-permute-done | bytes 262176 | tf_op jit(solution)/shard_map/ppermute | solution.py:39
  95.7 1.5 %finish.1 = f32[512,2048]{1,0:T(8,128)} custom-call(f32[256,256]{1,0:T(8,128)S(1)} %level1.11.refs_0_, f32[256,256]{1,0:T(8,128)S(1)} %collective-permute-done.18.refs_1_, bf16[256,512]{1,0:T(8,128)(2,1)S(1)} %get-tuple-element.56.refs_4_.refs_2_, bf16[256,512]{1,0:T(8,128)(2,1)S(1)} %get-tuple-element.58.refs_3_, ...), custom_call_target="tpu_custom_call", output_to_operand_aliasing={{}: (11, {})} | custom-call | flops 1000 | bytes 1000 | tf_op jit(solution)/shard_map/finish/pallas_call | solution.py:25
  (80 shorter events, 34.6 us)
Async XLA Ops:
  1.0 19.7 %collective-permute-start = (f32[320,256]{1,0:T(8,128)S(1)}, f32[320,256]{1,0:T(8,128)S(1)}, u32[]{:S(2)}, u32[]{:S(2)}) collective-permute-start(f32[320,256]{1,0:T(8,128)S(1)} %pack.1.refs_0_), channel_id=1, source_target_pairs={{0,2},{1,3},{2,0},{3,1},{4,6},{5,7},{6,4},{7,5},{8,10},{9,11},{10,... | collective-permute-start | bytes 983048 | tf_op jit(solution)/shard_map/ppermute | solution.py:39
  5.1 19.3 %collective-permute-start.1 = (f32[320,256]{1,0:T(8,128)S(1)}, f32[320,256]{1,0:T(8,128)S(1)}, u32[]{:S(2)}, u32[]{:S(2)}) collective-permute-start(f32[320,256]{1,0:T(8,128)S(1)} %pack.1.refs_0_), channel_id=1, source_target_pairs={{0,1},{1,0},{2,3},{3,2},{4,5},{5,4},{6,7},{7,6},{8,9},{9,8},{10,11... | collective-permute-start | bytes 983048 | tf_op jit(solution)/shard_map/ppermute | solution.py:39
  6.7 17.8 %collective-permute-start.2 = (f32[320,256]{1,0:T(8,128)S(1)}, f32[320,256]{1,0:T(8,128)S(1)}, u32[]{:S(2)}, u32[]{:S(2)}) collective-permute-start(f32[320,256]{1,0:T(8,128)S(1)} %pack.1.refs_0_), channel_id=1, source_target_pairs={{1,2},{2,1},{5,6},{6,5},{9,10},{10,9},{13,14},{14,13},{17,18},{18,... | collective-permute-start | bytes 983048 | tf_op jit(solution)/shard_map/ppermute | solution.py:48
  20.7 10.0 %collective-permute-start.3 = (f32[320,256]{1,0:T(8,128)S(1)}, f32[320,256]{1,0:T(8,128)S(1)}, u32[]{:S(2)}, u32[]{:S(2)}) collective-permute-start(f32[320,256]{1,0:T(8,128)S(1)} %collective-permute-done.refs_1_.refs_2_), channel_id=1, source_target_pairs={{1,0},{2,3},{5,4},{6,7},{9,8},{10,11},{13,12},{14,15},{17,16},{18,... | collective-permute-start | bytes 983048 | tf_op jit(solution)/shard_map/ppermute | solution.py:49
  32.7 9.2 %collective-permute-start.6 = (f32[256,256]{1,0:T(8,128)S(1)}, f32[256,256]{1,0:T(8,128)S(1)}, u32[]{:S(2)}, u32[]{:S(2)}) collective-permute-start(f32[256,256]{1,0:T(8,128)S(1)} %get-tuple-element.51.refs_0_), channel_id=1, source_target_pairs={{0,8},{4,12},{8,0},{12,4},{16,24},{20,28},{24,16},{28,20},{1,9},{5... | collective-permute-start | bytes 786440 | tf_op jit(solution)/shard_map/ppermute | solution.py:39
  35.6 11.9 %collective-permute-start.20 = (f32[256,256]{1,0:T(8,128)S(1)}, f32[256,256]{1,0:T(8,128)S(1)}, u32[]{:S(2)}, u32[]{:S(2)}) collective-permute-start(f32[256,256]{1,0:T(8,128)S(1)} %level0.12.refs_0_.refs_7_), channel_id=1, source_target_pairs={{0,8},{4,12},{8,0},{12,4},{16,24},{20,28},{24,16},{28,20},{1,9},{5... | collective-permute-start | bytes 786440 | tf_op jit(solution)/shard_map/ppermute | solution.py:39
  37.5 11.7 %collective-permute-start.22 = (f32[256,256]{1,0:T(8,128)S(1)}, f32[256,256]{1,0:T(8,128)S(1)}, u32[]{:S(2)}, u32[]{:S(2)}) collective-permute-start(f32[256,256]{1,0:T(8,128)S(1)} %get-tuple-element.60.refs_0_), channel_id=1, source_target_pairs={{0,4},{4,0},{8,12},{12,8},{16,20},{20,16},{24,28},{28,24},{1,5},{5... | collective-permute-start | bytes 786440 | tf_op jit(solution)/shard_map/ppermute | solution.py:39
  38.0 13.1 %collective-permute-start.9 = (f32[256,256]{1,0:T(8,128)S(1)}, f32[256,256]{1,0:T(8,128)S(1)}, u32[]{:S(2)}, u32[]{:S(2)}) collective-permute-start(f32[256,256]{1,0:T(8,128)S(1)} %get-tuple-element.55.refs_0_), channel_id=1, source_target_pairs={{0,16},{4,20},{8,24},{12,28},{16,0},{20,4},{24,8},{28,12},{1,17},{... | collective-permute-start | bytes 786440 | tf_op jit(solution)/shard_map/ppermute | solution.py:39
  42.6 10.5 %collective-permute-start.8 = (f32[256,256]{1,0:T(8,128)S(1)}, f32[256,256]{1,0:T(8,128)S(1)}, u32[]{:S(2)}, u32[]{:S(2)}) collective-permute-start(f32[256,256]{1,0:T(8,128)S(1)} %level0.8.refs_7_.refs_0_.refs_4_), channel_id=1, source_target_pairs={{0,8},{4,12},{8,0},{12,4},{16,24},{20,28},{24,16},{28,20},{1,9},{5... | collective-permute-start | bytes 786440 | tf_op jit(solution)/shard_map/ppermute | solution.py:39
  45.3 9.5 %collective-permute-start.7 = (f32[256,256]{1,0:T(8,128)S(1)}, f32[256,256]{1,0:T(8,128)S(1)}, u32[]{:S(2)}, u32[]{:S(2)}) collective-permute-start(f32[256,256]{1,0:T(8,128)S(1)} %get-tuple-element.53.refs_0_), channel_id=1, source_target_pairs={{0,4},{4,0},{8,12},{12,8},{16,20},{20,16},{24,28},{28,24},{1,5},{5... | collective-permute-start | bytes 786440 | tf_op jit(solution)/shard_map/ppermute | solution.py:39
  47.8 10.0 %collective-permute-start.21 = (f32[256,256]{1,0:T(8,128)S(1)}, f32[256,256]{1,0:T(8,128)S(1)}, u32[]{:S(2)}, u32[]{:S(2)}) collective-permute-start(f32[256,256]{1,0:T(8,128)S(1)} %level1.12.refs_0_.refs_4_), channel_id=1, source_target_pairs={{0,16},{4,20},{8,24},{12,28},{16,0},{20,4},{24,8},{28,12},{1,17},{... | collective-permute-start | bytes 786440 | tf_op jit(solution)/shard_map/ppermute | solution.py:39
  49.6 8.7 %collective-permute-start.23 = (f32[256,256]{1,0:T(8,128)S(1)}, f32[256,256]{1,0:T(8,128)S(1)}, u32[]{:S(2)}, u32[]{:S(2)}) collective-permute-start(f32[256,256]{1,0:T(8,128)S(1)} %level0.13.refs_0_.refs_7_), channel_id=1, source_target_pairs={{0,8},{4,12},{8,0},{12,4},{16,24},{20,28},{24,16},{28,20},{1,9},{5... | collective-permute-start | bytes 786440 | tf_op jit(solution)/shard_map/ppermute | solution.py:39
  53.5 10.0 %collective-permute-start.12 = (f32[256,256]{1,0:T(8,128)S(1)}, f32[256,256]{1,0:T(8,128)S(1)}, u32[]{:S(2)}, u32[]{:S(2)}) collective-permute-start(f32[256,256]{1,0:T(8,128)S(1)} %level1.8.refs_4_.refs_0_), channel_id=1, source_target_pairs={{0,16},{4,20},{8,24},{12,28},{16,0},{20,4},{24,8},{28,12},{1,17},{... | collective-permute-start | bytes 786440 | tf_op jit(solution)/shard_map/ppermute | solution.py:39
  55.2 8.7 %collective-permute-start.11 = (f32[256,256]{1,0:T(8,128)S(1)}, f32[256,256]{1,0:T(8,128)S(1)}, u32[]{:S(2)}, u32[]{:S(2)}) collective-permute-start(f32[256,256]{1,0:T(8,128)S(1)} %level0.9.refs_7_.refs_0_), channel_id=1, source_target_pairs={{0,8},{4,12},{8,0},{12,4},{16,24},{20,28},{24,16},{28,20},{1,9},{5... | collective-permute-start | bytes 786440 | tf_op jit(solution)/shard_map/ppermute | solution.py:39
  58.7 9.9 %collective-permute-start.24 = (f32[256,256]{1,0:T(8,128)S(1)}, f32[256,256]{1,0:T(8,128)S(1)}, u32[]{:S(2)}, u32[]{:S(2)}) collective-permute-start(f32[256,256]{1,0:T(8,128)S(1)} %level1.13.refs_0_.refs_4_), channel_id=1, source_target_pairs={{0,16},{4,20},{8,24},{12,28},{16,0},{20,4},{24,8},{28,12},{1,17},{... | collective-permute-start | bytes 786440 | tf_op jit(solution)/shard_map/ppermute | solution.py:39
  61.4 9.0 %collective-permute-start.26 = (f32[256,256]{1,0:T(8,128)S(1)}, f32[256,256]{1,0:T(8,128)S(1)}, u32[]{:S(2)}, u32[]{:S(2)}) collective-permute-start(f32[256,256]{1,0:T(8,128)S(1)} %level0.14.refs_0_.refs_7_), channel_id=1, source_target_pairs={{0,8},{4,12},{8,0},{12,4},{16,24},{20,28},{24,16},{28,20},{1,9},{5... | collective-permute-start | bytes 786440 | tf_op jit(solution)/shard_map/ppermute | solution.py:39
  64.3 9.8 %collective-permute-start.15 = (f32[256,256]{1,0:T(8,128)S(1)}, f32[256,256]{1,0:T(8,128)S(1)}, u32[]{:S(2)}, u32[]{:S(2)}) collective-permute-start(f32[256,256]{1,0:T(8,128)S(1)} %level1.9.refs_4_.refs_0_), channel_id=1, source_target_pairs={{0,16},{4,20},{8,24},{12,28},{16,0},{20,4},{24,8},{28,12},{1,17},{... | collective-permute-start | bytes 786440 | tf_op jit(solution)/shard_map/ppermute | solution.py:39
  65.6 10.5 %collective-permute-start.14 = (f32[256,256]{1,0:T(8,128)S(1)}, f32[256,256]{1,0:T(8,128)S(1)}, u32[]{:S(2)}, u32[]{:S(2)}) collective-permute-start(f32[256,256]{1,0:T(8,128)S(1)} %level0.10.refs_7_.refs_0_), channel_id=1, source_target_pairs={{0,8},{4,12},{8,0},{12,4},{16,24},{20,28},{24,16},{28,20},{1,9},{5... | collective-permute-start | bytes 786440 | tf_op jit(solution)/shard_map/ppermute | solution.py:39
  68.6 9.0 %collective-permute-start.13 = (f32[256,256]{1,0:T(8,128)S(1)}, f32[256,256]{1,0:T(8,128)S(1)}, u32[]{:S(2)}, u32[]{:S(2)}) collective-permute-start(f32[256,256]{1,0:T(8,128)S(1)} %get-tuple-element.59.refs_0_), channel_id=1, source_target_pairs={{0,4},{4,0},{8,12},{12,8},{16,20},{20,16},{24,28},{28,24},{1,5},{5... | collective-permute-start | bytes 786440 | tf_op jit(solution)/shard_map/ppermute | solution.py:39
  70.8 9.3 %collective-permute-start.27 = (f32[256,256]{1,0:T(8,128)S(1)}, f32[256,256]{1,0:T(8,128)S(1)}, u32[]{:S(2)}, u32[]{:S(2)}) collective-permute-start(f32[256,256]{1,0:T(8,128)S(1)} %level1.14.refs_0_.refs_4_), channel_id=1, source_target_pairs={{0,16},{4,20},{8,24},{12,28},{16,0},{20,4},{24,8},{28,12},{1,17},{... | collective-permute-start | bytes 786440 | tf_op jit(solution)/shard_map/ppermute | solution.py:39
  72.4 9.3 %collective-permute-start.29 = (f32[256,256]{1,0:T(8,128)S(1)}, f32[256,256]{1,0:T(8,128)S(1)}, u32[]{:S(2)}, u32[]{:S(2)}) collective-permute-start(f32[256,256]{1,0:T(8,128)S(1)} %level0.15.refs_0_), channel_id=1, source_target_pairs={{0,8},{4,12},{8,0},{12,4},{16,24},{20,28},{24,16},{28,20},{1,9},{5... | collective-permute-start | bytes 786440 | tf_op jit(solution)/shard_map/ppermute | solution.py:39
  76.4 9.3 %collective-permute-start.17 = (f32[256,256]{1,0:T(8,128)S(1)}, f32[256,256]{1,0:T(8,128)S(1)}, u32[]{:S(2)}, u32[]{:S(2)}) collective-permute-start(f32[256,256]{1,0:T(8,128)S(1)} %level1.10.refs_4_.refs_0_), channel_id=1, source_target_pairs={{0,16},{4,20},{8,24},{12,28},{16,0},{20,4},{24,8},{28,12},{1,17},{... | collective-permute-start | bytes 786440 | tf_op jit(solution)/shard_map/ppermute | solution.py:39
  82.1 9.3 %collective-permute-start.30 = (f32[256,256]{1,0:T(8,128)S(1)}, f32[256,256]{1,0:T(8,128)S(1)}, u32[]{:S(2)}, u32[]{:S(2)}) collective-permute-start(f32[256,256]{1,0:T(8,128)S(1)} %level1.15.refs_0_), channel_id=1, source_target_pairs={{0,16},{4,20},{8,24},{12,28},{16,0},{20,4},{24,8},{28,12},{1,17},{... | collective-permute-start | bytes 786440 | tf_op jit(solution)/shard_map/ppermute | solution.py:39
  86.6 9.2 %collective-permute-start.18 = (f32[256,256]{1,0:T(8,128)S(1)}, f32[256,256]{1,0:T(8,128)S(1)}, u32[]{:S(2)}, u32[]{:S(2)}) collective-permute-start(f32[256,256]{1,0:T(8,128)S(1)} %level1.11.refs_0_), channel_id=1, source_target_pairs={{0,16},{4,20},{8,24},{12,28},{16,0},{20,4},{24,8},{28,12},{1,17},{... | collective-permute-start | bytes 786440 | tf_op jit(solution)/shard_map/ppermute | solution.py:39
  (7 other events, 45.7 us)

commit v3 on v2

--- a/solution.py
+++ b/solution.py
@@ -39,15 +39,15 @@
     return lax.ppermute(value, axis, [(i, i ^ mask) for i in range(lax.axis_size(axis))])
 
 
-def spread(piece, axis):
+def spread(whole, halves, axis):
     n = lax.axis_size(axis)
     if n != 4:
-        return [piece] + [swap(piece, axis, k) for k in range(1, n)]
-    second = swap(piece, axis, 2)
-    first = swap(piece, axis, 1)
-    middle = lax.ppermute(piece, axis, [(1, 2), (2, 1)])
-    ends = lax.ppermute(second, axis, [(1, 0), (2, 3)])
-    return [piece, first, second, middle, ends]
+        return [whole] + [swap(whole, axis, k) for k in range(1, n)]
+    seconds = [swap(half, axis, 2) for half in halves]
+    first = swap(whole, axis, 1)
+    middle = lax.ppermute(whole, axis, [(1, 2), (2, 1)])
+    ends = [lax.ppermute(second, axis, [(1, 0), (2, 3)]) for second in seconds]
+    return [whole, first, middle, *seconds, *ends]
 
 
 def split(x):
@@ -68,28 +68,37 @@
     return (lax.axis_index("row") >> level) & 1
 
 
-def place(pieces, offset, rows, out):
+def place(pieces, start, rows, out):
     mine = lax.axis_index("col")
-
-    def put(k, piece):
+    span = pl.ds(start, rows)
+
+    def put(k, *parts):
         to = pl.ds(pl.multiple_of((mine ^ k) * rows, rows), rows)
-        out[to, :] = piece[pl.ds(offset, rows), :]
-
-    whole = pieces if out.shape[0] == rows * len(pieces) else pieces[:-2]
-    for k, piece in enumerate(whole):
-        put(k, piece)
-    if len(whole) < len(pieces):
-        inner = (mine == 1) | (mine == 2)
-        pl.when(inner)(lambda: put(3, pieces[-2]))
-        pl.when(jnp.logical_not(inner))(lambda: put(3, pieces[-1]))
+        size = out.shape[1] // len(parts)
+        for i, part in enumerate(parts):
+            out[to, pl.ds(i * size, size)] = part[span, :]
+
+    if out.shape[0] == rows * len(pieces):
+        for k, piece in enumerate(pieces):
+            put(k, piece)
+        return
+    put(0, pieces[0])
+    put(1, pieces[1])
+    put(2, *pieces[3:5])
+    inner = (mine == 1) | (mine == 2)
+    pl.when(inner)(lambda: put(3, pieces[2]))
+    pl.when(jnp.logical_not(inner))(lambda: put(3, *pieces[5:7]))
 
 
 def pack(*refs):
-    *sources, out, sems = refs
+    *sources, whole, left, right, sems = refs
+    size = left.shape[1]
     copies, start = [], 0
-    for k, source in enumerate(sources):
-        copies.append(pltpu.make_async_copy(source, out.at[pl.ds(start, source.shape[0])], sems.at[k]))
-        copies[-1].start()
+    for source in sources:
+        to = pl.ds(start, source.shape[0])
+        for half, target in ((pl.ds(0, 2 * size), whole), (pl.ds(0, size), left), (pl.ds(size, size), right)):
+            copies.append(pltpu.make_async_copy(source.at[:, half], target.at[to], sems.at[len(copies)]))
+            copies[-1].start()
         start += source.shape[0]
     for c in copies:
         c.wait()
@@ -206,15 +215,16 @@
     steps = columns // STEP
     block, block16 = pltpu.VMEM((width, width), F32), lambda *shape: pltpu.VMEM(shape, BF16)
 
-    (packed,) = call(
+    rows = vr + 3 * tr
+    whole, *halves = call(
         pack,
         "pack",
         (leaf_v, leaf_t, tree_t, tree_y),
-        [pltpu.VMEM((vr + 3 * tr, width), F32)],
-        [pltpu.SemaphoreType.DMA((4,))],
+        [pltpu.VMEM((rows, width), F32)] + [pltpu.VMEM((rows, width // 2), F32)] * 2,
+        [pltpu.SemaphoreType.DMA((12,))],
         hbm_in=range(4),
     )
-    pieces = spread(packed, "col")
+    pieces = spread(whole, halves, "col")
     c, ch, cl = call(
         load,
         "load",
@@ -222,7 +232,7 @@
         [pltpu.VMEM((height, columns), F32)] + [block16(height, columns)] * 2,
         [pltpu.VMEM((steps, height, STEP), F32), pltpu.SemaphoreType.DMA((steps,))],
         hbm_in=(0,),
-        after=pieces[2:3],
+        after=pieces[3:5],
     )
     owns = call(functools.partial(tree_blocks, len(pieces), vr + tr, tr), "tree_blocks", pieces, [block] * depth, after=[ch])
     factors = [
@@ -268,7 +278,7 @@
 
     done, rests, tops, fars = [], [], [], []
 
-    def leaf(k):
+    def make_leaf(k):
         above, below = pltpu.VMEM((width, part), F32), pltpu.VMEM((height - width, part), F32)
         top, *others = call(
             functools.partial(leaf_apply, k * part),
@@ -289,17 +299,17 @@
         waits = made[min(1, depth - 2)][k - 2:k - 1] if k >= 2 else [factors[1][0]] * k
         advance(0, tops[k], fars[k], 0, waits)
 
-    leaf(0)
-    leaf(1)
+    make_leaf(0)
+    make_leaf(1)
     first_level(0)
     first_level(1)
-    leaf(2)
+    make_leaf(2)
     for k in range(CHUNKS):
         later(k)
         if k + 2 < CHUNKS:
             first_level(k + 2)
         if k + 3 < CHUNKS:
-            leaf(k + 3)
+            make_leaf(k + 3)
         if k < CHUNKS - 1:
             done += call(
                 functools.partial(level_apply, 0),

time: 97.5 us -> 95.7 us (0.982)
  waiting for transfers between devices: 36.7 us -> 29 us
  starting transfers between devices: 34.4 us -> 40 us
    ppermute x29 -> x30, waiting for transfers between devices: 30.5 us -> 25.5 us  [swap(): lax.ppermute(value, axis, [(i, i ^ mask) for i in range(lax.axis_size(axi...]
    ppermute x29 -> x30, starting transfers between devices: 32.5 us -> 36.8 us  [swap(): lax.ppermute(value, axis, [(i, i ^ mask) for i in range(lax.axis_size(axi...]
    ppermute x2 -> x3, waiting for transfers between devices: 6.21 us -> 3.53 us  [the longest x2 3.53 us: spread(): ends = [lax.ppermute(second, axis, [(1, 0), (2, 3)]) for second in seconds]]
    ppermute x2 -> x3, starting transfers between devices: 1.95 us -> 3.23 us  [the longest x2 2.56 us: spread(): ends = [lax.ppermute(second, axis, [(1, 0), (2, 3)]) for second in seconds]]
  transfers between devices with their start and end apart: 31 -> 33, of which waited for: 12 -> 13; matrix products, arithmetic and copies ran while one was open for 0% -> 0% of each run, Pallas kernels for 24% -> 24%
where the time goes in v3:
time: 95.7 us; the launch traced here: 95.5 us
  starting transfers between devices  40 us (42%)
  waiting for transfers between devices  29 us (30%)
  Pallas kernels  25.8 us (27%)
    ppermute x30, starting transfers between devices, swap(): lax.ppermute(value, axis, [(i, i ^ mask) for i in range(lax.axis_size(axi...  36.8 us
    pallas_call x42, Pallas kernels, call(): pl.pallas_call(body, out_shape=[jax.ShapeDtypeStruct(o.shape, o.dtype) if...  25.8 us
    ppermute x30, waiting for transfers between devices, swap(): lax.ppermute(value, axis, [(i, i ^ mask) for i in range(lax.axis_size(axi...  25.5 us
    ppermute x2, waiting for transfers between devices, spread(): ends = [lax.ppermute(second, axis, [(1, 0), (2, 3)]) for second in seconds]  3.53 us
    ppermute x2, starting transfers between devices, spread(): ends = [lax.ppermute(second, axis, [(1, 0), (2, 3)]) for second in seconds]  2.56 us
  transfers between devices with their start and end apart: 33, of which 13 were waited for; matrix products, arithmetic and copies ran while one was open for 0% of the time, Pallas kernels for 24%

profile of v3, /device:TPU:0, one launch (start us, length us, event | category | flops | bytes accessed | tf_op | source)
XLA Modules:
  0.0 95.5 jit_solution(2101806273816860636)
XLA Ops:
  1.2 4.1 %collective-permute-start = (f32[320,128]{1,0:T(8,128)S(1)}, f32[320,128]{1,0:T(8,128)S(1)}, u32[]{:S(2)}, u32[]{:S(2)}) collective-permute-start(f32[320,128]{1,0:T(8,128)S(1)} %get-tuple-element.42), channel_id=1, source_target_pairs={{0,2},{1,3},{2,0},{3,1},{4,6},{5,7},{6,4},{7,5},{8,10},{9,11},{10,... | collective-permute-start | bytes 491528 | tf_op jit(solution)/shard_map/ppermute | solution.py:39
  5.4 1.8 %collective-permute-start.2 = (f32[320,256]{1,0:T(8,128)S(1)}, f32[320,256]{1,0:T(8,128)S(1)}, u32[]{:S(2)}, u32[]{:S(2)}) collective-permute-start(f32[320,256]{1,0:T(8,128)S(1)} %get-tuple-element.47.refs_0_), channel_id=1, source_target_pairs={{0,1},{1,0},{2,3},{3,2},{4,5},{5,4},{6,7},{7,6},{8,9},{9,8},{10,11... | collective-permute-start | bytes 983048 | tf_op jit(solution)/shard_map/ppermute | solution.py:39
  7.9 9.6 %collective-permute-done.refs_1_.refs_3_ = f32[320,128]{1,0:T(8,128)S(1)} collective-permute-done((f32[320,128]{1,0:T(8,128)S(1)}, f32[320,128]{1,0:T(8,128)S(1)}, u32[]{:S(2)}, u32[]{:S(2)}) %collective-permute-start) | collective-permute-done | bytes 163872 | tf_op jit(solution)/shard_map/ppermute | solution.py:39
  18.7 2.2 %collective-permute-done.1.refs_2_.refs_4_ = f32[320,128]{1,0:T(8,128)S(1)} collective-permute-done((f32[320,128]{1,0:T(8,128)S(1)}, f32[320,128]{1,0:T(8,128)S(1)}, u32[]{:S(2)}, u32[]{:S(2)}) %collective-permute-start.1) | collective-permute-done | bytes 163872 | tf_op jit(solution)/shard_map/ppermute | solution.py:39
  22.2 2.4 %load.1 = (f32[512,2048]{1,0:T(8,128)S(1)}, bf16[512,2048]{1,0:T(8,128)(2,1)S(1)}, bf16[512,2048]{1,0:T(8,128)(2,1)S(1)}) custom-call(f32[512,2048]{1,0:T(8,128)} %refs_0_.3, f32[320,128]{1,0:T(8,128)S(1)} %collective-permute-done.refs_1_.refs_3_, f32[320,128]{1,0:T(8,128)S(1)} %collective-permute-done.1.refs_2_.refs_4_), custom_call_target="tpu_custom_call" | custom-call | flops 1000 | bytes 1000 | tf_op jit(solution)/shard_map/load/pallas_call | solution.py:25
  25.5 2.7 %collective-permute-done.5.refs_6_ = f32[320,128]{1,0:T(8,128)S(1)} collective-permute-done((f32[320,128]{1,0:T(8,128)S(1)}, f32[320,128]{1,0:T(8,128)S(1)}, u32[]{:S(2)}, u32[]{:S(2)}) %collective-permute-start.5) | collective-permute-done | bytes 163872 | tf_op jit(solution)/shard_map/ppermute | solution.py:49
  30.2 1.8 %collective-permute-start.8 = (f32[256,256]{1,0:T(8,128)S(1)}, f32[256,256]{1,0:T(8,128)S(1)}, u32[]{:S(2)}, u32[]{:S(2)}) collective-permute-start(f32[256,256]{1,0:T(8,128)S(1)} %get-tuple-element.57.refs_0_), channel_id=1, source_target_pairs={{0,8},{4,12},{8,0},{12,4},{16,24},{20,28},{24,16},{28,20},{1,9},{5... | collective-permute-start | bytes 786440 | tf_op jit(solution)/shard_map/ppermute | solution.py:39
  35.7 1.8 %collective-permute-start.11 = (f32[256,256]{1,0:T(8,128)S(1)}, f32[256,256]{1,0:T(8,128)S(1)}, u32[]{:S(2)}, u32[]{:S(2)}) collective-permute-start(f32[256,256]{1,0:T(8,128)S(1)} %get-tuple-element.61.refs_0_), channel_id=1, source_target_pairs={{0,16},{4,20},{8,24},{12,28},{16,0},{20,4},{24,8},{28,12},{1,17},{... | collective-permute-start | bytes 786440 | tf_op jit(solution)/shard_map/ppermute | solution.py:39
  37.4 1.9 %collective-permute-done.8.refs_1_ = f32[256,256]{1,0:T(8,128)S(1)} collective-permute-done((f32[256,256]{1,0:T(8,128)S(1)}, f32[256,256]{1,0:T(8,128)S(1)}, u32[]{:S(2)}, u32[]{:S(2)}) %collective-permute-start.8) | collective-permute-done | bytes 262176 | tf_op jit(solution)/shard_map/ppermute | solution.py:39
  40.1 2.2 %collective-permute-start.10 = (f32[256,256]{1,0:T(8,128)S(1)}, f32[256,256]{1,0:T(8,128)S(1)}, u32[]{:S(2)}, u32[]{:S(2)}) collective-permute-start(f32[256,256]{1,0:T(8,128)S(1)} %level0.8.refs_7_.refs_0_.refs_4_), channel_id=1, source_target_pairs={{0,8},{4,12},{8,0},{12,4},{16,24},{20,28},{24,16},{28,20},{1,9},{5... | collective-permute-start | bytes 786440 | tf_op jit(solution)/shard_map/ppermute | solution.py:39
  43.5 1.5 %collective-permute-done.22.refs_1_ = f32[256,256]{1,0:T(8,128)S(1)} collective-permute-done((f32[256,256]{1,0:T(8,128)S(1)}, f32[256,256]{1,0:T(8,128)S(1)}, u32[]{:S(2)}, u32[]{:S(2)}) %collective-permute-start.22) | collective-permute-done | bytes 262176 | tf_op jit(solution)/shard_map/ppermute | solution.py:39
  45.3 1.9 %collective-permute-start.23 = (f32[256,256]{1,0:T(8,128)S(1)}, f32[256,256]{1,0:T(8,128)S(1)}, u32[]{:S(2)}, u32[]{:S(2)}) collective-permute-start(f32[256,256]{1,0:T(8,128)S(1)} %level1.12.refs_0_.refs_4_), channel_id=1, source_target_pairs={{0,16},{4,20},{8,24},{12,28},{16,0},{20,4},{24,8},{28,12},{1,17},{... | collective-permute-start | bytes 786440 | tf_op jit(solution)/shard_map/ppermute | solution.py:39
  47.7 1.6 %collective-permute-start.25 = (f32[256,256]{1,0:T(8,128)S(1)}, f32[256,256]{1,0:T(8,128)S(1)}, u32[]{:S(2)}, u32[]{:S(2)}) collective-permute-start(f32[256,256]{1,0:T(8,128)S(1)} %level0.13.refs_0_.refs_7_), channel_id=1, source_target_pairs={{0,8},{4,12},{8,0},{12,4},{16,24},{20,28},{24,16},{28,20},{1,9},{5... | collective-permute-start | bytes 786440 | tf_op jit(solution)/shard_map/ppermute | solution.py:39
  51.4 1.5 %collective-permute-start.14 = (f32[256,256]{1,0:T(8,128)S(1)}, f32[256,256]{1,0:T(8,128)S(1)}, u32[]{:S(2)}, u32[]{:S(2)}) collective-permute-start(f32[256,256]{1,0:T(8,128)S(1)} %level1.8.refs_4_.refs_0_), channel_id=1, source_target_pairs={{0,16},{4,20},{8,24},{12,28},{16,0},{20,4},{24,8},{28,12},{1,17},{... | collective-permute-start | bytes 786440 | tf_op jit(solution)/shard_map/ppermute | solution.py:39
  53.3 1.6 %collective-permute-start.13 = (f32[256,256]{1,0:T(8,128)S(1)}, f32[256,256]{1,0:T(8,128)S(1)}, u32[]{:S(2)}, u32[]{:S(2)}) collective-permute-start(f32[256,256]{1,0:T(8,128)S(1)} %level0.9.refs_7_.refs_0_), channel_id=1, source_target_pairs={{0,8},{4,12},{8,0},{12,4},{16,24},{20,28},{24,16},{28,20},{1,9},{5... | collective-permute-start | bytes 786440 | tf_op jit(solution)/shard_map/ppermute | solution.py:39
  59.5 2.0 %collective-permute-start.28 = (f32[256,256]{1,0:T(8,128)S(1)}, f32[256,256]{1,0:T(8,128)S(1)}, u32[]{:S(2)}, u32[]{:S(2)}) collective-permute-start(f32[256,256]{1,0:T(8,128)S(1)} %level0.14.refs_0_.refs_7_), channel_id=1, source_target_pairs={{0,8},{4,12},{8,0},{12,4},{16,24},{20,28},{24,16},{28,20},{1,9},{5... | collective-permute-start | bytes 786440 | tf_op jit(solution)/shard_map/ppermute | solution.py:39
  63.8 1.8 %collective-permute-start.16 = (f32[256,256]{1,0:T(8,128)S(1)}, f32[256,256]{1,0:T(8,128)S(1)}, u32[]{:S(2)}, u32[]{:S(2)}) collective-permute-start(f32[256,256]{1,0:T(8,128)S(1)} %level0.10.refs_7_.refs_0_), channel_id=1, source_target_pairs={{0,8},{4,12},{8,0},{12,4},{16,24},{20,28},{24,16},{28,20},{1,9},{5... | collective-permute-start | bytes 786440 | tf_op jit(solution)/shard_map/ppermute | solution.py:39
  68.4 1.7 %collective-permute-start.29 = (f32[256,256]{1,0:T(8,128)S(1)}, f32[256,256]{1,0:T(8,128)S(1)}, u32[]{:S(2)}, u32[]{:S(2)}) collective-permute-start(f32[256,256]{1,0:T(8,128)S(1)} %level1.14.refs_0_.refs_4_), channel_id=1, source_target_pairs={{0,16},{4,20},{8,24},{12,28},{16,0},{20,4},{24,8},{28,12},{1,17},{... | collective-permute-start | bytes 786440 | tf_op jit(solution)/shard_map/ppermute | solution.py:39
  70.5 2.2 %collective-permute-start.31 = (f32[256,256]{1,0:T(8,128)S(1)}, f32[256,256]{1,0:T(8,128)S(1)}, u32[]{:S(2)}, u32[]{:S(2)}) collective-permute-start(f32[256,256]{1,0:T(8,128)S(1)} %level0.15.refs_0_), channel_id=1, source_target_pairs={{0,8},{4,12},{8,0},{12,4},{16,24},{20,28},{24,16},{28,20},{1,9},{5... | collective-permute-start | bytes 786440 | tf_op jit(solution)/shard_map/ppermute | solution.py:39
  74.0 1.7 %collective-permute-start.19 = (f32[256,256]{1,0:T(8,128)S(1)}, f32[256,256]{1,0:T(8,128)S(1)}, u32[]{:S(2)}, u32[]{:S(2)}) collective-permute-start(f32[256,256]{1,0:T(8,128)S(1)} %level1.10.refs_4_.refs_0_), channel_id=1, source_target_pairs={{0,16},{4,20},{8,24},{12,28},{16,0},{20,4},{24,8},{28,12},{1,17},{... | collective-permute-start | bytes 786440 | tf_op jit(solution)/shard_map/ppermute | solution.py:39
  76.1 2.2 %collective-permute-start.18 = (f32[256,256]{1,0:T(8,128)S(1)}, f32[256,256]{1,0:T(8,128)S(1)}, u32[]{:S(2)}, u32[]{:S(2)}) collective-permute-start(f32[256,256]{1,0:T(8,128)S(1)} %level0.11.refs_0_), channel_id=1, source_target_pairs={{0,8},{4,12},{8,0},{12,4},{16,24},{20,28},{24,16},{28,20},{1,9},{5... | collective-permute-start | bytes 786440 | tf_op jit(solution)/shard_map/ppermute | solution.py:39
  81.3 2.0 %collective-permute-done.19.refs_1_ = f32[256,256]{1,0:T(8,128)S(1)} collective-permute-done((f32[256,256]{1,0:T(8,128)S(1)}, f32[256,256]{1,0:T(8,128)S(1)}, u32[]{:S(2)}, u32[]{:S(2)}) %collective-permute-start.19) | collective-permute-done | bytes 262176 | tf_op jit(solution)/shard_map/ppermute | solution.py:39
  84.6 1.6 %collective-permute-start.20 = (f32[256,256]{1,0:T(8,128)S(1)}, f32[256,256]{1,0:T(8,128)S(1)}, u32[]{:S(2)}, u32[]{:S(2)}) collective-permute-start(f32[256,256]{1,0:T(8,128)S(1)} %level1.11.refs_0_), channel_id=1, source_target_pairs={{0,16},{4,20},{8,24},{12,28},{16,0},{20,4},{24,8},{28,12},{1,17},{... | collective-permute-start | bytes 786440 | tf_op jit(solution)/shard_map/ppermute | solution.py:39
  90.0 3.8 %collective-permute-done.20.refs_1_ = f32[256,256]{1,0:T(8,128)S(1)} collective-permute-done((f32[256,256]{1,0:T(8,128)S(1)}, f32[256,256]{1,0:T(8,128)S(1)}, u32[]{:S(2)}, u32[]{:S(2)}) %collective-permute-start.20) | collective-permute-done | bytes 262176 | tf_op jit(solution)/shard_map/ppermute | solution.py:39
  (84 shorter events, 37.3 us)
Async XLA Ops:
  1.2 16.3 %collective-permute-start = (f32[320,128]{1,0:T(8,128)S(1)}, f32[320,128]{1,0:T(8,128)S(1)}, u32[]{:S(2)}, u32[]{:S(2)}) collective-permute-start(f32[320,128]{1,0:T(8,128)S(1)} %get-tuple-element.42), channel_id=1, source_target_pairs={{0,2},{1,3},{2,0},{3,1},{4,6},{5,7},{6,4},{7,5},{8,10},{9,11},{10,... | collective-permute-start | bytes 491528 | tf_op jit(solution)/shard_map/ppermute | solution.py:39
  5.3 15.6 %collective-permute-start.1 = (f32[320,128]{1,0:T(8,128)S(1)}, f32[320,128]{1,0:T(8,128)S(1)}, u32[]{:S(2)}, u32[]{:S(2)}) collective-permute-start(f32[320,128]{1,0:T(8,128)S(1)} %get-tuple-element.43), channel_id=1, source_target_pairs={{0,2},{1,3},{2,0},{3,1},{4,6},{5,7},{6,4},{7,5},{8,10},{9,11},{10,... | collective-permute-start | bytes 491528 | tf_op jit(solution)/shard_map/ppermute | solution.py:39
  5.4 22.8 %collective-permute-start.2 = (f32[320,256]{1,0:T(8,128)S(1)}, f32[320,256]{1,0:T(8,128)S(1)}, u32[]{:S(2)}, u32[]{:S(2)}) collective-permute-start(f32[320,256]{1,0:T(8,128)S(1)} %get-tuple-element.47.refs_0_), channel_id=1, source_target_pairs={{0,1},{1,0},{2,3},{3,2},{4,5},{5,4},{6,7},{7,6},{8,9},{9,8},{10,11... | collective-permute-start | bytes 983048 | tf_op jit(solution)/shard_map/ppermute | solution.py:39
  7.2 21.0 %collective-permute-start.3 = (f32[320,256]{1,0:T(8,128)S(1)}, f32[320,256]{1,0:T(8,128)S(1)}, u32[]{:S(2)}, u32[]{:S(2)}) collective-permute-start(f32[320,256]{1,0:T(8,128)S(1)} %get-tuple-element.47.refs_0_), channel_id=1, source_target_pairs={{1,2},{2,1},{5,6},{6,5},{9,10},{10,9},{13,14},{14,13},{17,18},{18,... | collective-permute-start | bytes 983048 | tf_op jit(solution)/shard_map/ppermute | solution.py:48
  30.2 9.1 %collective-permute-start.8 = (f32[256,256]{1,0:T(8,128)S(1)}, f32[256,256]{1,0:T(8,128)S(1)}, u32[]{:S(2)}, u32[]{:S(2)}) collective-permute-start(f32[256,256]{1,0:T(8,128)S(1)} %get-tuple-element.57.refs_0_), channel_id=1, source_target_pairs={{0,8},{4,12},{8,0},{12,4},{16,24},{20,28},{24,16},{28,20},{1,9},{5... | collective-permute-start | bytes 786440 | tf_op jit(solution)/shard_map/ppermute | solution.py:39
  33.7 11.3 %collective-permute-start.22 = (f32[256,256]{1,0:T(8,128)S(1)}, f32[256,256]{1,0:T(8,128)S(1)}, u32[]{:S(2)}, u32[]{:S(2)}) collective-permute-start(f32[256,256]{1,0:T(8,128)S(1)} %level0.12.refs_0_.refs_7_), channel_id=1, source_target_pairs={{0,8},{4,12},{8,0},{12,4},{16,24},{20,28},{24,16},{28,20},{1,9},{5... | collective-permute-start | bytes 786440 | tf_op jit(solution)/shard_map/ppermute | solution.py:39
  35.0 12.3 %collective-permute-start.24 = (f32[256,256]{1,0:T(8,128)S(1)}, f32[256,256]{1,0:T(8,128)S(1)}, u32[]{:S(2)}, u32[]{:S(2)}) collective-permute-start(f32[256,256]{1,0:T(8,128)S(1)} %get-tuple-element.66.refs_0_), channel_id=1, source_target_pairs={{0,4},{4,0},{8,12},{12,8},{16,20},{20,16},{24,28},{28,24},{1,5},{5... | collective-permute-start | bytes 786440 | tf_op jit(solution)/shard_map/ppermute | solution.py:39
  35.7 13.6 %collective-permute-start.11 = (f32[256,256]{1,0:T(8,128)S(1)}, f32[256,256]{1,0:T(8,128)S(1)}, u32[]{:S(2)}, u32[]{:S(2)}) collective-permute-start(f32[256,256]{1,0:T(8,128)S(1)} %get-tuple-element.61.refs_0_), channel_id=1, source_target_pairs={{0,16},{4,20},{8,24},{12,28},{16,0},{20,4},{24,8},{28,12},{1,17},{... | collective-permute-start | bytes 786440 | tf_op jit(solution)/shard_map/ppermute | solution.py:39
  40.1 10.9 %collective-permute-start.10 = (f32[256,256]{1,0:T(8,128)S(1)}, f32[256,256]{1,0:T(8,128)S(1)}, u32[]{:S(2)}, u32[]{:S(2)}) collective-permute-start(f32[256,256]{1,0:T(8,128)S(1)} %level0.8.refs_7_.refs_0_.refs_4_), channel_id=1, source_target_pairs={{0,8},{4,12},{8,0},{12,4},{16,24},{20,28},{24,16},{28,20},{1,9},{5... | collective-permute-start | bytes 786440 | tf_op jit(solution)/shard_map/ppermute | solution.py:39
  43.4 9.5 %collective-permute-start.9 = (f32[256,256]{1,0:T(8,128)S(1)}, f32[256,256]{1,0:T(8,128)S(1)}, u32[]{:S(2)}, u32[]{:S(2)}) collective-permute-start(f32[256,256]{1,0:T(8,128)S(1)} %get-tuple-element.59.refs_0_), channel_id=1, source_target_pairs={{0,4},{4,0},{8,12},{12,8},{16,20},{20,16},{24,28},{28,24},{1,5},{5... | collective-permute-start | bytes 786440 | tf_op jit(solution)/shard_map/ppermute | solution.py:39
  45.3 10.6 %collective-permute-start.23 = (f32[256,256]{1,0:T(8,128)S(1)}, f32[256,256]{1,0:T(8,128)S(1)}, u32[]{:S(2)}, u32[]{:S(2)}) collective-permute-start(f32[256,256]{1,0:T(8,128)S(1)} %level1.12.refs_0_.refs_4_), channel_id=1, source_target_pairs={{0,16},{4,20},{8,24},{12,28},{16,0},{20,4},{24,8},{28,12},{1,17},{... | collective-permute-start | bytes 786440 | tf_op jit(solution)/shard_map/ppermute | solution.py:39
  47.7 8.7 %collective-permute-start.25 = (f32[256,256]{1,0:T(8,128)S(1)}, f32[256,256]{1,0:T(8,128)S(1)}, u32[]{:S(2)}, u32[]{:S(2)}) collective-permute-start(f32[256,256]{1,0:T(8,128)S(1)} %level0.13.refs_0_.refs_7_), channel_id=1, source_target_pairs={{0,8},{4,12},{8,0},{12,4},{16,24},{20,28},{24,16},{28,20},{1,9},{5... | collective-permute-start | bytes 786440 | tf_op jit(solution)/shard_map/ppermute | solution.py:39
  51.4 10.2 %collective-permute-start.14 = (f32[256,256]{1,0:T(8,128)S(1)}, f32[256,256]{1,0:T(8,128)S(1)}, u32[]{:S(2)}, u32[]{:S(2)}) collective-permute-start(f32[256,256]{1,0:T(8,128)S(1)} %level1.8.refs_4_.refs_0_), channel_id=1, source_target_pairs={{0,16},{4,20},{8,24},{12,28},{16,0},{20,4},{24,8},{28,12},{1,17},{... | collective-permute-start | bytes 786440 | tf_op jit(solution)/shard_map/ppermute | solution.py:39
  53.3 8.7 %collective-permute-start.13 = (f32[256,256]{1,0:T(8,128)S(1)}, f32[256,256]{1,0:T(8,128)S(1)}, u32[]{:S(2)}, u32[]{:S(2)}) collective-permute-start(f32[256,256]{1,0:T(8,128)S(1)} %level0.9.refs_7_.refs_0_), channel_id=1, source_target_pairs={{0,8},{4,12},{8,0},{12,4},{16,24},{20,28},{24,16},{28,20},{1,9},{5... | collective-permute-start | bytes 786440 | tf_op jit(solution)/shard_map/ppermute | solution.py:39
  56.8 9.9 %collective-permute-start.26 = (f32[256,256]{1,0:T(8,128)S(1)}, f32[256,256]{1,0:T(8,128)S(1)}, u32[]{:S(2)}, u32[]{:S(2)}) collective-permute-start(f32[256,256]{1,0:T(8,128)S(1)} %level1.13.refs_0_.refs_4_), channel_id=1, source_target_pairs={{0,16},{4,20},{8,24},{12,28},{16,0},{20,4},{24,8},{28,12},{1,17},{... | collective-permute-start | bytes 786440 | tf_op jit(solution)/shard_map/ppermute | solution.py:39
  61.6 8.5 %collective-permute-start.30 = (f32[256,256]{1,0:T(8,128)S(1)}, f32[256,256]{1,0:T(8,128)S(1)}, u32[]{:S(2)}, u32[]{:S(2)}) collective-permute-start(f32[256,256]{1,0:T(8,128)S(1)} %get-tuple-element.68.refs_0_), channel_id=1, source_target_pairs={{0,4},{4,0},{8,12},{12,8},{16,20},{20,16},{24,28},{28,24},{1,5},{5... | collective-permute-start | bytes 786440 | tf_op jit(solution)/shard_map/ppermute | solution.py:39
  62.4 10.3 %collective-permute-start.17 = (f32[256,256]{1,0:T(8,128)S(1)}, f32[256,256]{1,0:T(8,128)S(1)}, u32[]{:S(2)}, u32[]{:S(2)}) collective-permute-start(f32[256,256]{1,0:T(8,128)S(1)} %level1.9.refs_4_.refs_0_), channel_id=1, source_target_pairs={{0,16},{4,20},{8,24},{12,28},{16,0},{20,4},{24,8},{28,12},{1,17},{... | collective-permute-start | bytes 786440 | tf_op jit(solution)/shard_map/ppermute | solution.py:39
  63.8 9.8 %collective-permute-start.16 = (f32[256,256]{1,0:T(8,128)S(1)}, f32[256,256]{1,0:T(8,128)S(1)}, u32[]{:S(2)}, u32[]{:S(2)}) collective-permute-start(f32[256,256]{1,0:T(8,128)S(1)} %level0.10.refs_7_.refs_0_), channel_id=1, source_target_pairs={{0,8},{4,12},{8,0},{12,4},{16,24},{20,28},{24,16},{28,20},{1,9},{5... | collective-permute-start | bytes 786440 | tf_op jit(solution)/shard_map/ppermute | solution.py:39
  66.7 9.0 %collective-permute-start.15 = (f32[256,256]{1,0:T(8,128)S(1)}, f32[256,256]{1,0:T(8,128)S(1)}, u32[]{:S(2)}, u32[]{:S(2)}) collective-permute-start(f32[256,256]{1,0:T(8,128)S(1)} %get-tuple-element.65.refs_0_), channel_id=1, source_target_pairs={{0,4},{4,0},{8,12},{12,8},{16,20},{20,16},{24,28},{28,24},{1,5},{5... | collective-permute-start | bytes 786440 | tf_op jit(solution)/shard_map/ppermute | solution.py:39
  68.4 9.9 %collective-permute-start.29 = (f32[256,256]{1,0:T(8,128)S(1)}, f32[256,256]{1,0:T(8,128)S(1)}, u32[]{:S(2)}, u32[]{:S(2)}) collective-permute-start(f32[256,256]{1,0:T(8,128)S(1)} %level1.14.refs_0_.refs_4_), channel_id=1, source_target_pairs={{0,16},{4,20},{8,24},{12,28},{16,0},{20,4},{24,8},{28,12},{1,17},{... | collective-permute-start | bytes 786440 | tf_op jit(solution)/shard_map/ppermute | solution.py:39
  70.5 9.4 %collective-permute-start.31 = (f32[256,256]{1,0:T(8,128)S(1)}, f32[256,256]{1,0:T(8,128)S(1)}, u32[]{:S(2)}, u32[]{:S(2)}) collective-permute-start(f32[256,256]{1,0:T(8,128)S(1)} %level0.15.refs_0_), channel_id=1, source_target_pairs={{0,8},{4,12},{8,0},{12,4},{16,24},{20,28},{24,16},{28,20},{1,9},{5... | collective-permute-start | bytes 786440 | tf_op jit(solution)/shard_map/ppermute | solution.py:39
  74.0 9.3 %collective-permute-start.19 = (f32[256,256]{1,0:T(8,128)S(1)}, f32[256,256]{1,0:T(8,128)S(1)}, u32[]{:S(2)}, u32[]{:S(2)}) collective-permute-start(f32[256,256]{1,0:T(8,128)S(1)} %level1.10.refs_4_.refs_0_), channel_id=1, source_target_pairs={{0,16},{4,20},{8,24},{12,28},{16,0},{20,4},{24,8},{28,12},{1,17},{... | collective-permute-start | bytes 786440 | tf_op jit(solution)/shard_map/ppermute | solution.py:39
  80.3 9.3 %collective-permute-start.32 = (f32[256,256]{1,0:T(8,128)S(1)}, f32[256,256]{1,0:T(8,128)S(1)}, u32[]{:S(2)}, u32[]{:S(2)}) collective-permute-start(f32[256,256]{1,0:T(8,128)S(1)} %level1.15.refs_0_), channel_id=1, source_target_pairs={{0,16},{4,20},{8,24},{12,28},{16,0},{20,4},{24,8},{28,12},{1,17},{... | collective-permute-start | bytes 786440 | tf_op jit(solution)/shard_map/ppermute | solution.py:39
  84.6 9.2 %collective-permute-start.20 = (f32[256,256]{1,0:T(8,128)S(1)}, f32[256,256]{1,0:T(8,128)S(1)}, u32[]{:S(2)}, u32[]{:S(2)}) collective-permute-start(f32[256,256]{1,0:T(8,128)S(1)} %level1.11.refs_0_), channel_id=1, source_target_pairs={{0,16},{4,20},{8,24},{12,28},{16,0},{20,4},{24,8},{28,12},{1,17},{... | collective-permute-start | bytes 786440 | tf_op jit(solution)/shard_map/ppermute | solution.py:39
  (9 other events, 61.7 us)

commit v4 on v3

--- a/solution.py
+++ b/solution.py
@@ -8,6 +8,7 @@
 from jax.sharding import PartitionSpec as P
 
 CHUNKS = 8
+LEAVES = {2: (2, 4), 3: (3, 5)}
 STEP = 512
 F32, BF16 = jnp.float32, jnp.bfloat16
 VMEM = pl.BlockSpec(memory_space=pltpu.VMEM)
@@ -15,7 +16,7 @@
 TOKEN = pltpu.VMEM((8, 128), F32)
 
 
-def call(kernel, name, args, outs, scratch=(), hbm_in=(), hbm_out=(), alias=None, after=()):
+def call(kernel, name, args, outs, scratch=(), hbm_in=(), hbm_out=(), alias=None, after=(), size=1000):
     count, waits = len(args), len(after)
 
     def body(*refs):
@@ -30,7 +31,7 @@
         scratch_shapes=list(scratch),
         input_output_aliases=alias or {},
         compiler_params=pltpu.CompilerParams(vmem_limit_bytes=20 << 20),
-        cost_estimate=pl.CostEstimate(flops=1000, bytes_accessed=1000, transcendentals=0),
+        cost_estimate=pl.CostEstimate(flops=size, bytes_accessed=1000, transcendentals=0),
         name=name,
     )(*map(pltpu.with_memory_space_constraint, (*args, *after), spaces))
 
@@ -105,13 +106,37 @@
 
 
 def tree_blocks(n, start, rows, *refs):
-    pieces, outs = refs[:n], refs[n:]
+    pieces, outs, odd = refs[:n], refs[n:-1], refs[-1]
     for level, out in enumerate(outs):
         place(pieces, pl.multiple_of(start + bit_of(level) * rows, rows), rows, out)
-
-
-def level_factors(level, own, far, fh, fl):
+    mine = lax.axis_index("col")
+    for k in range(odd.shape[0] // rows):
+        odd[pl.ds(k * rows, rows), :] = outs[1][pl.ds(pl.multiple_of((mine ^ (2 * k + 1)) * rows, rows), rows), :]
+
+
+def even_rows(n, start, rows, *refs):
+    span = pl.ds(pl.multiple_of(start + bit_of(1) * rows, rows), rows)
+    out = refs[-1]
+    if n == 4:
+        whole, left, right = refs[:-1]
+        size = left.shape[1]
+        out[:rows, :] = whole[span, :]
+        out[rows:, :size], out[rows:, size:] = left[span, :], right[span, :]
+    else:
+        for k, piece in enumerate(refs[:-1]):
+            out[pl.ds(k * rows, rows), :] = piece[span, :]
+
+
+def level_factors(level, rows, own, *refs):
     width = own.shape[0]
+    if len(refs) == 3:
+        far, fh, fl = refs
+    else:
+        even, odd, fh, fl, far = refs
+        mine = lax.axis_index("col")
+        for k in range(width // rows):
+            to = pl.ds(pl.multiple_of((mine ^ k) * rows, rows), rows)
+            far[to, :] = (odd if k % 2 else even)[pl.ds(k // 2 * rows, rows), :]
 
     @pl.when(bit_of(level) == 0)
     def _():
@@ -149,17 +174,19 @@
     ph[...], plo[...] = split(dotf(full, t[...], ((1,), (1,))))
 
 
-def leaf_apply(start, c, ch, cl, vth, vtl, ph, plo, top, *outs):
-    width, size = top.shape
-    at = pl.ds(start, size)
-    h, l = split(dot3(vth[...], vtl[...], ch[:, at], cl[:, at]))
-    if len(outs) == 2:
-        outs[0][...], outs[1][...] = h, l
-        top[...] = c[:width, at] - dot3(ph[:width, :], plo[:width, :], h, l)
-    else:
-        change = dot3(ph[...], plo[...], h, l)
-        top[...] = c[:width, at] - change[:width]
-        outs[0][...] = c[width:, at] - change[width:]
+def leaf_apply(starts, c, ch, cl, vth, vtl, ph, plo, *outs):
+    for k, start in enumerate(starts):
+        top, *others = outs[k * len(outs) // len(starts):(k + 1) * len(outs) // len(starts)]
+        width, size = top.shape
+        at = pl.ds(start, size)
+        h, l = split(dot3(vth[...], vtl[...], ch[:, at], cl[:, at]))
+        if len(others) == 2:
+            others[0][...], others[1][...] = h, l
+            top[...] = c[:width, at] - dot3(ph[:width, :], plo[:width, :], h, l)
+        else:
+            change = dot3(ph[...], plo[...], h, l)
+            top[...] = c[:width, at] - change[:width]
+            others[0][...] = c[width:, at] - change[width:]
 
 
 def rest_apply(start, c, ph, plo, ih, il, out):
@@ -178,28 +205,29 @@
     out[...] = level_result(start, own, far, fh, fl, out.shape[1])
 
 
-def store(sources, out, top, sems):
+def store(sources, out, top, left, sems, first=0):
     copies = []
     for k, source in enumerate(sources):
         rows, size = source.shape
-        to = out.at[pl.ds(top, rows), pl.ds(k * size, size)]
-        copies.append(pltpu.make_async_copy(source, to, sems.at[k]))
+        to = out.at[pl.ds(top, rows), pl.ds(left + k * size, size)]
+        copies.append(pltpu.make_async_copy(source, to, sems.at[first + k]))
         copies[-1].start()
     return copies
 
 
-def lower_store(*refs):
+def early_store(*refs):
     *sources, out, sems = refs
-    for copy in store(sources, out, out.shape[0] - sources[0].shape[0], sems):
+    lower, upper = sources[:CHUNKS], sources[CHUNKS:]
+    for copy in store(lower, out, out.shape[0] - lower[0].shape[0], 0, sems) + store(upper, out, 0, 0, sems, CHUNKS):
         copy.wait()
 
 
 def last_apply(own, far, fh, fl, *refs):
     *sources, _, out, buffer, sems = refs
-    copies = store(sources, out, 0, sems)
     width, size = own.shape
+    copies = store(sources, out, 0, out.shape[1] - (len(sources) + 1) * size, sems)
     buffer[...] = level_result(0, own, far, fh, fl, size)
-    to = out.at[pl.ds(0, width), pl.ds(len(sources) * size, size)]
+    to = out.at[pl.ds(0, width), pl.ds(out.shape[1] - size, size)]
     copies.append(pltpu.make_async_copy(buffer, to, sems.at[len(sources)]))
     copies[-1].start()
     for copy in copies:
@@ -225,6 +253,11 @@
         hbm_in=range(4),
     )
     pieces = spread(whole, halves, "col")
+    n = lax.axis_size("col")
+    some = [pieces[0], *pieces[3:5]] if n == 4 else pieces[0::2]
+    half = pltpu.VMEM((width // 2, width), F32)
+    (even,) = call(functools.partial(even_rows, n, vr + tr, tr), "even_rows", some, [half])
+    even = swap(even, "row", 2)
     c, ch, cl = call(
         load,
         "load",
@@ -234,13 +267,18 @@
         hbm_in=(0,),
         after=pieces[3:5],
     )
-    owns = call(functools.partial(tree_blocks, len(pieces), vr + tr, tr), "tree_blocks", pieces, [block] * depth, after=[ch])
+    *owns, odd = call(
+        functools.partial(tree_blocks, len(pieces), vr + tr, tr), "tree_blocks", pieces, [block] * depth + [half], after=[ch]
+    )
+    odd = swap(odd, "row", 2)
     factors = [
         call(
-            functools.partial(level_factors, level),
+            functools.partial(level_factors, level, tr),
             f"factors{level}",
-            (owns[level], swap(owns[level], "row", 1 << level)),
+            (owns[level], *([even, odd] if level == 1 else [swap(owns[level], "row", 1 << level)])),
             [block16(width, 2 * width)] * 2,
+            [block] * (level == 1),
+            size=2 * 10**9 if level == 1 else 1000,
         )
         for level in range(depth)
     ]
@@ -250,6 +288,7 @@
         pieces,
         [block16(width, height)] * 2 + [block16(height, width)] * 2,
         [pltpu.VMEM((height, width), F32), block],
+        after=[even],
     )
 
     made = [[] for _ in range(depth - 1)]
@@ -276,27 +315,29 @@
                 waits = done[k - 2:k - 1]
             advance(level, made[level - 1][k], sent[level - 1][k], 0, waits)
 
-    done, rests, tops, fars = [], [], [], []
+    done, rests, tops, fars = [], {}, {}, {}
 
     def make_leaf(k):
+        if k in tops:
+            return
         above, below = pltpu.VMEM((width, part), F32), pltpu.VMEM((height - width, part), F32)
-        top, *others = call(
-            functools.partial(leaf_apply, k * part),
+        ks = LEAVES.get(k, (k,))
+        outs = call(
+            functools.partial(leaf_apply, [j * part for j in ks]),
             f"leaf_{k}",
             (c, ch, cl, vth, vtl, ph, plo),
-            [above] + ([block16(width, part)] * 2 if k < 2 else [below]),
-            after=tops if k == 1 else made[0][k - 2:k - 1] if k else (),
+            [above, *([block16(width, part)] * 2 if k < 2 else [below])] * len(ks),
+            after=[tops[0]] if k == 1 else made[0][k - 2:k - 1] if k else (),
         )
         if k < 2:
-            others = call(
-                functools.partial(rest_apply, k * part), f"rest_{k}", (c, ph, plo, *others), [below], after=made[0][k:k + 1]
-            )
-        rests.extend(others)
-        tops.append(top)
-        fars.append(swap(top, "row", 1))
+            outs = (outs[0], *call(
+                functools.partial(rest_apply, k * part), f"rest_{k}", (c, ph, plo, *outs[1:]), [below], after=made[0][k:k + 1]
+            ))
+        for j, top, rest in zip(ks, outs[0::2], outs[1::2]):
+            tops[j], rests[j], fars[j] = top, rest, swap(top, "row", 1)
 
     def first_level(k):
-        waits = made[min(1, depth - 2)][k - 2:k - 1] if k >= 2 else [factors[1][0]] * k
+        waits = made[min(1, depth - 2)][k - 2:k - 1] if k >= 2 else [factors[1][0]]
         advance(0, tops[k], fars[k], 0, waits)
 
     make_leaf(0)
@@ -318,17 +359,19 @@
                 [pltpu.VMEM((width, part), F32)],
             )
     whole = jax.ShapeDtypeStruct((height, columns), F32)
-    sems = pltpu.SemaphoreType.DMA((CHUNKS,))
-    (out,) = call(lower_store, "lower_store", rests, [whole], [sems], hbm_out=(0,))
+    sems, kept = pltpu.SemaphoreType.DMA((2 * CHUNKS,)), CHUNKS - 3
+    early = [rests[k] for k in range(CHUNKS)] + done[:kept]
+    (out,) = call(early_store, "early_store", early, [whole], [sems], hbm_out=(0,))
+    late = done[kept:]
     (out,) = call(
         last_apply,
         "finish",
-        (made[-1][-1], sent[-1][-1], *factors[-1], *done, out),
+        (made[-1][-1], sent[-1][-1], *factors[-1], *late, out),
         [whole],
         [pltpu.VMEM((width, part), F32), sems],
-        hbm_in=(3 + CHUNKS,),
+        hbm_in=(4 + len(late),),
         hbm_out=(0,),
-        alias={3 + CHUNKS: 0},
+        alias={4 + len(late): 0},
     )
     return out
 

time: 95.7 us -> 93.8 us (0.980)
  starting transfers between devices: 40 us -> 38.7 us
  Pallas kernels: 25.8 us -> 24.8 us
    ppermute x30 -> x31, waiting for transfers between devices: 25.5 us -> 27.9 us  [swap(): lax.ppermute(value, axis, [(i, i ^ mask) for i in range(lax.axis_size(axi...]
    ppermute x2, waiting for transfers between devices: 3.53 us -> 1.6 us  [spread(): ends = [lax.ppermute(second, axis, [(1, 0), (2, 3)]) for second in seconds]]
    ppermute x30 -> x31, starting transfers between devices: 36.8 us -> 35.5 us  [swap(): lax.ppermute(value, axis, [(i, i ^ mask) for i in range(lax.axis_size(axi...]
    pallas_call x42 -> x41, Pallas kernels: 25.8 us -> 24.8 us  [call(): pl.pallas_call(body, out_shape=[jax.ShapeDtypeStruct(o.shape, o.dtype) if...]
  transfers between devices with their start and end apart: 33 -> 34, of which waited for: 13 -> 17; matrix products, arithmetic and copies ran while one was open for 0% -> 0% of each run, Pallas kernels for 24% -> 24%
where the time goes in v4:
time: 93.8 us; the launch traced here: 93.6 us
  starting transfers between devices  38.7 us (41%)
  waiting for transfers between devices  29.5 us (31%)
  Pallas kernels  24.8 us (26%)
    ppermute x31, starting transfers between devices, swap(): lax.ppermute(value, axis, [(i, i ^ mask) for i in range(lax.axis_size(axi...  35.5 us
    ppermute x31, waiting for transfers between devices, swap(): lax.ppermute(value, axis, [(i, i ^ mask) for i in range(lax.axis_size(axi...  27.9 us
    pallas_call x41, Pallas kernels, call(): pl.pallas_call(body, out_shape=[jax.ShapeDtypeStruct(o.shape, o.dtype) if...  24.8 us
    ppermute x2, starting transfers between devices, spread(): ends = [lax.ppermute(second, axis, [(1, 0), (2, 3)]) for second in seconds]  2.56 us
  transfers between devices with their start and end apart: 34, of which 17 were waited for; matrix products, arithmetic and copies ran while one was open for 0% of the time, Pallas kernels for 24%

profile of v4, /device:TPU:0, one launch (start us, length us, event | category | flops | bytes accessed | tf_op | source)
XLA Modules:
  0.0 93.6 jit_solution(3773850095587883569)
XLA Ops:
  1.2 4.1 %collective-permute-start = (f32[320,128]{1,0:T(8,128)S(1)}, f32[320,128]{1,0:T(8,128)S(1)}, u32[]{:S(2)}, u32[]{:S(2)}) collective-permute-start(f32[320,128]{1,0:T(8,128)S(1)} %get-tuple-element.43), channel_id=1, source_target_pairs={{0,2},{1,3},{2,0},{3,1},{4,6},{5,7},{6,4},{7,5},{8,10},{9,11},{10,... | collective-permute-start | bytes 491528 | tf_op jit(solution)/shard_map/ppermute | solution.py:40
  5.4 1.8 %collective-permute-start.2 = (f32[320,256]{1,0:T(8,128)S(1)}, f32[320,256]{1,0:T(8,128)S(1)}, u32[]{:S(2)}, u32[]{:S(2)}) collective-permute-start(f32[320,256]{1,0:T(8,128)S(1)} %get-tuple-element.48.refs_0_), channel_id=1, source_target_pairs={{0,1},{1,0},{2,3},{3,2},{4,5},{5,4},{6,7},{7,6},{8,9},{9,8},{10,11... | collective-permute-start | bytes 983048 | tf_op jit(solution)/shard_map/ppermute | solution.py:40
  7.9 9.6 %collective-permute-done.refs_1_.refs_3_ = f32[320,128]{1,0:T(8,128)S(1)} collective-permute-done((f32[320,128]{1,0:T(8,128)S(1)}, f32[320,128]{1,0:T(8,128)S(1)}, u32[]{:S(2)}, u32[]{:S(2)}) %collective-permute-start) | collective-permute-done | bytes 163872 | tf_op jit(solution)/shard_map/ppermute | solution.py:40
  18.7 2.2 %collective-permute-done.1.refs_2_.refs_4_ = f32[320,128]{1,0:T(8,128)S(1)} collective-permute-done((f32[320,128]{1,0:T(8,128)S(1)}, f32[320,128]{1,0:T(8,128)S(1)}, u32[]{:S(2)}, u32[]{:S(2)}) %collective-permute-start.1) | collective-permute-done | bytes 163872 | tf_op jit(solution)/shard_map/ppermute | solution.py:40
  22.2 1.9 %collective-permute-start.6 = (f32[128,256]{1,0:T(8,128)S(1)}, f32[128,256]{1,0:T(8,128)S(1)}, u32[]{:S(2)}, u32[]{:S(2)}) collective-permute-start(f32[128,256]{1,0:T(8,128)S(1)} %even_rows.1), channel_id=1, source_target_pairs={{0,8},{4,12},{8,0},{12,4},{16,24},{20,28},{24,16},{28,20},{1,9},{5... | collective-permute-start | bytes 393224 | tf_op jit(solution)/shard_map/ppermute | solution.py:40
  24.1 2.4 %load.1 = (f32[512,2048]{1,0:T(8,128)S(1)}, bf16[512,2048]{1,0:T(8,128)(2,1)S(1)}, bf16[512,2048]{1,0:T(8,128)(2,1)S(1)}) custom-call(f32[512,2048]{1,0:T(8,128)} %refs_0_.3, f32[320,128]{1,0:T(8,128)S(1)} %collective-permute-done.refs_1_.refs_3_, f32[320,128]{1,0:T(8,128)S(1)} %collective-permute-done.1.refs_2_.refs_4_), custom_call_target="tpu_custom_call" | custom-call | flops 1000 | bytes 1000 | tf_op jit(solution)/shard_map/load/pallas_call | solution.py:26
  26.6 1.6 %collective-permute-done.5.refs_6_ = f32[320,128]{1,0:T(8,128)S(1)} collective-permute-done((f32[320,128]{1,0:T(8,128)S(1)}, f32[320,128]{1,0:T(8,128)S(1)}, u32[]{:S(2)}, u32[]{:S(2)}) %collective-permute-start.5) | collective-permute-done | bytes 163872 | tf_op jit(solution)/shard_map/ppermute | solution.py:50
  28.3 1.9 %collective-permute-start.9 = (f32[128,256]{1,0:T(8,128)S(1)}, f32[128,256]{1,0:T(8,128)S(1)}, u32[]{:S(2)}, u32[]{:S(2)}) collective-permute-start(f32[128,256]{1,0:T(8,128)S(1)} %get-tuple-element.59), channel_id=1, source_target_pairs={{0,8},{4,12},{8,0},{12,4},{16,24},{20,28},{24,16},{28,20},{1,9},{5... | collective-permute-start | bytes 393224 | tf_op jit(solution)/shard_map/ppermute | solution.py:40
  34.5 2.2 %collective-permute-start.25 = (f32[256,256]{1,0:T(8,128)S(1)}, f32[256,256]{1,0:T(8,128)S(1)}, u32[]{:S(2)}, u32[]{:S(2)}) collective-permute-start(f32[256,256]{1,0:T(8,128)S(1)} %level0.12.refs_7_.refs_0_), channel_id=1, source_target_pairs={{0,8},{4,12},{8,0},{12,4},{16,24},{20,28},{24,16},{28,20},{1,9},{5... | collective-permute-start | bytes 786440 | tf_op jit(solution)/shard_map/ppermute | solution.py:40
  36.7 1.5 %leaf_2.1 = (f32[256,256]{1,0:T(8,128)S(1)}, f32[256,256]{1,0:T(8,128)S(1)}, f32[256,256]{1,0:T(8,128)S(1)}, f32[256,256]{1,0:T(8,128)S(1)}) custom-call(f32[512,2048]{1,0:T(8,128)S(1)} %get-tuple-element.45.refs_0_, bf16[512,2048]{1,0:T(8,128)(2,1)S(1)} %get-tuple-element.46.refs_1_.refs_7_, bf16[512,2048]{1,0:T(8,128)(2,1)S(1)} %get-tuple-element.47.refs_2_, ...), custom_call_target="tpu_custom_call" | custom-call | flops 1000 | bytes 1000 | tf_op jit(solution)/shard_map/leaf_2/pallas_call | solution.py:26
  38.2 1.6 %collective-permute-start.13 = (f32[256,256]{1,0:T(8,128)S(1)}, f32[256,256]{1,0:T(8,128)S(1)}, u32[]{:S(2)}, u32[]{:S(2)}) collective-permute-start(f32[256,256]{1,0:T(8,128)S(1)} %get-tuple-element.64.refs_0_), channel_id=1, source_target_pairs={{0,16},{4,20},{8,24},{12,28},{16,0},{20,4},{24,8},{28,12},{1,17},{... | collective-permute-start | bytes 786440 | tf_op jit(solution)/shard_map/ppermute | solution.py:40
  40.5 1.5 %leaf_3.1 = (f32[256,256]{1,0:T(8,128)S(1)}, f32[256,256]{1,0:T(8,128)S(1)}, f32[256,256]{1,0:T(8,128)S(1)}, f32[256,256]{1,0:T(8,128)S(1)}) custom-call(f32[512,2048]{1,0:T(8,128)S(1)} %get-tuple-element.45.refs_0_, bf16[512,2048]{1,0:T(8,128)(2,1)S(1)} %get-tuple-element.46.refs_1_.refs_7_, bf16[512,2048]{1,0:T(8,128)(2,1)S(1)} %get-tuple-element.47.refs_2_, ...), custom_call_target="tpu_custom_call" | custom-call | flops 1000 | bytes 1000 | tf_op jit(solution)/shard_map/leaf_3/pallas_call | solution.py:26
  43.6 2.5 %collective-permute-start.27 = (f32[256,256]{1,0:T(8,128)S(1)}, f32[256,256]{1,0:T(8,128)S(1)}, u32[]{:S(2)}, u32[]{:S(2)}) collective-permute-start(f32[256,256]{1,0:T(8,128)S(1)} %level1.12.refs_4_.refs_0_), channel_id=1, source_target_pairs={{0,16},{4,20},{8,24},{12,28},{16,0},{20,4},{24,8},{28,12},{1,17},{... | collective-permute-start | bytes 786440 | tf_op jit(solution)/shard_map/ppermute | solution.py:40
  46.4 1.5 %collective-permute-start.26 = (f32[256,256]{1,0:T(8,128)S(1)}, f32[256,256]{1,0:T(8,128)S(1)}, u32[]{:S(2)}, u32[]{:S(2)}) collective-permute-start(f32[256,256]{1,0:T(8,128)S(1)} %level0.13.refs_0_), channel_id=1, source_target_pairs={{0,8},{4,12},{8,0},{12,4},{16,24},{20,28},{24,16},{28,20},{1,9},{5... | collective-permute-start | bytes 786440 | tf_op jit(solution)/shard_map/ppermute | solution.py:40
  49.8 1.8 %collective-permute-start.15 = (f32[256,256]{1,0:T(8,128)S(1)}, f32[256,256]{1,0:T(8,128)S(1)}, u32[]{:S(2)}, u32[]{:S(2)}) collective-permute-start(f32[256,256]{1,0:T(8,128)S(1)} %level1.8.refs_4_.refs_0_), channel_id=1, source_target_pairs={{0,16},{4,20},{8,24},{12,28},{16,0},{20,4},{24,8},{28,12},{1,17},{... | collective-permute-start | bytes 786440 | tf_op jit(solution)/shard_map/ppermute | solution.py:40
  55.6 1.7 %collective-permute-start.30 = (f32[256,256]{1,0:T(8,128)S(1)}, f32[256,256]{1,0:T(8,128)S(1)}, u32[]{:S(2)}, u32[]{:S(2)}) collective-permute-start(f32[256,256]{1,0:T(8,128)S(1)} %level1.13.refs_4_.refs_0_), channel_id=1, source_target_pairs={{0,16},{4,20},{8,24},{12,28},{16,0},{20,4},{24,8},{28,12},{1,17},{... | collective-permute-start | bytes 786440 | tf_op jit(solution)/shard_map/ppermute | solution.py:40
  61.4 1.5 %collective-permute-start.18 = (f32[256,256]{1,0:T(8,128)S(1)}, f32[256,256]{1,0:T(8,128)S(1)}, u32[]{:S(2)}, u32[]{:S(2)}) collective-permute-start(f32[256,256]{1,0:T(8,128)S(1)} %level1.9.refs_4_.refs_0_), channel_id=1, source_target_pairs={{0,16},{4,20},{8,24},{12,28},{16,0},{20,4},{24,8},{28,12},{1,17},{... | collective-permute-start | bytes 786440 | tf_op jit(solution)/shard_map/ppermute | solution.py:40
  66.8 1.5 %collective-permute-start.32 = (f32[256,256]{1,0:T(8,128)S(1)}, f32[256,256]{1,0:T(8,128)S(1)}, u32[]{:S(2)}, u32[]{:S(2)}) collective-permute-start(f32[256,256]{1,0:T(8,128)S(1)} %level1.14.refs_4_.refs_0_), channel_id=1, source_target_pairs={{0,16},{4,20},{8,24},{12,28},{16,0},{20,4},{24,8},{28,12},{1,17},{... | collective-permute-start | bytes 786440 | tf_op jit(solution)/shard_map/ppermute | solution.py:40
  70.2 2.0 %collective-permute-done.17.refs_1_ = f32[256,256]{1,0:T(8,128)S(1)} collective-permute-done((f32[256,256]{1,0:T(8,128)S(1)}, f32[256,256]{1,0:T(8,128)S(1)}, u32[]{:S(2)}, u32[]{:S(2)}) %collective-permute-start.17) | collective-permute-done | bytes 262176 | tf_op jit(solution)/shard_map/ppermute | solution.py:40
  76.4 1.6 %collective-permute-done.31.refs_1_ = f32[256,256]{1,0:T(8,128)S(1)} collective-permute-done((f32[256,256]{1,0:T(8,128)S(1)}, f32[256,256]{1,0:T(8,128)S(1)}, u32[]{:S(2)}, u32[]{:S(2)}) %collective-permute-start.31) | collective-permute-done | bytes 262176 | tf_op jit(solution)/shard_map/ppermute | solution.py:40
  79.5 2.3 %collective-permute-done.20.refs_1_ = f32[256,256]{1,0:T(8,128)S(1)} collective-permute-done((f32[256,256]{1,0:T(8,128)S(1)}, f32[256,256]{1,0:T(8,128)S(1)}, u32[]{:S(2)}, u32[]{:S(2)}) %collective-permute-start.20) | collective-permute-done | bytes 262176 | tf_op jit(solution)/shard_map/ppermute | solution.py:40
  82.9 1.6 %collective-permute-start.21 = (f32[256,256]{1,0:T(8,128)S(1)}, f32[256,256]{1,0:T(8,128)S(1)}, u32[]{:S(2)}, u32[]{:S(2)}) collective-permute-start(f32[256,256]{1,0:T(8,128)S(1)} %level1.11.refs_0_), channel_id=1, source_target_pairs={{0,16},{4,20},{8,24},{12,28},{16,0},{20,4},{24,8},{28,12},{1,17},{... | collective-permute-start | bytes 786440 | tf_op jit(solution)/shard_map/ppermute | solution.py:40
  85.0 1.9 %early_store.1.refs_6_ = f32[512,2048]{1,0:T(8,128)} custom-call(f32[256,256]{1,0:T(8,128)S(1)} %rest_0.1.refs_0_, f32[256,256]{1,0:T(8,128)S(1)} %rest_1.1.refs_1_, f32[256,256]{1,0:T(8,128)S(1)} %get-tuple-element.75.refs_2_, f32[256,256]{1,0:T(8,128)S(1)} %get-tuple-element.76.refs_3_, f32[256,256]{1,0:T(8,128)S(1)} %get-tuple-element.77.refs_4_, ...), custom_call_target="tpu_custom_call" | custom-call | flops 1000 | bytes 1000 | tf_op jit(solution)/shard_map/early_store/pallas_call | solution.py:26
  88.1 4.1 %collective-permute-done.21.refs_1_ = f32[256,256]{1,0:T(8,128)S(1)} collective-permute-done((f32[256,256]{1,0:T(8,128)S(1)}, f32[256,256]{1,0:T(8,128)S(1)}, u32[]{:S(2)}, u32[]{:S(2)}) %collective-permute-start.21) | collective-permute-done | bytes 262176 | tf_op jit(solution)/shard_map/ppermute | solution.py:40
  (85 shorter events, 36.7 us)
Async XLA Ops:
  1.2 16.3 %collective-permute-start = (f32[320,128]{1,0:T(8,128)S(1)}, f32[320,128]{1,0:T(8,128)S(1)}, u32[]{:S(2)}, u32[]{:S(2)}) collective-permute-start(f32[320,128]{1,0:T(8,128)S(1)} %get-tuple-element.43), channel_id=1, source_target_pairs={{0,2},{1,3},{2,0},{3,1},{4,6},{5,7},{6,4},{7,5},{8,10},{9,11},{10,... | collective-permute-start | bytes 491528 | tf_op jit(solution)/shard_map/ppermute | solution.py:40
  5.3 15.6 %collective-permute-start.1 = (f32[320,128]{1,0:T(8,128)S(1)}, f32[320,128]{1,0:T(8,128)S(1)}, u32[]{:S(2)}, u32[]{:S(2)}) collective-permute-start(f32[320,128]{1,0:T(8,128)S(1)} %get-tuple-element.44), channel_id=1, source_target_pairs={{0,2},{1,3},{2,0},{3,1},{4,6},{5,7},{6,4},{7,5},{8,10},{9,11},{10,... | collective-permute-start | bytes 491528 | tf_op jit(solution)/shard_map/ppermute | solution.py:40
  5.4 22.8 %collective-permute-start.2 = (f32[320,256]{1,0:T(8,128)S(1)}, f32[320,256]{1,0:T(8,128)S(1)}, u32[]{:S(2)}, u32[]{:S(2)}) collective-permute-start(f32[320,256]{1,0:T(8,128)S(1)} %get-tuple-element.48.refs_0_), channel_id=1, source_target_pairs={{0,1},{1,0},{2,3},{3,2},{4,5},{5,4},{6,7},{7,6},{8,9},{9,8},{10,11... | collective-permute-start | bytes 983048 | tf_op jit(solution)/shard_map/ppermute | solution.py:40
  7.2 21.0 %collective-permute-start.3 = (f32[320,256]{1,0:T(8,128)S(1)}, f32[320,256]{1,0:T(8,128)S(1)}, u32[]{:S(2)}, u32[]{:S(2)}) collective-permute-start(f32[320,256]{1,0:T(8,128)S(1)} %get-tuple-element.48.refs_0_), channel_id=1, source_target_pairs={{1,2},{2,1},{5,6},{6,5},{9,10},{10,9},{13,14},{14,13},{17,18},{18,... | collective-permute-start | bytes 983048 | tf_op jit(solution)/shard_map/ppermute | solution.py:49
  17.5 9.1 %collective-permute-start.4 = (f32[320,128]{1,0:T(8,128)S(1)}, f32[320,128]{1,0:T(8,128)S(1)}, u32[]{:S(2)}, u32[]{:S(2)}) collective-permute-start(f32[320,128]{1,0:T(8,128)S(1)} %collective-permute-done.refs_1_.refs_3_), channel_id=1, source_target_pairs={{1,0},{2,3},{5,4},{6,7},{9,8},{10,11},{13,12},{14,15},{17,16},{18,... | collective-permute-start | bytes 491528 | tf_op jit(solution)/shard_map/ppermute | solution.py:50
  34.5 8.7 %collective-permute-start.25 = (f32[256,256]{1,0:T(8,128)S(1)}, f32[256,256]{1,0:T(8,128)S(1)}, u32[]{:S(2)}, u32[]{:S(2)}) collective-permute-start(f32[256,256]{1,0:T(8,128)S(1)} %level0.12.refs_7_.refs_0_), channel_id=1, source_target_pairs={{0,8},{4,12},{8,0},{12,4},{16,24},{20,28},{24,16},{28,20},{1,9},{5... | collective-permute-start | bytes 786440 | tf_op jit(solution)/shard_map/ppermute | solution.py:40
  38.2 9.7 %collective-permute-start.13 = (f32[256,256]{1,0:T(8,128)S(1)}, f32[256,256]{1,0:T(8,128)S(1)}, u32[]{:S(2)}, u32[]{:S(2)}) collective-permute-start(f32[256,256]{1,0:T(8,128)S(1)} %get-tuple-element.64.refs_0_), channel_id=1, source_target_pairs={{0,16},{4,20},{8,24},{12,28},{16,0},{20,4},{24,8},{28,12},{1,17},{... | collective-permute-start | bytes 786440 | tf_op jit(solution)/shard_map/ppermute | solution.py:40
  40.2 9.2 %collective-permute-start.12 = (f32[256,256]{1,0:T(8,128)S(1)}, f32[256,256]{1,0:T(8,128)S(1)}, u32[]{:S(2)}, u32[]{:S(2)}) collective-permute-start(f32[256,256]{1,0:T(8,128)S(1)} %level0.8.refs_7_.refs_0_.refs_4_), channel_id=1, source_target_pairs={{0,8},{4,12},{8,0},{12,4},{16,24},{20,28},{24,16},{28,20},{1,9},{5... | collective-permute-start | bytes 786440 | tf_op jit(solution)/shard_map/ppermute | solution.py:40
  42.0 9.6 %collective-permute-start.11 = (f32[256,256]{1,0:T(8,128)S(1)}, f32[256,256]{1,0:T(8,128)S(1)}, u32[]{:S(2)}, u32[]{:S(2)}) collective-permute-start(f32[256,256]{1,0:T(8,128)S(1)} %get-tuple-element.62.refs_0_), channel_id=1, source_target_pairs={{0,4},{4,0},{8,12},{12,8},{16,20},{20,16},{24,28},{28,24},{1,5},{5... | collective-permute-start | bytes 786440 | tf_op jit(solution)/shard_map/ppermute | solution.py:40
  43.6 9.9 %collective-permute-start.27 = (f32[256,256]{1,0:T(8,128)S(1)}, f32[256,256]{1,0:T(8,128)S(1)}, u32[]{:S(2)}, u32[]{:S(2)}) collective-permute-start(f32[256,256]{1,0:T(8,128)S(1)} %level1.12.refs_4_.refs_0_), channel_id=1, source_target_pairs={{0,16},{4,20},{8,24},{12,28},{16,0},{20,4},{24,8},{28,12},{1,17},{... | collective-permute-start | bytes 786440 | tf_op jit(solution)/shard_map/ppermute | solution.py:40
  46.4 8.7 %collective-permute-start.26 = (f32[256,256]{1,0:T(8,128)S(1)}, f32[256,256]{1,0:T(8,128)S(1)}, u32[]{:S(2)}, u32[]{:S(2)}) collective-permute-start(f32[256,256]{1,0:T(8,128)S(1)} %level0.13.refs_0_), channel_id=1, source_target_pairs={{0,8},{4,12},{8,0},{12,4},{16,24},{20,28},{24,16},{28,20},{1,9},{5... | collective-permute-start | bytes 786440 | tf_op jit(solution)/shard_map/ppermute | solution.py:40
  48.0 9.3 %collective-permute-start.23 = (f32[256,256]{1,0:T(8,128)S(1)}, f32[256,256]{1,0:T(8,128)S(1)}, u32[]{:S(2)}, u32[]{:S(2)}) collective-permute-start(f32[256,256]{1,0:T(8,128)S(1)} %get-tuple-element.68.refs_0_), channel_id=1, source_target_pairs={{0,4},{4,0},{8,12},{12,8},{16,20},{20,16},{24,28},{28,24},{1,5},{5... | collective-permute-start | bytes 786440 | tf_op jit(solution)/shard_map/ppermute | solution.py:40
  49.8 10.3 %collective-permute-start.15 = (f32[256,256]{1,0:T(8,128)S(1)}, f32[256,256]{1,0:T(8,128)S(1)}, u32[]{:S(2)}, u32[]{:S(2)}) collective-permute-start(f32[256,256]{1,0:T(8,128)S(1)} %level1.8.refs_4_.refs_0_), channel_id=1, source_target_pairs={{0,16},{4,20},{8,24},{12,28},{16,0},{20,4},{24,8},{28,12},{1,17},{... | collective-permute-start | bytes 786440 | tf_op jit(solution)/shard_map/ppermute | solution.py:40
  52.1 8.9 %collective-permute-start.14 = (f32[256,256]{1,0:T(8,128)S(1)}, f32[256,256]{1,0:T(8,128)S(1)}, u32[]{:S(2)}, u32[]{:S(2)}) collective-permute-start(f32[256,256]{1,0:T(8,128)S(1)} %level0.9.refs_0_), channel_id=1, source_target_pairs={{0,8},{4,12},{8,0},{12,4},{16,24},{20,28},{24,16},{28,20},{1,9},{5... | collective-permute-start | bytes 786440 | tf_op jit(solution)/shard_map/ppermute | solution.py:40
  53.4 9.5 %collective-permute-start.10 = (f32[256,256]{1,0:T(8,128)S(1)}, f32[256,256]{1,0:T(8,128)S(1)}, u32[]{:S(2)}, u32[]{:S(2)}) collective-permute-start(f32[256,256]{1,0:T(8,128)S(1)} %get-tuple-element.61.refs_0_), channel_id=1, source_target_pairs={{0,4},{4,0},{8,12},{12,8},{16,20},{20,16},{24,28},{28,24},{1,5},{5... | collective-permute-start | bytes 786440 | tf_op jit(solution)/shard_map/ppermute | solution.py:40
  55.6 10.2 %collective-permute-start.30 = (f32[256,256]{1,0:T(8,128)S(1)}, f32[256,256]{1,0:T(8,128)S(1)}, u32[]{:S(2)}, u32[]{:S(2)}) collective-permute-start(f32[256,256]{1,0:T(8,128)S(1)} %level1.13.refs_4_.refs_0_), channel_id=1, source_target_pairs={{0,16},{4,20},{8,24},{12,28},{16,0},{20,4},{24,8},{28,12},{1,17},{... | collective-permute-start | bytes 786440 | tf_op jit(solution)/shard_map/ppermute | solution.py:40
  57.7 8.7 %collective-permute-start.29 = (f32[256,256]{1,0:T(8,128)S(1)}, f32[256,256]{1,0:T(8,128)S(1)}, u32[]{:S(2)}, u32[]{:S(2)}) collective-permute-start(f32[256,256]{1,0:T(8,128)S(1)} %level0.14.refs_7_.refs_0_), channel_id=1, source_target_pairs={{0,8},{4,12},{8,0},{12,4},{16,24},{20,28},{24,16},{28,20},{1,9},{5... | collective-permute-start | bytes 786440 | tf_op jit(solution)/shard_map/ppermute | solution.py:40
  61.4 8.4 %collective-permute-start.18 = (f32[256,256]{1,0:T(8,128)S(1)}, f32[256,256]{1,0:T(8,128)S(1)}, u32[]{:S(2)}, u32[]{:S(2)}) collective-permute-start(f32[256,256]{1,0:T(8,128)S(1)} %level1.9.refs_4_.refs_0_), channel_id=1, source_target_pairs={{0,16},{4,20},{8,24},{12,28},{16,0},{20,4},{24,8},{28,12},{1,17},{... | collective-permute-start | bytes 786440 | tf_op jit(solution)/shard_map/ppermute | solution.py:40
  63.3 8.8 %collective-permute-start.17 = (f32[256,256]{1,0:T(8,128)S(1)}, f32[256,256]{1,0:T(8,128)S(1)}, u32[]{:S(2)}, u32[]{:S(2)}) collective-permute-start(f32[256,256]{1,0:T(8,128)S(1)} %level0.10.refs_7_.refs_0_), channel_id=1, source_target_pairs={{0,8},{4,12},{8,0},{12,4},{16,24},{20,28},{24,16},{28,20},{1,9},{5... | collective-permute-start | bytes 786440 | tf_op jit(solution)/shard_map/ppermute | solution.py:40
  66.8 9.2 %collective-permute-start.32 = (f32[256,256]{1,0:T(8,128)S(1)}, f32[256,256]{1,0:T(8,128)S(1)}, u32[]{:S(2)}, u32[]{:S(2)}) collective-permute-start(f32[256,256]{1,0:T(8,128)S(1)} %level1.14.refs_4_.refs_0_), channel_id=1, source_target_pairs={{0,16},{4,20},{8,24},{12,28},{16,0},{20,4},{24,8},{28,12},{1,17},{... | collective-permute-start | bytes 786440 | tf_op jit(solution)/shard_map/ppermute | solution.py:40
  68.7 9.3 %collective-permute-start.31 = (f32[256,256]{1,0:T(8,128)S(1)}, f32[256,256]{1,0:T(8,128)S(1)}, u32[]{:S(2)}, u32[]{:S(2)}) collective-permute-start(f32[256,256]{1,0:T(8,128)S(1)} %level0.15.refs_0_), channel_id=1, source_target_pairs={{0,8},{4,12},{8,0},{12,4},{16,24},{20,28},{24,16},{28,20},{1,9},{5... | collective-permute-start | bytes 786440 | tf_op jit(solution)/shard_map/ppermute | solution.py:40
  72.5 9.3 %collective-permute-start.20 = (f32[256,256]{1,0:T(8,128)S(1)}, f32[256,256]{1,0:T(8,128)S(1)}, u32[]{:S(2)}, u32[]{:S(2)}) collective-permute-start(f32[256,256]{1,0:T(8,128)S(1)} %level1.10.refs_4_.refs_0_), channel_id=1, source_target_pairs={{0,16},{4,20},{8,24},{12,28},{16,0},{20,4},{24,8},{28,12},{1,17},{... | collective-permute-start | bytes 786440 | tf_op jit(solution)/shard_map/ppermute | solution.py:40
  78.4 9.3 %collective-permute-start.33 = (f32[256,256]{1,0:T(8,128)S(1)}, f32[256,256]{1,0:T(8,128)S(1)}, u32[]{:S(2)}, u32[]{:S(2)}) collective-permute-start(f32[256,256]{1,0:T(8,128)S(1)} %level1.15.refs_0_), channel_id=1, source_target_pairs={{0,16},{4,20},{8,24},{12,28},{16,0},{20,4},{24,8},{28,12},{1,17},{... | collective-permute-start | bytes 786440 | tf_op jit(solution)/shard_map/ppermute | solution.py:40
  82.9 9.4 %collective-permute-start.21 = (f32[256,256]{1,0:T(8,128)S(1)}, f32[256,256]{1,0:T(8,128)S(1)}, u32[]{:S(2)}, u32[]{:S(2)}) collective-permute-start(f32[256,256]{1,0:T(8,128)S(1)} %level1.11.refs_0_), channel_id=1, source_target_pairs={{0,16},{4,20},{8,24},{12,28},{16,0},{20,4},{24,8},{28,12},{1,17},{... | collective-permute-start | bytes 786440 | tf_op jit(solution)/shard_map/ppermute | solution.py:40
  (10 other events, 65.8 us)

commit v5 on v4

--- a/solution.py
+++ b/solution.py
@@ -103,6 +103,10 @@
         start += source.shape[0]
     for c in copies:
         c.wait()
+
+
+def token(out):
+    out[...] = jnp.zeros_like(out)
 
 
 def tree_blocks(n, start, rows, *refs):
@@ -222,14 +226,24 @@
         copy.wait()
 
 
-def last_apply(own, far, fh, fl, *refs):
+def own_part(own, fh, fl, out):
+    width = own.shape[0]
+    mine = own[...]
+    out[...] = mine - dot3(fh[:, :width], fl[:, :width], *split(mine))
+
+
+def last_apply(part, far, fh, fl, *refs):
     *sources, _, out, buffer, sems = refs
-    width, size = own.shape
-    copies = store(sources, out, 0, out.shape[1] - (len(sources) + 1) * size, sems)
-    buffer[...] = level_result(0, own, far, fh, fl, size)
-    to = out.at[pl.ds(0, width), pl.ds(out.shape[1] - size, size)]
-    copies.append(pltpu.make_async_copy(buffer, to, sems.at[len(sources)]))
-    copies[-1].start()
+    width, size = part.shape
+    start = out.shape[1] - size
+    copies = store(sources, out, 0, start - len(sources) * size, sems)
+    half = size // 2
+    for k in range(2):
+        at = pl.ds(k * half, half)
+        buffer[:, at] = part[:, at] - dot3(fh[:, width:], fl[:, width:], *split(far[:, at]))
+        to = out.at[pl.ds(0, width), pl.ds(start + k * half, half)]
+        copies.append(pltpu.make_async_copy(buffer.at[:, at], to, sems.at[len(sources) + k]))
+        copies[-1].start()
     for copy in copies:
         copy.wait()
 
@@ -271,6 +285,7 @@
         functools.partial(tree_blocks, len(pieces), vr + tr, tr), "tree_blocks", pieces, [block] * depth + [half], after=[ch]
     )
     odd = swap(odd, "row", 2)
+    (arrived,) = call(token, "arrived", (), [pltpu.VMEM((8, 128), F32)], after=[odd], size=2 * 10**9)
     factors = [
         call(
             functools.partial(level_factors, level, tr),
@@ -278,7 +293,6 @@
             (owns[level], *([even, odd] if level == 1 else [swap(owns[level], "row", 1 << level)])),
             [block16(width, 2 * width)] * 2,
             [block] * (level == 1),
-            size=2 * 10**9 if level == 1 else 1000,
         )
         for level in range(depth)
     ]
@@ -337,7 +351,7 @@
             tops[j], rests[j], fars[j] = top, rest, swap(top, "row", 1)
 
     def first_level(k):
-        waits = made[min(1, depth - 2)][k - 2:k - 1] if k >= 2 else [factors[1][0]]
+        waits = made[min(1, depth - 2)][k - 2:k - 1] if k >= 2 else [arrived] * (1 - k)
         advance(0, tops[k], fars[k], 0, waits)
 
     make_leaf(0)
@@ -363,10 +377,11 @@
     early = [rests[k] for k in range(CHUNKS)] + done[:kept]
     (out,) = call(early_store, "early_store", early, [whole], [sems], hbm_out=(0,))
     late = done[kept:]
+    (mine,) = call(own_part, "own_part", (made[-1][-1], *factors[-1]), [pltpu.VMEM((width, part), F32)])
     (out,) = call(
         last_apply,
         "finish",
-        (made[-1][-1], sent[-1][-1], *factors[-1], *late, out),
+        (mine, sent[-1][-1], *factors[-1], *late, out),
         [whole],
         [pltpu.VMEM((width, part), F32), sems],
         hbm_in=(4 + len(late),),

time: 93.8 us -> 92.7 us (0.988)
  starting transfers between devices: 38.7 us -> 33.3 us
  waiting for transfers between devices: 29.5 us -> 33.6 us
    ppermute x31, starting transfers between devices: 35.5 us -> 30.1 us  [swap(): lax.ppermute(value, axis, [(i, i ^ mask) for i in range(lax.axis_size(axi...]
    ppermute x31, waiting for transfers between devices: 27.9 us -> 32 us  [swap(): lax.ppermute(value, axis, [(i, i ^ mask) for i in range(lax.axis_size(axi...]
    pallas_call x41 -> x43, Pallas kernels: 24.8 us -> 25 us  [call(): pl.pallas_call(body, out_shape=[jax.ShapeDtypeStruct(o.shape, o.dtype) if...]
  transfers between devices with their start and end apart: 34 -> 34, of which waited for: 17 -> 18; matrix products, arithmetic and copies ran while one was open for 0% -> 0% of each run, Pallas kernels for 24% -> 24%
where the time goes in v5:
time: 92.7 us; the launch traced here: 92.5 us
  waiting for transfers between devices  33.6 us (36%)
  starting transfers between devices  33.3 us (36%)
  Pallas kernels  25 us (27%)
    ppermute x31, waiting for transfers between devices, swap(): lax.ppermute(value, axis, [(i, i ^ mask) for i in range(lax.axis_size(axi...  32 us
    ppermute x31, starting transfers between devices, swap(): lax.ppermute(value, axis, [(i, i ^ mask) for i in range(lax.axis_size(axi...  30.1 us
    pallas_call x43, Pallas kernels, call(): pl.pallas_call(body, out_shape=[jax.ShapeDtypeStruct(o.shape, o.dtype) if...  25 us
    ppermute x2, starting transfers between devices, spread(): ends = [lax.ppermute(second, axis, [(1, 0), (2, 3)]) for second in seconds]  2.56 us
  transfers between devices with their start and end apart: 34, of which 18 were waited for; matrix products, arithmetic and copies ran while one was open for 0% of the time, Pallas kernels for 24%

profile of v5, /device:TPU:0, one launch (start us, length us, event | category | flops | bytes accessed | tf_op | source)
XLA Modules:
  0.0 92.5 jit_solution(9548357226593070895)
XLA Ops:
  1.2 4.1 %collective-permute-start = (f32[320,128]{1,0:T(8,128)S(1)}, f32[320,128]{1,0:T(8,128)S(1)}, u32[]{:S(2)}, u32[]{:S(2)}) collective-permute-start(f32[320,128]{1,0:T(8,128)S(1)} %get-tuple-element.43), channel_id=1, source_target_pairs={{0,2},{1,3},{2,0},{3,1},{4,6},{5,7},{6,4},{7,5},{8,10},{9,11},{10,... | collective-permute-start | bytes 491528 | tf_op jit(solution)/shard_map/ppermute | solution.py:40
  5.4 1.8 %collective-permute-start.2 = (f32[320,256]{1,0:T(8,128)S(1)}, f32[320,256]{1,0:T(8,128)S(1)}, u32[]{:S(2)}, u32[]{:S(2)}) collective-permute-start(f32[320,256]{1,0:T(8,128)S(1)} %get-tuple-element.48.refs_0_), channel_id=1, source_target_pairs={{0,1},{1,0},{2,3},{3,2},{4,5},{5,4},{6,7},{7,6},{8,9},{9,8},{10,11... | collective-permute-start | bytes 983048 | tf_op jit(solution)/shard_map/ppermute | solution.py:40
  7.9 9.6 %collective-permute-done.refs_1_.refs_3_ = f32[320,128]{1,0:T(8,128)S(1)} collective-permute-done((f32[320,128]{1,0:T(8,128)S(1)}, f32[320,128]{1,0:T(8,128)S(1)}, u32[]{:S(2)}, u32[]{:S(2)}) %collective-permute-start) | collective-permute-done | bytes 163872 | tf_op jit(solution)/shard_map/ppermute | solution.py:40
  18.7 2.2 %collective-permute-done.1.refs_2_.refs_4_ = f32[320,128]{1,0:T(8,128)S(1)} collective-permute-done((f32[320,128]{1,0:T(8,128)S(1)}, f32[320,128]{1,0:T(8,128)S(1)}, u32[]{:S(2)}, u32[]{:S(2)}) %collective-permute-start.1) | collective-permute-done | bytes 163872 | tf_op jit(solution)/shard_map/ppermute | solution.py:40
  22.2 1.9 %collective-permute-start.6 = (f32[128,256]{1,0:T(8,128)S(1)}, f32[128,256]{1,0:T(8,128)S(1)}, u32[]{:S(2)}, u32[]{:S(2)}) collective-permute-start(f32[128,256]{1,0:T(8,128)S(1)} %even_rows.1), channel_id=1, source_target_pairs={{0,8},{4,12},{8,0},{12,4},{16,24},{20,28},{24,16},{28,20},{1,9},{5... | collective-permute-start | bytes 393224 | tf_op jit(solution)/shard_map/ppermute | solution.py:40
  24.1 2.4 %load.1 = (f32[512,2048]{1,0:T(8,128)S(1)}, bf16[512,2048]{1,0:T(8,128)(2,1)S(1)}, bf16[512,2048]{1,0:T(8,128)(2,1)S(1)}) custom-call(f32[512,2048]{1,0:T(8,128)} %refs_0_.3, f32[320,128]{1,0:T(8,128)S(1)} %collective-permute-done.refs_1_.refs_3_, f32[320,128]{1,0:T(8,128)S(1)} %collective-permute-done.1.refs_2_.refs_4_), custom_call_target="tpu_custom_call" | custom-call | flops 1000 | bytes 1000 | tf_op jit(solution)/shard_map/load/pallas_call | solution.py:26
  26.6 1.6 %collective-permute-done.5.refs_6_ = f32[320,128]{1,0:T(8,128)S(1)} collective-permute-done((f32[320,128]{1,0:T(8,128)S(1)}, f32[320,128]{1,0:T(8,128)S(1)}, u32[]{:S(2)}, u32[]{:S(2)}) %collective-permute-start.5) | collective-permute-done | bytes 163872 | tf_op jit(solution)/shard_map/ppermute | solution.py:50
  28.3 1.9 %collective-permute-start.12 = (f32[128,256]{1,0:T(8,128)S(1)}, f32[128,256]{1,0:T(8,128)S(1)}, u32[]{:S(2)}, u32[]{:S(2)}) collective-permute-start(f32[128,256]{1,0:T(8,128)S(1)} %get-tuple-element.61), channel_id=1, source_target_pairs={{0,8},{4,12},{8,0},{12,4},{16,24},{20,28},{24,16},{28,20},{1,9},{5... | collective-permute-start | bytes 393224 | tf_op jit(solution)/shard_map/ppermute | solution.py:40
  34.1 1.9 %collective-permute-start.25 = (f32[256,256]{1,0:T(8,128)S(1)}, f32[256,256]{1,0:T(8,128)S(1)}, u32[]{:S(2)}, u32[]{:S(2)}) collective-permute-start(f32[256,256]{1,0:T(8,128)S(1)} %level0.12.refs_7_.refs_0_), channel_id=1, source_target_pairs={{0,8},{4,12},{8,0},{12,4},{16,24},{20,28},{24,16},{28,20},{1,9},{5... | collective-permute-start | bytes 786440 | tf_op jit(solution)/shard_map/ppermute | solution.py:40
  36.0 1.5 %leaf_2.1 = (f32[256,256]{1,0:T(8,128)S(1)}, f32[256,256]{1,0:T(8,128)S(1)}, f32[256,256]{1,0:T(8,128)S(1)}, f32[256,256]{1,0:T(8,128)S(1)}) custom-call(f32[512,2048]{1,0:T(8,128)S(1)} %get-tuple-element.45.refs_0_, bf16[512,2048]{1,0:T(8,128)(2,1)S(1)} %get-tuple-element.46.refs_1_.refs_7_, bf16[512,2048]{1,0:T(8,128)(2,1)S(1)} %get-tuple-element.47.refs_2_, ...), custom_call_target="tpu_custom_call" | custom-call | flops 1000 | bytes 1000 | tf_op jit(solution)/shard_map/leaf_2/pallas_call | solution.py:26
  37.5 1.6 %collective-permute-start.13 = (f32[256,256]{1,0:T(8,128)S(1)}, f32[256,256]{1,0:T(8,128)S(1)}, u32[]{:S(2)}, u32[]{:S(2)}) collective-permute-start(f32[256,256]{1,0:T(8,128)S(1)} %get-tuple-element.64.refs_0_), channel_id=1, source_target_pairs={{0,16},{4,20},{8,24},{12,28},{16,0},{20,4},{24,8},{28,12},{1,17},{... | collective-permute-start | bytes 786440 | tf_op jit(solution)/shard_map/ppermute | solution.py:40
  40.8 1.5 %leaf_3.1 = (f32[256,256]{1,0:T(8,128)S(1)}, f32[256,256]{1,0:T(8,128)S(1)}, f32[256,256]{1,0:T(8,128)S(1)}, f32[256,256]{1,0:T(8,128)S(1)}) custom-call(f32[512,2048]{1,0:T(8,128)S(1)} %get-tuple-element.45.refs_0_, bf16[512,2048]{1,0:T(8,128)(2,1)S(1)} %get-tuple-element.46.refs_1_.refs_7_, bf16[512,2048]{1,0:T(8,128)(2,1)S(1)} %get-tuple-element.47.refs_2_, ...), custom_call_target="tpu_custom_call" | custom-call | flops 1000 | bytes 1000 | tf_op jit(solution)/shard_map/leaf_3/pallas_call | solution.py:26
  43.1 2.5 %collective-permute-start.27 = (f32[256,256]{1,0:T(8,128)S(1)}, f32[256,256]{1,0:T(8,128)S(1)}, u32[]{:S(2)}, u32[]{:S(2)}) collective-permute-start(f32[256,256]{1,0:T(8,128)S(1)} %level1.12.refs_4_.refs_0_), channel_id=1, source_target_pairs={{0,16},{4,20},{8,24},{12,28},{16,0},{20,4},{24,8},{28,12},{1,17},{... | collective-permute-start | bytes 786440 | tf_op jit(solution)/shard_map/ppermute | solution.py:40
  47.1 2.0 %collective-permute-done.11.refs_1_ = f32[256,256]{1,0:T(8,128)S(1)} collective-permute-done((f32[256,256]{1,0:T(8,128)S(1)}, f32[256,256]{1,0:T(8,128)S(1)}, u32[]{:S(2)}, u32[]{:S(2)}) %collective-permute-start.11) | collective-permute-done | bytes 262176 | tf_op jit(solution)/shard_map/ppermute | solution.py:40
  49.5 1.7 %collective-permute-start.15 = (f32[256,256]{1,0:T(8,128)S(1)}, f32[256,256]{1,0:T(8,128)S(1)}, u32[]{:S(2)}, u32[]{:S(2)}) collective-permute-start(f32[256,256]{1,0:T(8,128)S(1)} %level1.8.refs_4_.refs_0_), channel_id=1, source_target_pairs={{0,16},{4,20},{8,24},{12,28},{16,0},{20,4},{24,8},{28,12},{1,17},{... | collective-permute-start | bytes 786440 | tf_op jit(solution)/shard_map/ppermute | solution.py:40
  53.2 1.9 %collective-permute-done.26.refs_1_ = f32[256,256]{1,0:T(8,128)S(1)} collective-permute-done((f32[256,256]{1,0:T(8,128)S(1)}, f32[256,256]{1,0:T(8,128)S(1)}, u32[]{:S(2)}, u32[]{:S(2)}) %collective-permute-start.26) | collective-permute-done | bytes 262176 | tf_op jit(solution)/shard_map/ppermute | solution.py:40
  59.4 1.5 %collective-permute-done.14.refs_1_ = f32[256,256]{1,0:T(8,128)S(1)} collective-permute-done((f32[256,256]{1,0:T(8,128)S(1)}, f32[256,256]{1,0:T(8,128)S(1)}, u32[]{:S(2)}, u32[]{:S(2)}) %collective-permute-start.14) | collective-permute-done | bytes 262176 | tf_op jit(solution)/shard_map/ppermute | solution.py:40
  69.2 2.7 %collective-permute-done.17.refs_1_ = f32[256,256]{1,0:T(8,128)S(1)} collective-permute-done((f32[256,256]{1,0:T(8,128)S(1)}, f32[256,256]{1,0:T(8,128)S(1)}, u32[]{:S(2)}, u32[]{:S(2)}) %collective-permute-start.17) | collective-permute-done | bytes 262176 | tf_op jit(solution)/shard_map/ppermute | solution.py:40
  74.3 1.5 %collective-permute-done.32.refs_1_ = f32[256,256]{1,0:T(8,128)S(1)} collective-permute-done((f32[256,256]{1,0:T(8,128)S(1)}, f32[256,256]{1,0:T(8,128)S(1)}, u32[]{:S(2)}, u32[]{:S(2)}) %collective-permute-start.32) | collective-permute-done | bytes 262176 | tf_op jit(solution)/shard_map/ppermute | solution.py:40
  76.2 1.7 %collective-permute-done.31.refs_1_ = f32[256,256]{1,0:T(8,128)S(1)} collective-permute-done((f32[256,256]{1,0:T(8,128)S(1)}, f32[256,256]{1,0:T(8,128)S(1)}, u32[]{:S(2)}, u32[]{:S(2)}) %collective-permute-start.31) | collective-permute-done | bytes 262176 | tf_op jit(solution)/shard_map/ppermute | solution.py:40
  79.3 2.0 %collective-permute-done.20.refs_1_ = f32[256,256]{1,0:T(8,128)S(1)} collective-permute-done((f32[256,256]{1,0:T(8,128)S(1)}, f32[256,256]{1,0:T(8,128)S(1)}, u32[]{:S(2)}, u32[]{:S(2)}) %collective-permute-start.20) | collective-permute-done | bytes 262176 | tf_op jit(solution)/shard_map/ppermute | solution.py:40
  82.5 1.6 %collective-permute-start.21 = (f32[256,256]{1,0:T(8,128)S(1)}, f32[256,256]{1,0:T(8,128)S(1)}, u32[]{:S(2)}, u32[]{:S(2)}) collective-permute-start(f32[256,256]{1,0:T(8,128)S(1)} %level1.11.refs_0_), channel_id=1, source_target_pairs={{0,16},{4,20},{8,24},{12,28},{16,0},{20,4},{24,8},{28,12},{1,17},{... | collective-permute-start | bytes 786440 | tf_op jit(solution)/shard_map/ppermute | solution.py:40
  84.9 1.9 %early_store.1.refs_6_ = f32[512,2048]{1,0:T(8,128)} custom-call(f32[256,256]{1,0:T(8,128)S(1)} %rest_0.1.refs_0_, f32[256,256]{1,0:T(8,128)S(1)} %rest_1.1.refs_1_, f32[256,256]{1,0:T(8,128)S(1)} %get-tuple-element.75.refs_2_, f32[256,256]{1,0:T(8,128)S(1)} %get-tuple-element.76.refs_3_, f32[256,256]{1,0:T(8,128)S(1)} %get-tuple-element.77.refs_4_, ...), custom_call_target="tpu_custom_call" | custom-call | flops 1000 | bytes 1000 | tf_op jit(solution)/shard_map/early_store/pallas_call | solution.py:26
  87.4 3.8 %collective-permute-done.21.refs_1_ = f32[256,256]{1,0:T(8,128)S(1)} collective-permute-done((f32[256,256]{1,0:T(8,128)S(1)}, f32[256,256]{1,0:T(8,128)S(1)}, u32[]{:S(2)}, u32[]{:S(2)}) %collective-permute-start.21) | collective-permute-done | bytes 262176 | tf_op jit(solution)/shard_map/ppermute | solution.py:40
  (87 shorter events, 35.3 us)
Async XLA Ops:
  1.2 16.3 %collective-permute-start = (f32[320,128]{1,0:T(8,128)S(1)}, f32[320,128]{1,0:T(8,128)S(1)}, u32[]{:S(2)}, u32[]{:S(2)}) collective-permute-start(f32[320,128]{1,0:T(8,128)S(1)} %get-tuple-element.43), channel_id=1, source_target_pairs={{0,2},{1,3},{2,0},{3,1},{4,6},{5,7},{6,4},{7,5},{8,10},{9,11},{10,... | collective-permute-start | bytes 491528 | tf_op jit(solution)/shard_map/ppermute | solution.py:40
  5.3 15.6 %collective-permute-start.1 = (f32[320,128]{1,0:T(8,128)S(1)}, f32[320,128]{1,0:T(8,128)S(1)}, u32[]{:S(2)}, u32[]{:S(2)}) collective-permute-start(f32[320,128]{1,0:T(8,128)S(1)} %get-tuple-element.44), channel_id=1, source_target_pairs={{0,2},{1,3},{2,0},{3,1},{4,6},{5,7},{6,4},{7,5},{8,10},{9,11},{10,... | collective-permute-start | bytes 491528 | tf_op jit(solution)/shard_map/ppermute | solution.py:40
  5.4 22.8 %collective-permute-start.2 = (f32[320,256]{1,0:T(8,128)S(1)}, f32[320,256]{1,0:T(8,128)S(1)}, u32[]{:S(2)}, u32[]{:S(2)}) collective-permute-start(f32[320,256]{1,0:T(8,128)S(1)} %get-tuple-element.48.refs_0_), channel_id=1, source_target_pairs={{0,1},{1,0},{2,3},{3,2},{4,5},{5,4},{6,7},{7,6},{8,9},{9,8},{10,11... | collective-permute-start | bytes 983048 | tf_op jit(solution)/shard_map/ppermute | solution.py:40
  7.2 21.0 %collective-permute-start.3 = (f32[320,256]{1,0:T(8,128)S(1)}, f32[320,256]{1,0:T(8,128)S(1)}, u32[]{:S(2)}, u32[]{:S(2)}) collective-permute-start(f32[320,256]{1,0:T(8,128)S(1)} %get-tuple-element.48.refs_0_), channel_id=1, source_target_pairs={{1,2},{2,1},{5,6},{6,5},{9,10},{10,9},{13,14},{14,13},{17,18},{18,... | collective-permute-start | bytes 983048 | tf_op jit(solution)/shard_map/ppermute | solution.py:49
  17.5 9.1 %collective-permute-start.4 = (f32[320,128]{1,0:T(8,128)S(1)}, f32[320,128]{1,0:T(8,128)S(1)}, u32[]{:S(2)}, u32[]{:S(2)}) collective-permute-start(f32[320,128]{1,0:T(8,128)S(1)} %collective-permute-done.refs_1_.refs_3_), channel_id=1, source_target_pairs={{1,0},{2,3},{5,4},{6,7},{9,8},{10,11},{13,12},{14,15},{17,16},{18,... | collective-permute-start | bytes 491528 | tf_op jit(solution)/shard_map/ppermute | solution.py:50
  37.5 9.1 %collective-permute-start.13 = (f32[256,256]{1,0:T(8,128)S(1)}, f32[256,256]{1,0:T(8,128)S(1)}, u32[]{:S(2)}, u32[]{:S(2)}) collective-permute-start(f32[256,256]{1,0:T(8,128)S(1)} %get-tuple-element.64.refs_0_), channel_id=1, source_target_pairs={{0,16},{4,20},{8,24},{12,28},{16,0},{20,4},{24,8},{28,12},{1,17},{... | collective-permute-start | bytes 786440 | tf_op jit(solution)/shard_map/ppermute | solution.py:40
  39.9 9.2 %collective-permute-start.11 = (f32[256,256]{1,0:T(8,128)S(1)}, f32[256,256]{1,0:T(8,128)S(1)}, u32[]{:S(2)}, u32[]{:S(2)}) collective-permute-start(f32[256,256]{1,0:T(8,128)S(1)} %level0.8.refs_7_.refs_0_.refs_4_), channel_id=1, source_target_pairs={{0,8},{4,12},{8,0},{12,4},{16,24},{20,28},{24,16},{28,20},{1,9},{5... | collective-permute-start | bytes 786440 | tf_op jit(solution)/shard_map/ppermute | solution.py:40
  42.3 8.9 %collective-permute-start.10 = (f32[256,256]{1,0:T(8,128)S(1)}, f32[256,256]{1,0:T(8,128)S(1)}, u32[]{:S(2)}, u32[]{:S(2)}) collective-permute-start(f32[256,256]{1,0:T(8,128)S(1)} %get-tuple-element.59.refs_0_), channel_id=1, source_target_pairs={{0,4},{4,0},{8,12},{12,8},{16,20},{20,16},{24,28},{28,24},{1,5},{5... | collective-permute-start | bytes 786440 | tf_op jit(solution)/shard_map/ppermute | solution.py:40
  43.1 9.7 %collective-permute-start.27 = (f32[256,256]{1,0:T(8,128)S(1)}, f32[256,256]{1,0:T(8,128)S(1)}, u32[]{:S(2)}, u32[]{:S(2)}) collective-permute-start(f32[256,256]{1,0:T(8,128)S(1)} %level1.12.refs_4_.refs_0_), channel_id=1, source_target_pairs={{0,16},{4,20},{8,24},{12,28},{16,0},{20,4},{24,8},{28,12},{1,17},{... | collective-permute-start | bytes 786440 | tf_op jit(solution)/shard_map/ppermute | solution.py:40
  46.0 9.0 %collective-permute-start.26 = (f32[256,256]{1,0:T(8,128)S(1)}, f32[256,256]{1,0:T(8,128)S(1)}, u32[]{:S(2)}, u32[]{:S(2)}) collective-permute-start(f32[256,256]{1,0:T(8,128)S(1)} %level0.13.refs_0_), channel_id=1, source_target_pairs={{0,8},{4,12},{8,0},{12,4},{16,24},{20,28},{24,16},{28,20},{1,9},{5... | collective-permute-start | bytes 786440 | tf_op jit(solution)/shard_map/ppermute | solution.py:40
  46.6 10.3 %collective-permute-start.23 = (f32[256,256]{1,0:T(8,128)S(1)}, f32[256,256]{1,0:T(8,128)S(1)}, u32[]{:S(2)}, u32[]{:S(2)}) collective-permute-start(f32[256,256]{1,0:T(8,128)S(1)} %get-tuple-element.68.refs_0_), channel_id=1, source_target_pairs={{0,4},{4,0},{8,12},{12,8},{16,20},{20,16},{24,28},{28,24},{1,5},{5... | collective-permute-start | bytes 786440 | tf_op jit(solution)/shard_map/ppermute | solution.py:40
  49.5 9.4 %collective-permute-start.15 = (f32[256,256]{1,0:T(8,128)S(1)}, f32[256,256]{1,0:T(8,128)S(1)}, u32[]{:S(2)}, u32[]{:S(2)}) collective-permute-start(f32[256,256]{1,0:T(8,128)S(1)} %level1.8.refs_4_.refs_0_), channel_id=1, source_target_pairs={{0,16},{4,20},{8,24},{12,28},{16,0},{20,4},{24,8},{28,12},{1,17},{... | collective-permute-start | bytes 786440 | tf_op jit(solution)/shard_map/ppermute | solution.py:40
  51.7 9.2 %collective-permute-start.14 = (f32[256,256]{1,0:T(8,128)S(1)}, f32[256,256]{1,0:T(8,128)S(1)}, u32[]{:S(2)}, u32[]{:S(2)}) collective-permute-start(f32[256,256]{1,0:T(8,128)S(1)} %level0.9.refs_0_), channel_id=1, source_target_pairs={{0,8},{4,12},{8,0},{12,4},{16,24},{20,28},{24,16},{28,20},{1,9},{5... | collective-permute-start | bytes 786440 | tf_op jit(solution)/shard_map/ppermute | solution.py:40
  52.8 9.7 %collective-permute-start.9 = (f32[256,256]{1,0:T(8,128)S(1)}, f32[256,256]{1,0:T(8,128)S(1)}, u32[]{:S(2)}, u32[]{:S(2)}) collective-permute-start(f32[256,256]{1,0:T(8,128)S(1)} %get-tuple-element.58.refs_0_), channel_id=1, source_target_pairs={{0,4},{4,0},{8,12},{12,8},{16,20},{20,16},{24,28},{28,24},{1,5},{5... | collective-permute-start | bytes 786440 | tf_op jit(solution)/shard_map/ppermute | solution.py:40
  55.5 9.1 %collective-permute-start.30 = (f32[256,256]{1,0:T(8,128)S(1)}, f32[256,256]{1,0:T(8,128)S(1)}, u32[]{:S(2)}, u32[]{:S(2)}) collective-permute-start(f32[256,256]{1,0:T(8,128)S(1)} %level1.13.refs_4_.refs_0_), channel_id=1, source_target_pairs={{0,16},{4,20},{8,24},{12,28},{16,0},{20,4},{24,8},{28,12},{1,17},{... | collective-permute-start | bytes 786440 | tf_op jit(solution)/shard_map/ppermute | solution.py:40
  57.3 9.0 %collective-permute-start.29 = (f32[256,256]{1,0:T(8,128)S(1)}, f32[256,256]{1,0:T(8,128)S(1)}, u32[]{:S(2)}, u32[]{:S(2)}) collective-permute-start(f32[256,256]{1,0:T(8,128)S(1)} %level0.14.refs_7_.refs_0_), channel_id=1, source_target_pairs={{0,8},{4,12},{8,0},{12,4},{16,24},{20,28},{24,16},{28,20},{1,9},{5... | collective-permute-start | bytes 786440 | tf_op jit(solution)/shard_map/ppermute | solution.py:40
  58.9 9.2 %collective-permute-start.28 = (f32[256,256]{1,0:T(8,128)S(1)}, f32[256,256]{1,0:T(8,128)S(1)}, u32[]{:S(2)}, u32[]{:S(2)}) collective-permute-start(f32[256,256]{1,0:T(8,128)S(1)} %get-tuple-element.70.refs_0_), channel_id=1, source_target_pairs={{0,4},{4,0},{8,12},{12,8},{16,20},{20,16},{24,28},{28,24},{1,5},{5... | collective-permute-start | bytes 786440 | tf_op jit(solution)/shard_map/ppermute | solution.py:40
  62.9 9.0 %collective-permute-start.17 = (f32[256,256]{1,0:T(8,128)S(1)}, f32[256,256]{1,0:T(8,128)S(1)}, u32[]{:S(2)}, u32[]{:S(2)}) collective-permute-start(f32[256,256]{1,0:T(8,128)S(1)} %level0.10.refs_7_.refs_0_), channel_id=1, source_target_pairs={{0,8},{4,12},{8,0},{12,4},{16,24},{20,28},{24,16},{28,20},{1,9},{5... | collective-permute-start | bytes 786440 | tf_op jit(solution)/shard_map/ppermute | solution.py:40
  64.5 9.2 %collective-permute-start.16 = (f32[256,256]{1,0:T(8,128)S(1)}, f32[256,256]{1,0:T(8,128)S(1)}, u32[]{:S(2)}, u32[]{:S(2)}) collective-permute-start(f32[256,256]{1,0:T(8,128)S(1)} %get-tuple-element.67.refs_0_), channel_id=1, source_target_pairs={{0,4},{4,0},{8,12},{12,8},{16,20},{20,16},{24,28},{28,24},{1,5},{5... | collective-permute-start | bytes 786440 | tf_op jit(solution)/shard_map/ppermute | solution.py:40
  66.7 9.1 %collective-permute-start.32 = (f32[256,256]{1,0:T(8,128)S(1)}, f32[256,256]{1,0:T(8,128)S(1)}, u32[]{:S(2)}, u32[]{:S(2)}) collective-permute-start(f32[256,256]{1,0:T(8,128)S(1)} %level1.14.refs_4_.refs_0_), channel_id=1, source_target_pairs={{0,16},{4,20},{8,24},{12,28},{16,0},{20,4},{24,8},{28,12},{1,17},{... | collective-permute-start | bytes 786440 | tf_op jit(solution)/shard_map/ppermute | solution.py:40
  68.5 9.3 %collective-permute-start.31 = (f32[256,256]{1,0:T(8,128)S(1)}, f32[256,256]{1,0:T(8,128)S(1)}, u32[]{:S(2)}, u32[]{:S(2)}) collective-permute-start(f32[256,256]{1,0:T(8,128)S(1)} %level0.15.refs_0_), channel_id=1, source_target_pairs={{0,8},{4,12},{8,0},{12,4},{16,24},{20,28},{24,16},{28,20},{1,9},{5... | collective-permute-start | bytes 786440 | tf_op jit(solution)/shard_map/ppermute | solution.py:40
  72.3 9.1 %collective-permute-start.20 = (f32[256,256]{1,0:T(8,128)S(1)}, f32[256,256]{1,0:T(8,128)S(1)}, u32[]{:S(2)}, u32[]{:S(2)}) collective-permute-start(f32[256,256]{1,0:T(8,128)S(1)} %level1.10.refs_4_.refs_0_), channel_id=1, source_target_pairs={{0,16},{4,20},{8,24},{12,28},{16,0},{20,4},{24,8},{28,12},{1,17},{... | collective-permute-start | bytes 786440 | tf_op jit(solution)/shard_map/ppermute | solution.py:40
  78.2 8.8 %collective-permute-start.33 = (f32[256,256]{1,0:T(8,128)S(1)}, f32[256,256]{1,0:T(8,128)S(1)}, u32[]{:S(2)}, u32[]{:S(2)}) collective-permute-start(f32[256,256]{1,0:T(8,128)S(1)} %level1.15.refs_0_), channel_id=1, source_target_pairs={{0,16},{4,20},{8,24},{12,28},{16,0},{20,4},{24,8},{28,12},{1,17},{... | collective-permute-start | bytes 786440 | tf_op jit(solution)/shard_map/ppermute | solution.py:40
  82.5 8.7 %collective-permute-start.21 = (f32[256,256]{1,0:T(8,128)S(1)}, f32[256,256]{1,0:T(8,128)S(1)}, u32[]{:S(2)}, u32[]{:S(2)}) collective-permute-start(f32[256,256]{1,0:T(8,128)S(1)} %level1.11.refs_0_), channel_id=1, source_target_pairs={{0,16},{4,20},{8,24},{12,28},{16,0},{20,4},{24,8},{28,12},{1,17},{... | collective-permute-start | bytes 786440 | tf_op jit(solution)/shard_map/ppermute | solution.py:40
  (10 other events, 64.6 us)

commit v6 on v5

--- a/solution.py
+++ b/solution.py
@@ -282,7 +282,7 @@
         after=pieces[3:5],
     )
     *owns, odd = call(
-        functools.partial(tree_blocks, len(pieces), vr + tr, tr), "tree_blocks", pieces, [block] * depth + [half], after=[ch]
+        functools.partial(tree_blocks, len(pieces), vr + tr, tr), "tree_blocks", pieces, [block] * depth + [half], after=[ch, even]
     )
     odd = swap(odd, "row", 2)
     (arrived,) = call(token, "arrived", (), [pltpu.VMEM((8, 128), F32)], after=[odd], size=2 * 10**9)
@@ -341,7 +341,7 @@
             f"leaf_{k}",
             (c, ch, cl, vth, vtl, ph, plo),
             [above, *([block16(width, part)] * 2 if k < 2 else [below])] * len(ks),
-            after=[tops[0]] if k == 1 else made[0][k - 2:k - 1] if k else (),
+            after=[tops[0], factors[0][0]] if k == 1 else made[0][k - 2:k - 1] if k else (),
         )
         if k < 2:
             outs = (outs[0], *call(

time: 92.7 us -> 94.2 us (1.016)
  starting transfers between devices: 33.3 us -> 42.2 us
  waiting for transfers between devices: 33.6 us -> 26.2 us
    ppermute x31, starting transfers between devices: 30.1 us -> 39 us  [swap(): lax.ppermute(value, axis, [(i, i ^ mask) for i in range(lax.axis_size(axi...]
    ppermute x31, waiting for transfers between devices: 32 us -> 25.3 us  [swap(): lax.ppermute(value, axis, [(i, i ^ mask) for i in range(lax.axis_size(axi...]
  transfers between devices with their start and end apart: 34 -> 34, of which waited for: 18 -> 13; matrix products, arithmetic and copies ran while one was open for 0% -> 0% of each run, Pallas kernels for 24% -> 24%
where the time goes in v6:
time: 94.2 us; the launch traced here: 94 us
  starting transfers between devices  42.2 us (45%)
  waiting for transfers between devices  26.2 us (28%)
  Pallas kernels  25 us (27%)
    ppermute x31, starting transfers between devices, swap(): lax.ppermute(value, axis, [(i, i ^ mask) for i in range(lax.axis_size(axi...  39 us
    ppermute x31, waiting for transfers between devices, swap(): lax.ppermute(value, axis, [(i, i ^ mask) for i in range(lax.axis_size(axi...  25.3 us
    pallas_call x43, Pallas kernels, call(): pl.pallas_call(body, out_shape=[jax.ShapeDtypeStruct(o.shape, o.dtype) if...  25 us
    ppermute x2, starting transfers between devices, spread(): ends = [lax.ppermute(second, axis, [(1, 0), (2, 3)]) for second in seconds]  2.56 us
  transfers between devices with their start and end apart: 34, of which 13 were waited for; matrix products, arithmetic and copies ran while one was open for 0% of the time, Pallas kernels for 24%

profile of v6, /device:TPU:0, one launch (start us, length us, event | category | flops | bytes accessed | tf_op | source)
XLA Modules:
  0.0 94.0 jit_solution(1886368540234132030)
XLA Ops:
  1.2 4.1 %collective-permute-start = (f32[320,128]{1,0:T(8,128)S(1)}, f32[320,128]{1,0:T(8,128)S(1)}, u32[]{:S(2)}, u32[]{:S(2)}) collective-permute-start(f32[320,128]{1,0:T(8,128)S(1)} %get-tuple-element.43), channel_id=1, source_target_pairs={{0,2},{1,3},{2,0},{3,1},{4,6},{5,7},{6,4},{7,5},{8,10},{9,11},{10,... | collective-permute-start | bytes 491528 | tf_op jit(solution)/shard_map/ppermute | solution.py:40
  5.4 1.8 %collective-permute-start.2 = (f32[320,256]{1,0:T(8,128)S(1)}, f32[320,256]{1,0:T(8,128)S(1)}, u32[]{:S(2)}, u32[]{:S(2)}) collective-permute-start(f32[320,256]{1,0:T(8,128)S(1)} %get-tuple-element.48.refs_0_), channel_id=1, source_target_pairs={{0,1},{1,0},{2,3},{3,2},{4,5},{5,4},{6,7},{7,6},{8,9},{9,8},{10,11... | collective-permute-start | bytes 983048 | tf_op jit(solution)/shard_map/ppermute | solution.py:40
  7.9 9.6 %collective-permute-done.refs_1_.refs_3_ = f32[320,128]{1,0:T(8,128)S(1)} collective-permute-done((f32[320,128]{1,0:T(8,128)S(1)}, f32[320,128]{1,0:T(8,128)S(1)}, u32[]{:S(2)}, u32[]{:S(2)}) %collective-permute-start) | collective-permute-done | bytes 163872 | tf_op jit(solution)/shard_map/ppermute | solution.py:40
  17.5 1.3 %collective-permute-start.4 = (f32[320,128]{1,0:T(8,128)S(1)}, f32[320,128]{1,0:T(8,128)S(1)}, u32[]{:S(2)}, u32[]{:S(2)}) collective-permute-start(f32[320,128]{1,0:T(8,128)S(1)} %collective-permute-done.refs_1_.refs_3_), channel_id=1, source_target_pairs={{1,0},{2,3},{5,4},{6,7},{9,8},{10,11},{13,12},{14,15},{17,16},{18,... | collective-permute-start | bytes 491528 | tf_op jit(solution)/shard_map/ppermute | solution.py:50
  18.7 2.2 %collective-permute-done.1.refs_2_.refs_4_ = f32[320,128]{1,0:T(8,128)S(1)} collective-permute-done((f32[320,128]{1,0:T(8,128)S(1)}, f32[320,128]{1,0:T(8,128)S(1)}, u32[]{:S(2)}, u32[]{:S(2)}) %collective-permute-start.1) | collective-permute-done | bytes 163872 | tf_op jit(solution)/shard_map/ppermute | solution.py:40
  20.9 1.3 %collective-permute-start.5 = (f32[320,128]{1,0:T(8,128)S(1)}, f32[320,128]{1,0:T(8,128)S(1)}, u32[]{:S(2)}, u32[]{:S(2)}) collective-permute-start(f32[320,128]{1,0:T(8,128)S(1)} %collective-permute-done.1.refs_2_.refs_4_), channel_id=1, source_target_pairs={{1,0},{2,3},{5,4},{6,7},{9,8},{10,11},{13,12},{14,15},{17,16},{18,... | collective-permute-start | bytes 491528 | tf_op jit(solution)/shard_map/ppermute | solution.py:50
  22.2 1.9 %collective-permute-start.6 = (f32[128,256]{1,0:T(8,128)S(1)}, f32[128,256]{1,0:T(8,128)S(1)}, u32[]{:S(2)}, u32[]{:S(2)}) collective-permute-start(f32[128,256]{1,0:T(8,128)S(1)} %even_rows.1), channel_id=1, source_target_pairs={{0,8},{4,12},{8,0},{12,4},{16,24},{20,28},{24,16},{28,20},{1,9},{5... | collective-permute-start | bytes 393224 | tf_op jit(solution)/shard_map/ppermute | solution.py:40
  24.1 2.4 %load.1 = (f32[512,2048]{1,0:T(8,128)S(1)}, bf16[512,2048]{1,0:T(8,128)(2,1)S(1)}, bf16[512,2048]{1,0:T(8,128)(2,1)S(1)}) custom-call(f32[512,2048]{1,0:T(8,128)} %refs_0_.3, f32[320,128]{1,0:T(8,128)S(1)} %collective-permute-done.refs_1_.refs_3_, f32[320,128]{1,0:T(8,128)S(1)} %collective-permute-done.1.refs_2_.refs_4_), custom_call_target="tpu_custom_call" | custom-call | flops 1000 | bytes 1000 | tf_op jit(solution)/shard_map/load/pallas_call | solution.py:26
  28.3 1.9 %collective-permute-start.12 = (f32[128,256]{1,0:T(8,128)S(1)}, f32[128,256]{1,0:T(8,128)S(1)}, u32[]{:S(2)}, u32[]{:S(2)}) collective-permute-start(f32[128,256]{1,0:T(8,128)S(1)} %get-tuple-element.61), channel_id=1, source_target_pairs={{0,8},{4,12},{8,0},{12,4},{16,24},{20,28},{24,16},{28,20},{1,9},{5... | collective-permute-start | bytes 393224 | tf_op jit(solution)/shard_map/ppermute | solution.py:40
  34.7 1.8 %collective-permute-start.25 = (f32[256,256]{1,0:T(8,128)S(1)}, f32[256,256]{1,0:T(8,128)S(1)}, u32[]{:S(2)}, u32[]{:S(2)}) collective-permute-start(f32[256,256]{1,0:T(8,128)S(1)} %level0.12.refs_7_.refs_0_), channel_id=1, source_target_pairs={{0,8},{4,12},{8,0},{12,4},{16,24},{20,28},{24,16},{28,20},{1,9},{5... | collective-permute-start | bytes 786440 | tf_op jit(solution)/shard_map/ppermute | solution.py:40
  36.6 1.5 %leaf_2.1 = (f32[256,256]{1,0:T(8,128)S(1)}, f32[256,256]{1,0:T(8,128)S(1)}, f32[256,256]{1,0:T(8,128)S(1)}, f32[256,256]{1,0:T(8,128)S(1)}) custom-call(f32[512,2048]{1,0:T(8,128)S(1)} %get-tuple-element.45.refs_0_, bf16[512,2048]{1,0:T(8,128)(2,1)S(1)} %get-tuple-element.46.refs_1_.refs_7_, bf16[512,2048]{1,0:T(8,128)(2,1)S(1)} %get-tuple-element.47.refs_2_, ...), custom_call_target="tpu_custom_call" | custom-call | flops 1000 | bytes 1000 | tf_op jit(solution)/shard_map/leaf_2/pallas_call | solution.py:26
  38.1 1.6 %collective-permute-start.13 = (f32[256,256]{1,0:T(8,128)S(1)}, f32[256,256]{1,0:T(8,128)S(1)}, u32[]{:S(2)}, u32[]{:S(2)}) collective-permute-start(f32[256,256]{1,0:T(8,128)S(1)} %get-tuple-element.64.refs_0_), channel_id=1, source_target_pairs={{0,16},{4,20},{8,24},{12,28},{16,0},{20,4},{24,8},{28,12},{1,17},{... | collective-permute-start | bytes 786440 | tf_op jit(solution)/shard_map/ppermute | solution.py:40
  41.4 1.5 %leaf_3.1 = (f32[256,256]{1,0:T(8,128)S(1)}, f32[256,256]{1,0:T(8,128)S(1)}, f32[256,256]{1,0:T(8,128)S(1)}, f32[256,256]{1,0:T(8,128)S(1)}) custom-call(f32[512,2048]{1,0:T(8,128)S(1)} %get-tuple-element.45.refs_0_, bf16[512,2048]{1,0:T(8,128)(2,1)S(1)} %get-tuple-element.46.refs_1_.refs_7_, bf16[512,2048]{1,0:T(8,128)(2,1)S(1)} %get-tuple-element.47.refs_2_, ...), custom_call_target="tpu_custom_call" | custom-call | flops 1000 | bytes 1000 | tf_op jit(solution)/shard_map/leaf_3/pallas_call | solution.py:26
  43.4 2.1 %collective-permute-start.27 = (f32[256,256]{1,0:T(8,128)S(1)}, f32[256,256]{1,0:T(8,128)S(1)}, u32[]{:S(2)}, u32[]{:S(2)}) collective-permute-start(f32[256,256]{1,0:T(8,128)S(1)} %level1.12.refs_4_.refs_0_), channel_id=1, source_target_pairs={{0,16},{4,20},{8,24},{12,28},{16,0},{20,4},{24,8},{28,12},{1,17},{... | collective-permute-start | bytes 786440 | tf_op jit(solution)/shard_map/ppermute | solution.py:40
  45.9 2.4 %collective-permute-start.26 = (f32[256,256]{1,0:T(8,128)S(1)}, f32[256,256]{1,0:T(8,128)S(1)}, u32[]{:S(2)}, u32[]{:S(2)}) collective-permute-start(f32[256,256]{1,0:T(8,128)S(1)} %level0.13.refs_0_), channel_id=1, source_target_pairs={{0,8},{4,12},{8,0},{12,4},{16,24},{20,28},{24,16},{28,20},{1,9},{5... | collective-permute-start | bytes 786440 | tf_op jit(solution)/shard_map/ppermute | solution.py:40
  51.5 2.4 %collective-permute-start.14 = (f32[256,256]{1,0:T(8,128)S(1)}, f32[256,256]{1,0:T(8,128)S(1)}, u32[]{:S(2)}, u32[]{:S(2)}) collective-permute-start(f32[256,256]{1,0:T(8,128)S(1)} %level0.9.refs_0_), channel_id=1, source_target_pairs={{0,8},{4,12},{8,0},{12,4},{16,24},{20,28},{24,16},{28,20},{1,9},{5... | collective-permute-start | bytes 786440 | tf_op jit(solution)/shard_map/ppermute | solution.py:40
  57.1 2.4 %collective-permute-start.29 = (f32[256,256]{1,0:T(8,128)S(1)}, f32[256,256]{1,0:T(8,128)S(1)}, u32[]{:S(2)}, u32[]{:S(2)}) collective-permute-start(f32[256,256]{1,0:T(8,128)S(1)} %level0.14.refs_7_.refs_0_), channel_id=1, source_target_pairs={{0,8},{4,12},{8,0},{12,4},{16,24},{20,28},{24,16},{28,20},{1,9},{5... | collective-permute-start | bytes 786440 | tf_op jit(solution)/shard_map/ppermute | solution.py:40
  62.8 2.3 %collective-permute-start.17 = (f32[256,256]{1,0:T(8,128)S(1)}, f32[256,256]{1,0:T(8,128)S(1)}, u32[]{:S(2)}, u32[]{:S(2)}) collective-permute-start(f32[256,256]{1,0:T(8,128)S(1)} %level0.10.refs_7_.refs_0_), channel_id=1, source_target_pairs={{0,8},{4,12},{8,0},{12,4},{16,24},{20,28},{24,16},{28,20},{1,9},{5... | collective-permute-start | bytes 786440 | tf_op jit(solution)/shard_map/ppermute | solution.py:40
  68.5 2.1 %collective-permute-start.31 = (f32[256,256]{1,0:T(8,128)S(1)}, f32[256,256]{1,0:T(8,128)S(1)}, u32[]{:S(2)}, u32[]{:S(2)}) collective-permute-start(f32[256,256]{1,0:T(8,128)S(1)} %level0.15.refs_0_), channel_id=1, source_target_pairs={{0,8},{4,12},{8,0},{12,4},{16,24},{20,28},{24,16},{28,20},{1,9},{5... | collective-permute-start | bytes 786440 | tf_op jit(solution)/shard_map/ppermute | solution.py:40
  71.8 1.5 %collective-permute-start.20 = (f32[256,256]{1,0:T(8,128)S(1)}, f32[256,256]{1,0:T(8,128)S(1)}, u32[]{:S(2)}, u32[]{:S(2)}) collective-permute-start(f32[256,256]{1,0:T(8,128)S(1)} %level1.10.refs_4_.refs_0_), channel_id=1, source_target_pairs={{0,16},{4,20},{8,24},{12,28},{16,0},{20,4},{24,8},{28,12},{1,17},{... | collective-permute-start | bytes 786440 | tf_op jit(solution)/shard_map/ppermute | solution.py:40
  73.7 2.5 %collective-permute-start.19 = (f32[256,256]{1,0:T(8,128)S(1)}, f32[256,256]{1,0:T(8,128)S(1)}, u32[]{:S(2)}, u32[]{:S(2)}) collective-permute-start(f32[256,256]{1,0:T(8,128)S(1)} %level0.11.refs_0_), channel_id=1, source_target_pairs={{0,8},{4,12},{8,0},{12,4},{16,24},{20,28},{24,16},{28,20},{1,9},{5... | collective-permute-start | bytes 786440 | tf_op jit(solution)/shard_map/ppermute | solution.py:40
  79.2 2.6 %collective-permute-done.20.refs_1_ = f32[256,256]{1,0:T(8,128)S(1)} collective-permute-done((f32[256,256]{1,0:T(8,128)S(1)}, f32[256,256]{1,0:T(8,128)S(1)}, u32[]{:S(2)}, u32[]{:S(2)}) %collective-permute-start.20) | collective-permute-done | bytes 262176 | tf_op jit(solution)/shard_map/ppermute | solution.py:40
  84.8 1.9 %early_store.1.refs_6_ = f32[512,2048]{1,0:T(8,128)} custom-call(f32[256,256]{1,0:T(8,128)S(1)} %rest_0.1.refs_0_, f32[256,256]{1,0:T(8,128)S(1)} %rest_1.1.refs_1_, f32[256,256]{1,0:T(8,128)S(1)} %get-tuple-element.75.refs_2_, f32[256,256]{1,0:T(8,128)S(1)} %get-tuple-element.76.refs_3_, f32[256,256]{1,0:T(8,128)S(1)} %get-tuple-element.77.refs_4_, ...), custom_call_target="tpu_custom_call" | custom-call | flops 1000 | bytes 1000 | tf_op jit(solution)/shard_map/early_store/pallas_call | solution.py:26
  87.9 4.8 %collective-permute-done.21.refs_1_ = f32[256,256]{1,0:T(8,128)S(1)} collective-permute-done((f32[256,256]{1,0:T(8,128)S(1)}, f32[256,256]{1,0:T(8,128)S(1)}, u32[]{:S(2)}, u32[]{:S(2)}) %collective-permute-start.21) | collective-permute-done | bytes 262176 | tf_op jit(solution)/shard_map/ppermute | solution.py:40
  (87 shorter events, 33.7 us)
Async XLA Ops:
  1.2 16.3 %collective-permute-start = (f32[320,128]{1,0:T(8,128)S(1)}, f32[320,128]{1,0:T(8,128)S(1)}, u32[]{:S(2)}, u32[]{:S(2)}) collective-permute-start(f32[320,128]{1,0:T(8,128)S(1)} %get-tuple-element.43), channel_id=1, source_target_pairs={{0,2},{1,3},{2,0},{3,1},{4,6},{5,7},{6,4},{7,5},{8,10},{9,11},{10,... | collective-permute-start | bytes 491528 | tf_op jit(solution)/shard_map/ppermute | solution.py:40
  5.3 15.6 %collective-permute-start.1 = (f32[320,128]{1,0:T(8,128)S(1)}, f32[320,128]{1,0:T(8,128)S(1)}, u32[]{:S(2)}, u32[]{:S(2)}) collective-permute-start(f32[320,128]{1,0:T(8,128)S(1)} %get-tuple-element.44), channel_id=1, source_target_pairs={{0,2},{1,3},{2,0},{3,1},{4,6},{5,7},{6,4},{7,5},{8,10},{9,11},{10,... | collective-permute-start | bytes 491528 | tf_op jit(solution)/shard_map/ppermute | solution.py:40
  5.4 22.8 %collective-permute-start.2 = (f32[320,256]{1,0:T(8,128)S(1)}, f32[320,256]{1,0:T(8,128)S(1)}, u32[]{:S(2)}, u32[]{:S(2)}) collective-permute-start(f32[320,256]{1,0:T(8,128)S(1)} %get-tuple-element.48.refs_0_), channel_id=1, source_target_pairs={{0,1},{1,0},{2,3},{3,2},{4,5},{5,4},{6,7},{7,6},{8,9},{9,8},{10,11... | collective-permute-start | bytes 983048 | tf_op jit(solution)/shard_map/ppermute | solution.py:40
  7.2 21.0 %collective-permute-start.3 = (f32[320,256]{1,0:T(8,128)S(1)}, f32[320,256]{1,0:T(8,128)S(1)}, u32[]{:S(2)}, u32[]{:S(2)}) collective-permute-start(f32[320,256]{1,0:T(8,128)S(1)} %get-tuple-element.48.refs_0_), channel_id=1, source_target_pairs={{1,2},{2,1},{5,6},{6,5},{9,10},{10,9},{13,14},{14,13},{17,18},{18,... | collective-permute-start | bytes 983048 | tf_op jit(solution)/shard_map/ppermute | solution.py:49
  17.5 9.8 %collective-permute-start.4 = (f32[320,128]{1,0:T(8,128)S(1)}, f32[320,128]{1,0:T(8,128)S(1)}, u32[]{:S(2)}, u32[]{:S(2)}) collective-permute-start(f32[320,128]{1,0:T(8,128)S(1)} %collective-permute-done.refs_1_.refs_3_), channel_id=1, source_target_pairs={{1,0},{2,3},{5,4},{6,7},{9,8},{10,11},{13,12},{14,15},{17,16},{18,... | collective-permute-start | bytes 491528 | tf_op jit(solution)/shard_map/ppermute | solution.py:50
  34.7 8.2 %collective-permute-start.25 = (f32[256,256]{1,0:T(8,128)S(1)}, f32[256,256]{1,0:T(8,128)S(1)}, u32[]{:S(2)}, u32[]{:S(2)}) collective-permute-start(f32[256,256]{1,0:T(8,128)S(1)} %level0.12.refs_7_.refs_0_), channel_id=1, source_target_pairs={{0,8},{4,12},{8,0},{12,4},{16,24},{20,28},{24,16},{28,20},{1,9},{5... | collective-permute-start | bytes 786440 | tf_op jit(solution)/shard_map/ppermute | solution.py:40
  38.1 10.1 %collective-permute-start.13 = (f32[256,256]{1,0:T(8,128)S(1)}, f32[256,256]{1,0:T(8,128)S(1)}, u32[]{:S(2)}, u32[]{:S(2)}) collective-permute-start(f32[256,256]{1,0:T(8,128)S(1)} %get-tuple-element.64.refs_0_), channel_id=1, source_target_pairs={{0,16},{4,20},{8,24},{12,28},{16,0},{20,4},{24,8},{28,12},{1,17},{... | collective-permute-start | bytes 786440 | tf_op jit(solution)/shard_map/ppermute | solution.py:40
  40.5 9.2 %collective-permute-start.11 = (f32[256,256]{1,0:T(8,128)S(1)}, f32[256,256]{1,0:T(8,128)S(1)}, u32[]{:S(2)}, u32[]{:S(2)}) collective-permute-start(f32[256,256]{1,0:T(8,128)S(1)} %level0.8.refs_7_.refs_0_.refs_4_), channel_id=1, source_target_pairs={{0,8},{4,12},{8,0},{12,4},{16,24},{20,28},{24,16},{28,20},{1,9},{5... | collective-permute-start | bytes 786440 | tf_op jit(solution)/shard_map/ppermute | solution.py:40
  43.4 10.5 %collective-permute-start.27 = (f32[256,256]{1,0:T(8,128)S(1)}, f32[256,256]{1,0:T(8,128)S(1)}, u32[]{:S(2)}, u32[]{:S(2)}) collective-permute-start(f32[256,256]{1,0:T(8,128)S(1)} %level1.12.refs_4_.refs_0_), channel_id=1, source_target_pairs={{0,16},{4,20},{8,24},{12,28},{16,0},{20,4},{24,8},{28,12},{1,17},{... | collective-permute-start | bytes 786440 | tf_op jit(solution)/shard_map/ppermute | solution.py:40
  45.9 9.6 %collective-permute-start.26 = (f32[256,256]{1,0:T(8,128)S(1)}, f32[256,256]{1,0:T(8,128)S(1)}, u32[]{:S(2)}, u32[]{:S(2)}) collective-permute-start(f32[256,256]{1,0:T(8,128)S(1)} %level0.13.refs_0_), channel_id=1, source_target_pairs={{0,8},{4,12},{8,0},{12,4},{16,24},{20,28},{24,16},{28,20},{1,9},{5... | collective-permute-start | bytes 786440 | tf_op jit(solution)/shard_map/ppermute | solution.py:40
  48.2 8.5 %collective-permute-start.23 = (f32[256,256]{1,0:T(8,128)S(1)}, f32[256,256]{1,0:T(8,128)S(1)}, u32[]{:S(2)}, u32[]{:S(2)}) collective-permute-start(f32[256,256]{1,0:T(8,128)S(1)} %get-tuple-element.68.refs_0_), channel_id=1, source_target_pairs={{0,4},{4,0},{8,12},{12,8},{16,20},{20,16},{24,28},{28,24},{1,5},{5... | collective-permute-start | bytes 786440 | tf_op jit(solution)/shard_map/ppermute | solution.py:40
  50.1 10.4 %collective-permute-start.15 = (f32[256,256]{1,0:T(8,128)S(1)}, f32[256,256]{1,0:T(8,128)S(1)}, u32[]{:S(2)}, u32[]{:S(2)}) collective-permute-start(f32[256,256]{1,0:T(8,128)S(1)} %level1.8.refs_4_.refs_0_), channel_id=1, source_target_pairs={{0,16},{4,20},{8,24},{12,28},{16,0},{20,4},{24,8},{28,12},{1,17},{... | collective-permute-start | bytes 786440 | tf_op jit(solution)/shard_map/ppermute | solution.py:40
  51.5 9.6 %collective-permute-start.14 = (f32[256,256]{1,0:T(8,128)S(1)}, f32[256,256]{1,0:T(8,128)S(1)}, u32[]{:S(2)}, u32[]{:S(2)}) collective-permute-start(f32[256,256]{1,0:T(8,128)S(1)} %level0.9.refs_0_), channel_id=1, source_target_pairs={{0,8},{4,12},{8,0},{12,4},{16,24},{20,28},{24,16},{28,20},{1,9},{5... | collective-permute-start | bytes 786440 | tf_op jit(solution)/shard_map/ppermute | solution.py:40
  53.9 8.5 %collective-permute-start.9 = (f32[256,256]{1,0:T(8,128)S(1)}, f32[256,256]{1,0:T(8,128)S(1)}, u32[]{:S(2)}, u32[]{:S(2)}) collective-permute-start(f32[256,256]{1,0:T(8,128)S(1)} %get-tuple-element.58.refs_0_), channel_id=1, source_target_pairs={{0,4},{4,0},{8,12},{12,8},{16,20},{20,16},{24,28},{28,24},{1,5},{5... | collective-permute-start | bytes 786440 | tf_op jit(solution)/shard_map/ppermute | solution.py:40
  55.9 10.3 %collective-permute-start.30 = (f32[256,256]{1,0:T(8,128)S(1)}, f32[256,256]{1,0:T(8,128)S(1)}, u32[]{:S(2)}, u32[]{:S(2)}) collective-permute-start(f32[256,256]{1,0:T(8,128)S(1)} %level1.13.refs_4_.refs_0_), channel_id=1, source_target_pairs={{0,16},{4,20},{8,24},{12,28},{16,0},{20,4},{24,8},{28,12},{1,17},{... | collective-permute-start | bytes 786440 | tf_op jit(solution)/shard_map/ppermute | solution.py:40
  57.1 9.5 %collective-permute-start.29 = (f32[256,256]{1,0:T(8,128)S(1)}, f32[256,256]{1,0:T(8,128)S(1)}, u32[]{:S(2)}, u32[]{:S(2)}) collective-permute-start(f32[256,256]{1,0:T(8,128)S(1)} %level0.14.refs_7_.refs_0_), channel_id=1, source_target_pairs={{0,8},{4,12},{8,0},{12,4},{16,24},{20,28},{24,16},{28,20},{1,9},{5... | collective-permute-start | bytes 786440 | tf_op jit(solution)/shard_map/ppermute | solution.py:40
  61.5 9.1 %collective-permute-start.18 = (f32[256,256]{1,0:T(8,128)S(1)}, f32[256,256]{1,0:T(8,128)S(1)}, u32[]{:S(2)}, u32[]{:S(2)}) collective-permute-start(f32[256,256]{1,0:T(8,128)S(1)} %level1.9.refs_4_.refs_0_), channel_id=1, source_target_pairs={{0,16},{4,20},{8,24},{12,28},{16,0},{20,4},{24,8},{28,12},{1,17},{... | collective-permute-start | bytes 786440 | tf_op jit(solution)/shard_map/ppermute | solution.py:40
  62.8 8.6 %collective-permute-start.17 = (f32[256,256]{1,0:T(8,128)S(1)}, f32[256,256]{1,0:T(8,128)S(1)}, u32[]{:S(2)}, u32[]{:S(2)}) collective-permute-start(f32[256,256]{1,0:T(8,128)S(1)} %level0.10.refs_7_.refs_0_), channel_id=1, source_target_pairs={{0,8},{4,12},{8,0},{12,4},{16,24},{20,28},{24,16},{28,20},{1,9},{5... | collective-permute-start | bytes 786440 | tf_op jit(solution)/shard_map/ppermute | solution.py:40
  67.1 9.2 %collective-permute-start.32 = (f32[256,256]{1,0:T(8,128)S(1)}, f32[256,256]{1,0:T(8,128)S(1)}, u32[]{:S(2)}, u32[]{:S(2)}) collective-permute-start(f32[256,256]{1,0:T(8,128)S(1)} %level1.14.refs_4_.refs_0_), channel_id=1, source_target_pairs={{0,16},{4,20},{8,24},{12,28},{16,0},{20,4},{24,8},{28,12},{1,17},{... | collective-permute-start | bytes 786440 | tf_op jit(solution)/shard_map/ppermute | solution.py:40
  68.5 9.2 %collective-permute-start.31 = (f32[256,256]{1,0:T(8,128)S(1)}, f32[256,256]{1,0:T(8,128)S(1)}, u32[]{:S(2)}, u32[]{:S(2)}) collective-permute-start(f32[256,256]{1,0:T(8,128)S(1)} %level0.15.refs_0_), channel_id=1, source_target_pairs={{0,8},{4,12},{8,0},{12,4},{16,24},{20,28},{24,16},{28,20},{1,9},{5... | collective-permute-start | bytes 786440 | tf_op jit(solution)/shard_map/ppermute | solution.py:40
  71.8 10.0 %collective-permute-start.20 = (f32[256,256]{1,0:T(8,128)S(1)}, f32[256,256]{1,0:T(8,128)S(1)}, u32[]{:S(2)}, u32[]{:S(2)}) collective-permute-start(f32[256,256]{1,0:T(8,128)S(1)} %level1.10.refs_4_.refs_0_), channel_id=1, source_target_pairs={{0,16},{4,20},{8,24},{12,28},{16,0},{20,4},{24,8},{28,12},{1,17},{... | collective-permute-start | bytes 786440 | tf_op jit(solution)/shard_map/ppermute | solution.py:40
  73.7 9.0 %collective-permute-start.19 = (f32[256,256]{1,0:T(8,128)S(1)}, f32[256,256]{1,0:T(8,128)S(1)}, u32[]{:S(2)}, u32[]{:S(2)}) collective-permute-start(f32[256,256]{1,0:T(8,128)S(1)} %level0.11.refs_0_), channel_id=1, source_target_pairs={{0,8},{4,12},{8,0},{12,4},{16,24},{20,28},{24,16},{28,20},{1,9},{5... | collective-permute-start | bytes 786440 | tf_op jit(solution)/shard_map/ppermute | solution.py:40
  78.1 9.3 %collective-permute-start.33 = (f32[256,256]{1,0:T(8,128)S(1)}, f32[256,256]{1,0:T(8,128)S(1)}, u32[]{:S(2)}, u32[]{:S(2)}) collective-permute-start(f32[256,256]{1,0:T(8,128)S(1)} %level1.15.refs_0_), channel_id=1, source_target_pairs={{0,16},{4,20},{8,24},{12,28},{16,0},{20,4},{24,8},{28,12},{1,17},{... | collective-permute-start | bytes 786440 | tf_op jit(solution)/shard_map/ppermute | solution.py:40
  83.1 9.6 %collective-permute-start.21 = (f32[256,256]{1,0:T(8,128)S(1)}, f32[256,256]{1,0:T(8,128)S(1)}, u32[]{:S(2)}, u32[]{:S(2)}) collective-permute-start(f32[256,256]{1,0:T(8,128)S(1)} %level1.11.refs_0_), channel_id=1, source_target_pairs={{0,16},{4,20},{8,24},{12,28},{16,0},{20,4},{24,8},{28,12},{1,17},{... | collective-permute-start | bytes 786440 | tf_op jit(solution)/shard_map/ppermute | solution.py:40
  (10 other events, 62.1 us)
